TPU v7x, 128 devices: a whole 4x4x4 slice. The times are simulated.
128 devices in a mesh: seq: 16 (over x, z), exp: 8 (over y, core).
Axes of the slice: x: 4, y: 4, z: 4, core: 2. Of those that a mesh axis runs over, the one named last changes fastest.
Arguments:
- hidden: bfloat16 [16384, 2048], P('seq'), may hold values from -9 to 9
- mixer_gain: float32 [2048], replicated, may hold values from 0.1 to 1.9
- gate_proj: bfloat16 [2048, 4096], P(None, 'exp'), may hold values from -0.125 to 0.125
- value_proj: bfloat16 [2048, 4096], P(None, 'exp'), may hold values from -0.125 to 0.125
- state_proj: bfloat16 [2048, 2048], P(None, 'exp'), may hold values from -0.125 to 0.125
- log_decay: float32 [16384, 64], P('seq', 'exp'), may hold values from -0.8 to 0
- step_size: float32 [16384, 64], P('seq', 'exp'), may hold values from 0 to 0.25
- skip_gain: float32 [64], P('exp'), may hold values from 0.5 to 1.5
- group_gain: float32 [4096], P('exp'), may hold values from 0.1 to 1.9
- out_proj: bfloat16 [4096, 2048], P('exp'), may hold values from -0.09375 to 0.09375
- moe_gain: float32 [2048], replicated, may hold values from 0.1 to 1.9
- router: bfloat16 [2048, 128], replicated, may hold values from -0.0625 to 0.0625
- expert_ids: int32 [16384, 8], P(('seq', 'exp')), may hold values from 0 to 127, all different within a row; in each aligned block of 128 rows (0 to 127, 128 to 255, ...) at most 12 rows name the same one
- expert_gate_up: bfloat16 [128, 2048, 1536], P(('seq', 'exp')), may hold values from -0.125 to 0.125
- expert_down: bfloat16 [128, 768, 2048], P(('seq', 'exp')), may hold values from -0.4375 to 0.4375
Outputs:
- mixer_out: bfloat16 [16384, 2048], P(('seq', 'exp'))
- layer_out: bfloat16 [16384, 2048], P(('seq', 'exp'))
Inputs may be any that keep to these rules, and one draw needn't show every extreme that they name: `expert_ids`: within the 128 rows of one device (aligned blocks) no expert is named more than 12 times, and in some blocks some expert is named exactly 12 times; a row never names an expert twice.
All inputs are finite; a program needn't handle non-finite values.
Results may differ from a plain program's by a relative error of at most 0.025.
Values may be sent and summed in bfloat16 or wider, within the bound.
No kernel may reach another device: no remote copies, remote signals or barrier semaphores. Data moves between devices by JAX's collectives and lax.ppermute only.
A program may use at most 128 MiB of HBM per device.

v0:
```python
import jax
import jax.numpy as jnp
from jax import lax
from jax.sharding import PartitionSpec as P

D = 2048
P_SIZE = 64
N = 128
Q = 256


epsilon = 1e-05
highest = lax.Precision.HIGHEST


def prefix(x, axis, join, neutral):
    place = lax.axis_index(axis)
    gathered = jax.tree.map(
        lambda a, kind: lax.all_gather(a.astype(kind), axis), x, (jnp.bfloat16, jnp.bfloat16)
    )
    state = jax.tree.map(lambda a, e: jnp.zeros_like(a) + jnp.asarray(e, a.dtype), x, neutral)

    def one(hop, state):
        return join(
            state,
            jax.tree.map(
                lambda a, own: lax.dynamic_index_in_dim(a, hop, 0, False).astype(own.dtype),
                gathered,
                x,
            ),
        )

    return lax.fori_loop(0, place, one, state)


def rms_rows(values, gain):
    wide = values.astype(jnp.float32)
    inv_scale = lax.rsqrt(jnp.mean(wide * wide, axis=-1, keepdims=True) + epsilon)
    return (wide * inv_scale * gain).astype(jnp.bfloat16)


def block_terms(out_maps, in_maps, inputs, log_decay_rates):
    block_len = log_decay_rates.shape[1]
    cumulative = jnp.cumsum(log_decay_rates, axis=1)
    lower_tri = jnp.arange(block_len)[:, None] >= jnp.arange(block_len)[None, :]
    gap_matrix = cumulative[:, :, None] - cumulative[:, None, :]
    decay_mask = jnp.exp(jnp.where(lower_tri[None, :, :, None, None], gap_matrix, -jnp.inf))
    scores = jnp.einsum("ctgn,csgn->ctsg", out_maps, in_maps, precision=highest)
    weights = scores[..., None] * decay_mask
    within = jnp.einsum("ctsgj,csgjp->ctgjp", weights, inputs, precision=highest)
    block_end = cumulative[:, -1]
    to_end = jnp.exp(block_end[:, None] - cumulative)
    states = jnp.einsum("csgn,csgjp->cgjnp", in_maps, inputs * to_end[..., None], precision=highest)
    return (cumulative, within, states, block_end)


def link_states(earlier, later):
    return (earlier[0] + later[0], jnp.exp(later[0])[..., None, None] * earlier[1] + later[1])


def apply_experts(arrived, gate_up, down_rows):
    hidden_width = down_rows.shape[1]
    projected = jnp.einsum("sjcd,jdf->sjcf", arrived, gate_up, preferred_element_type=jnp.float32)
    activated = (jax.nn.silu(projected[..., :hidden_width]) * projected[..., hidden_width:]).astype(
        jnp.bfloat16
    )
    return jnp.einsum(
        "sjcf,jfd->sjcd", activated, down_rows, preferred_element_type=jnp.float32
    ).astype(jnp.bfloat16)


def body(
    hidden,
    mixer_gain,
    gate_proj,
    value_proj,
    state_proj,
    log_decay,
    step_size,
    skip_gain,
    group_gain,
    out_proj,
    moe_gain,
    router,
    expert_ids,
    expert_gate_up,
    expert_down,
):
    shard_rows = hidden.shape[0]
    heads_here = log_decay.shape[1]
    groups_here = state_proj.shape[1] // (2 * N)
    heads_in = heads_here // groups_here
    blocks = shard_rows // Q
    mixer_in = rms_rows(hidden, mixer_gain)
    gate_act = jnp.dot(mixer_in, gate_proj, preferred_element_type=jnp.float32).astype(jnp.bfloat16)
    value_act = jnp.dot(mixer_in, value_proj, preferred_element_type=jnp.float32).astype(
        jnp.bfloat16
    )
    state_act = jnp.dot(mixer_in, state_proj, preferred_element_type=jnp.float32).astype(
        jnp.bfloat16
    )
    maps_all = state_act.astype(jnp.float32).reshape(blocks, Q, groups_here, 2, N)
    in_all = maps_all[:, :, :, 0]
    out_all = maps_all[:, :, :, 1]
    head_values = value_act.astype(jnp.float32).reshape(blocks, Q, groups_here, heads_in, P_SIZE)
    log_decay_rates = log_decay.reshape(blocks, Q, groups_here, heads_in)
    head_inputs = head_values * step_size.reshape(blocks, Q, groups_here, heads_in)[..., None]
    cumulative, within, states, block_end = block_terms(
        out_all, in_all, head_inputs, log_decay_rates
    )

    def advance(carry_state, segment):
        block_state, block_decay = segment
        return (jnp.exp(block_decay)[..., None, None] * carry_state + block_state, carry_state)

    start_state = jnp.zeros((groups_here, heads_in, N, P_SIZE), jnp.float32)
    final_state, entering = lax.scan(advance, start_state, (states, block_end))
    total_decay = jnp.sum(block_end, axis=0)
    before = jnp.cumsum(block_end, axis=0) - block_end
    prefix_decay, incoming = prefix(
        (total_decay, final_state),
        "seq",
        link_states,
        (jnp.zeros_like(total_decay), jnp.zeros_like(final_state)),
    )
    entering = entering + jnp.exp(before)[..., None, None] * incoming[None]
    carried = jnp.exp(cumulative)[..., None] * jnp.einsum(
        "ctgn,cgjnp->ctgjp", out_all, entering, precision=highest
    )
    mixer_heads = (within + carried).reshape(shard_rows, groups_here, heads_in, P_SIZE)
    mixer_heads = mixer_heads + skip_gain.reshape(groups_here, heads_in)[
        :, :, None
    ] * head_values.reshape(shard_rows, groups_here, heads_in, P_SIZE)
    gated = mixer_heads.reshape(shard_rows, groups_here, heads_in * P_SIZE) * jax.nn.silu(
        gate_act.astype(jnp.float32)
    ).reshape(shard_rows, groups_here, heads_in * P_SIZE)
    normed = gated * lax.rsqrt(jnp.mean(gated * gated, axis=-1, keepdims=True) + epsilon)
    normed_mix = (normed.reshape(shard_rows, heads_here * P_SIZE) * group_gain).astype(jnp.bfloat16)
    own_rows = shard_rows // lax.axis_size("exp")
    segment = normed_mix
    partial_value = jnp.dot(segment, out_proj, preferred_element_type=jnp.float32)
    head_sum = lax.psum_scatter(
        lax.optimization_barrier(partial_value.astype(jnp.bfloat16))
        .astype(jnp.float32)
        .astype(jnp.bfloat16),
        "exp",
        scatter_dimension=0,
        tiled=True,
    ).astype(jnp.float32)
    residual = lax.dynamic_slice_in_dim(hidden, lax.axis_index("exp") * own_rows, own_rows, 0)
    mixer_out = (residual.astype(jnp.float32) + head_sum).astype(jnp.bfloat16)
    expert_input = rms_rows(mixer_out, moe_gain)
    experts_all = router.shape[1]
    affinity = jax.nn.sigmoid(jnp.dot(expert_input, router, preferred_element_type=jnp.float32))
    chosen = expert_ids[:, :, None] == jnp.arange(experts_all, dtype=jnp.int32)[None, None, :]
    picked = jnp.sum(jnp.where(chosen, affinity[:, None, :], 0.0), axis=-1)
    route_weight = picked / jnp.sum(picked, axis=-1, keepdims=True)
    rows_here = expert_ids.shape[0]
    top_count = expert_ids.shape[1]
    capacity = rows_here * top_count * 3 // (2 * experts_all)
    onehot = chosen.reshape(rows_here * top_count, experts_all).astype(jnp.int32)
    rank_index = jnp.sum((jnp.cumsum(onehot, axis=0) - onehot) * onehot, axis=-1)
    slot_index = expert_ids.reshape(-1) * capacity + rank_index
    token_index = jnp.arange(rows_here * top_count, dtype=jnp.int32) // top_count
    outgoing = (
        jnp.zeros((experts_all * capacity, D), jnp.bfloat16)
        .at[slot_index]
        .set(expert_input[token_index])
    )
    seq_count = lax.axis_size("seq")
    exp_count = lax.axis_size("exp")
    peer_count = seq_count * exp_count
    local_count = expert_gate_up.shape[0]
    processed = apply_experts(
        lax.all_to_all(
            outgoing.reshape(peer_count, local_count, capacity, D),
            ("seq", "exp"),
            split_axis=0,
            concat_axis=0,
            tiled=True,
        ),
        expert_gate_up,
        expert_down,
    )
    gathered_back_rows = lax.all_to_all(
        processed, ("seq", "exp"), split_axis=0, concat_axis=0, tiled=True
    )
    fetched_all = gathered_back_rows.reshape(experts_all * capacity, D)[slot_index].reshape(
        rows_here, top_count, D
    )
    total = mixer_out.astype(jnp.float32)
    for position in range(top_count):
        total = (
            total
            + fetched_all[:, position].astype(jnp.float32)
            * route_weight[:, position : position + 1]
        )
    layer_out = total.astype(jnp.bfloat16)
    return (mixer_out, layer_out)


def solution(mesh):
    in_specs = (
        P("seq", None),
        P(),
        P(None, "exp"),
        P(None, "exp"),
        P(None, "exp"),
        P("seq", "exp"),
        P("seq", "exp"),
        P("exp"),
        P("exp"),
        P("exp", None),
        P(),
        P(),
        P(("seq", "exp"), None),
        P(("seq", "exp"), None, None),
        P(("seq", "exp"), None, None),
    )
    out_specs = (P(("seq", "exp"), None), P(("seq", "exp"), None))
    return jax.shard_map(body, mesh=mesh, in_specs=in_specs, out_specs=out_specs, check_vma=False)
```

profile of v0, /device:TPU:1, one launch (start us, length us, event | category | flops | bytes accessed | tf_op | source)
XLA Modules:
  0.0 578.4 jit_solution(611564801929291806)
XLA Ops:
  7.3 3.2 fusion.2
  10.5 2.3 reduce-window.14
  14.0 4.6 convolution_convert_fusion.3
  20.6 3.2 fusion.93
  23.7 6.7 %fusion.44 = f32[1024,512]{0,1:T(8,128)} fusion(bf16[2048,512]{1,0:T(8,128)(2,1)} %param.22, bf16[1024,2048]{1,0:T(8,128)(2,1)} %param.19, f32[2048]{0:T(1024)S(1)} %copy-done.16, f32[1024]{0:T(1024)S(1)} %add_rsqrt_fusion.1), kind=kOutput, calls=%fused_computation.63 | convolution fusion | flops 2156920832 | bytes 8400896 | tf_op jit(solution)/shard_map/dot_general | solution.py:96
  30.4 3.2 reshape.380
  33.6 4.0 fusion.45
  37.6 22.9 %while.26 = (s32[]{:T(128)}, f32[1,8,128,64]{3,2,1,0:T(8,128)}, f32[4,1,8,128,64]{4,3,2,1,0:T(8,128)}, f32[4,1,8]{2,1,0:T(1,128)S(1)}, f32[4,1,8,128,64]{3,4,2,0,1:T(8,128)}, /*index=5*/s32[]{:T(128)}, s32[]{:T(128)}) while((s32[]{:T(128)}, f32[1,8,128,64]{3,2,1,0:T(8,128)}, f32[4,1,8,128,64]{4,3,2,1,0:T(8,128)}, ...), condition=%wide.region_4.5_spmd.clone, body=%wide.region_3.4_spmd.clone.sunk | while | flops 262147 | bytes 2883788 | solution.py:117
  46.4 2.1 bitcast_add_fusion.3
  52.4 2.1 bitcast_add_fusion.3
  58.4 2.1 bitcast_add_fusion.3
  64.8 35.8 %all-reduce = bf16[128]{0:T(256)(128)(2,1)S(1)} all-reduce(bf16[128]{0:T(256)(128)(2,1)S(1)} %dynamic-update-slice), channel_id=2, replica_groups=mesh['seq'=16,'exp'=8] {'seq'}, use_global_device_ids=true, to_apply=%add | all-reduce | flops 128 | bytes 512
  100.6 2.5 convolution_bitcast_fusion
  103.2 2.5 copy.152
  105.8 12.0 %fusion.5 = f32[4,8,64,256]{3,2,1,0:T(8,128)} fusion(f32[4,256,8]{1,2,0:T(8,128)S(1)} %fusion.82, f32[4,256,256]{2,1,0:T(8,128)} %copy.152, pred[256,256]{1,0:T(8,128)(4,1)S(1)} %iota_compare_fusion.4, f32[4,256,8,64]{1,0,3,2:T(4,128)} %reshape.380, f32[4,256,8]{1,2,0:T(8,128)S(1)} %bitcast.211), kind=kOutput, calls=%fused_computation.17 | convolution fusion | flops 1617428480 | bytes 5373952 | tf_op jit(solution)/shard_map/ctsgj,csgjp->ctgjp/dot_general | solution.py:50
  118.7 4.6 fusion.35
  126.2 3.1 multiply_reduce_fusion
  129.3 4.4 convolution_convert_fusion
  139.5 77.9 %reduce-scatter.2.cloned.1.call-done = bf16[128,2048]{1,0:T(8,128)(2,1)} async-done(((bf16[1024,2048]{1,0:T(8,128)(2,1)}), bf16[128,2048]{1,0:T(8,128)(2,1)}) %reduce-scatter.2.cloned.1.call-update) | async-done | bytes 524304 | tf_op jit(solution)/shard_map/reduce_scatter | solution.py:142
  220.7 24.3 %scatter_custom_fusion = bf16[1536,2048]{1,0:T(8,128)(2,1)} fusion(s32[1024]{0:T(1024)S(1)} %bitcast.217, bf16[128,2048]{1,0:T(8,128)(2,1)} %fusion.53, s32[1024]{0:T(1024)S(1)} %broadcast_clamp_fusion.1, bf16[]{:T(256)} %constant.94.clone.1), kind=kCustom, calls=%fused_computation.30 | custom fusion | bytes 6291968 | tf_op jit(solution)/shard_map/scatter | solution.py:168
  245.0 10.6 %reshape.393 = bf16[128,1,12,2048]{3,2,0,1:T(8,128)(2,1)} reshape(bf16[1536,2048]{1,0:T(8,128)(2,1)} %scatter_custom_fusion) | data formatting | bytes 12582912 | tf_op jit(solution)/shard_map/reshape | solution.py:176
  255.6 108.6 %all_to_all.10 = bf16[128,1,12,2048]{3,2,1,0:T(8,128)(2,1)S(1)} all-to-all(bf16[128,1,12,2048]{3,2,1,0:T(8,128)(2,1)} %bitcast.205), channel_id=1, replica_groups=mesh['seq'=16,'exp'=8] {'seq','exp'}, dimensions={0} | all-to-all | bytes 12582912 | tf_op jit(solution)/shard_map/all_to_all | solution.py:175
  364.2 25.7 %fusion.14 = f32[128,1,12,1536]{3,0,2,1:T(8,128)} fusion(bf16[1,2048,1536]{2,1,0:T(8,128)(2,1)} %param.32, bf16[128,1,12,2048]{3,2,1,0:T(8,128)(2,1)S(1)} %all_to_all.10), kind=kOutput, calls=%fused_computation.27 | convolution fusion | flops 9663676416 | bytes 22020096 | tf_op jit(solution)/shard_map/sjcd,jdf->sjcf/dot_general | solution.py:63
  390.0 9.3 %convert_bitcast_fusion = bf16[128,1,12,2048]{3,0,2,1:T(8,128)(2,1)S(1)} fusion(bf16[1,768,2048]{2,1,0:T(8,128)(2,1)S(1)} %copy-done, f32[128,1,12,1536]{3,0,2,1:T(8,128)} %fusion.14), kind=kOutput, calls=%fused_computation.26 | convolution fusion | flops 4842061824 | bytes 18874368 | tf_op jit(solution)/shard_map/sjcf,jfd->sjcd/dot_general | solution.py:67
  399.3 6.8 %copy.169 = bf16[128,1,12,2048]{3,2,1,0:T(8,128)(2,1)} copy(bf16[128,1,12,2048]{3,0,2,1:T(8,128)(2,1)S(1)} %convert_bitcast_fusion) | data formatting | bytes 12582912 | tf_op jit(solution)/shard_map/convert_element_type | solution.py:69
  406.1 9.4 %all-to-all-start.1 = ((bf16[128,1,12,2048]{3,2,1,0:T(8,128)(2,1)}), bf16[128,1,12,2048]{3,2,1,0:T(8,128)(2,1)}, u32[]{:S(2)}, u32[]{:S(2)}) async-start(bf16[128,1,12,2048]{3,2,1,0:T(8,128)(2,1)} %copy.169), calls=%async_computation.2 | async-start | bytes 16777216 | tf_op jit(solution)/shard_map/all_to_all | solution.py:185
  417.0 2.0 select_reduce_fusion
  419.5 102.4 %all-to-all-done.1 = bf16[128,1,12,2048]{3,2,1,0:T(8,128)(2,1)} async-done(((bf16[128,1,12,2048]{3,2,1,0:T(8,128)(2,1)}), bf16[128,1,12,2048]{3,2,1,0:T(8,128)(2,1)}, u32[]{:S(2)}, u32[]{:S(2)}) %all-to-all-start.1) | async-done | bytes 6291488 | tf_op jit(solution)/shard_map/all_to_all | solution.py:185
  521.9 10.7 %reshape.398 = bf16[1536,2048]{1,0:T(8,128)(2,1)} reshape(bf16[128,1,12,2048]{3,2,1,0:T(8,128)(2,1)} %all-to-all-done.1) | data formatting | bytes 12582912 | tf_op jit(solution)/shard_map/reshape | solution.py:188
  532.6 12.4 %gather_fusion = bf16[1024,2048]{1,0:T(8,128)(2,1)} fusion(bf16[1536,2048]{1,0:T(8,128)(2,1)} %reshape.398, s32[1024]{0:T(1024)S(1)} %broadcast_clamp_fusion), kind=kCustom, calls=%fused_computation.1 | custom fusion | bytes 8392704 | tf_op jit(solution)/shard_map/gather | solution.py:188
  545.0 20.8 %fusion.92 = (bf16[128,1,2048]{2,1,0:T(2,128)(2,1)S(1)}, bf16[128,1,2048]{2,1,0:T(2,128)(2,1)S(1)}, bf16[128,1,2048]{2,1,0:T(2,128)(2,1)S(1)}, bf16[128,1,2048]{...) fusion(bf16[128,8,2048]{2,1,0:T(8,128)(2,1)} %bitcast.204), kind=kLoop, calls=%fused_computation.162 | loop fusion | bytes 8388608 | tf_op jit(solution)/shard_map/slice | solution.py:195
  565.9 5.4 fusion.61
  (114 shorter events, 38.0 us)
Async XLA Ops:
  7.2 382.8 %copy-start = (bf16[1,768,2048]{2,1,0:T(8,128)(2,1)S(1)}, bf16[1,768,2048]{2,1,0:T(8,128)(2,1)}, u32[]{:S(2)}) copy-start(bf16[1,768,2048]{2,1,0:T(8,128)(2,1)} %param.33) | copy-start | bytes 9437188
  7.2 3.3 copy-start.7
  7.2 6.8 %copy-start.16 = (f32[2048]{0:T(1024)S(1)}, f32[2048]{0:T(1024)}, u32[]{:S(2)}) copy-start(f32[2048]{0:T(1024)} %param.20) | copy-start | bytes 24580
  7.2 110.7 %all-gather.4.cloned.1.call-start = ((), (), s32[]{:S(2)}) async-start(), calls=%async_computation.4 | async-start | bytes 2228224 | tf_op jit(solution)/shard_map/all_gather | solution.py:19
  10.5 13.2 %copy-start.10 = (f32[1024]{0:T(1024)}, f32[1024]{0:T(1024)S(1)}, u32[]{:S(2)}) copy-start(f32[1024]{0:T(1024)S(1)} %add_rsqrt_fusion.1) | copy-start | bytes 12292
  30.4 3.2 copy-start.6
  37.6 24.9 %copy-start.13 = (f32[8]{0:T(128)S(1)}, f32[8]{0:T(128)}, u32[]{:S(2)}) copy-start(f32[8]{0:T(128)} %param.26) | copy-start | bytes 100
  37.6 25.6 %copy-start.19 = (u32[128]{0:T(128)S(1)}, u32[128]{0:T(128)}, u32[]{:S(2)}) copy-start(u32[128]{0:T(128)} %constant.105) | copy-start | bytes 1540
  62.4 155.1 %reduce-scatter.2.cloned.1.call-start = ((), (), s32[]{:S(2)}) async-start(), calls=%async_computation.3 | async-start | bytes 4718592 | tf_op jit(solution)/shard_map/reduce_scatter | solution.py:142
  118.7 6.5 %copy-start.14 = (bf16[2048,512]{1,0:T(8,128)(2,1)S(1)}, bf16[2048,512]{1,0:T(8,128)(2,1)}, u32[]{:S(2)}) copy-start(bf16[2048,512]{1,0:T(8,128)(2,1)} %param.21) | copy-start | bytes 6291460
  123.3 2.2 copy-start.1
  123.3 2.9 copy-start.5
  123.3 2.9 copy-start.11
  123.3 2.8 copy-start.12
  123.3 2.8 copy-start.17
  126.2 3.1 copy-start.15
  126.2 3.1 copy-start.18
  133.7 0.7 copy-start.8
  133.7 85.9 %copy-start.9 = (f32[2048]{0:T(1024)S(1)}, f32[2048]{0:T(1024)}, u32[]{:S(2)}) copy-start(f32[2048]{0:T(1024)} %param.29) | copy-start | bytes 24580
  135.2 0.8 copy-start.4
  218.9 0.8 copy-start.2
  406.1 115.8 %all-to-all-start.1 = ((bf16[128,1,12,2048]{3,2,1,0:T(8,128)(2,1)}), bf16[128,1,12,2048]{3,2,1,0:T(8,128)(2,1)}, u32[]{:S(2)}, u32[]{:S(2)}) async-start(bf16[128,1,12,2048]{3,2,1,0:T(8,128)(2,1)} %copy.169), calls=%async_computation.2 | async-start | bytes 16777216 | tf_op jit(solution)/shard_map/all_to_all | solution.py:185
  545.0 20.8 %copy-start.3 = (bf16[128,2048]{1,0:T(8,128)(2,1)S(1)}, bf16[128,2048]{1,0:T(8,128)(2,1)}, u32[]{:S(2)}) copy-start(bf16[128,2048]{1,0:T(8,128)(2,1)} %copy-done.2) | copy-start | bytes 1572868
Sparse Core Ops, SparseCore 0:
  62.5 47.4 all-gather.3
  133.9 83.4 reduce-scatter.1
where the time goes:
time: 588 us; the launch traced here: 578 us
  waiting for transfers between devices  180 us (31%)
  blocking collectives  144 us (24%)
  local copies, waits for them, and re-layouts  116 us (20%)
  matrix products  78.4 us (13%)
  other arithmetic  34.4 us (6%)
  between operations  15.3 us (3%)
  starting transfers between devices  9.44 us (2%)
    all_to_all x1, blocking collectives, body(): lax.all_to_all(outgoing.reshape(peer_count, local_count, capacity, D), ('...  109 us
    all_to_all x1, waiting for transfers between devices, body(): lax.all_to_all(processed, ('seq', 'exp'), split_axis=0, concat_axis=0, ti...  102 us
    reduce_scatter x1, waiting for transfers between devices, body(): lax.psum_scatter(lax.optimization_barrier(partial_value.astype(jnp.bfloat...  77.9 us
    unnamed x1, blocking collectives  35.8 us
    dot_general x1, matrix products, apply_experts(): jnp.einsum('sjcd,jdf->sjcf', arrived, gate_up, preferred_element_type=jnp...  25.7 us
    scatter x1, local copies, waits for them, and re-layouts, body(): outgoing = jnp.zeros((experts_all * capacity, D), jnp.bfloat16).at[slot_i...  24.3 us
    slice x1, local copies, waits for them, and re-layouts, body(): fetched_all[:, position].astype(jnp.float32)  20.8 us
    gather x1, local copies, waits for them, and re-layouts, body(): gathered_back_rows.reshape(experts_all * capacity, D)[slot_index]  12.4 us
  transfers between devices with their start and end apart: 3, of which 2 were waited for; matrix products, arithmetic and copies ran while one was open for 5% of the time, Pallas kernels for 0%

commit v1 on v0

v1 whole, which is shorter than its diff:
```python
import jax
import jax.numpy as jnp
from jax import lax
from jax.experimental import pallas as pl
from jax.experimental.pallas import tpu as pltpu
from jax.sharding import PartitionSpec as P

D = 2048
HALF = D // 2
P_SIZE = 64
N = 128
Q = 256
F = 768
CAP = 12
SLAB = 2 * CAP

f32 = jnp.float32
bf16 = jnp.bfloat16
epsilon = 1e-05
highest = lax.Precision.HIGHEST
VMEM_LIMIT = 50 * 2**20


def params():
    return pltpu.CompilerParams(
        dimension_semantics=("arbitrary",), vmem_limit_bytes=VMEM_LIMIT
    )


def cost(flops, nbytes, transcendentals=0):
    return pl.CostEstimate(
        flops=int(flops), bytes_accessed=int(nbytes), transcendentals=int(transcendentals)
    )


def iota(shape, axis, kind=jnp.int32):
    return lax.broadcasted_iota(jnp.int32, shape, axis).astype(kind)


def dot(a, b):
    return jnp.dot(a, b, preferred_element_type=f32)


def dot_first(a, b):
    return lax.dot_general(a, b, (((0,), (0,)), ((), ())), preferred_element_type=f32)


def dot_last(a, b):
    return lax.dot_general(a, b, (((1,), (1,)), ((), ())), preferred_element_type=f32)


def running_sum(rows):
    count = rows.shape[0]
    lower = (iota((count, count), 0) >= iota((count, count), 1)).astype(f32)
    return jnp.dot(lower, rows, precision=highest, preferred_element_type=f32)


def per_channel(values):
    heads = values.shape[1]
    lanes = heads * P_SIZE
    first = iota((heads, lanes), 0) * P_SIZE
    lane = iota((heads, lanes), 1)
    spread = ((lane >= first) & (lane < first + P_SIZE)).astype(f32).astype(bf16)
    coarse = values.astype(bf16)
    fine = (values - coarse.astype(f32)).astype(bf16)
    return dot(coarse, spread) + dot(fine, spread)


def row_per_channel(row):
    return per_channel(jnp.broadcast_to(row, (8, row.shape[1])))[0:1]


def local_state_kernel(
    hidden_ref,
    gain_ref,
    value_ref,
    state_ref,
    decay_ref,
    step_ref,
    mixed_ref,
    x_ref,
    maps_ref,
    enter_ref,
    sent_ref,
    state,
    total,
):
    block = pl.program_id(0)

    @pl.when(block == 0)
    def _():
        state[...] = jnp.zeros_like(state)
        total[...] = jnp.zeros_like(total)

    wide = hidden_ref[...].astype(f32)
    scale = lax.rsqrt(jnp.mean(wide * wide, axis=-1, keepdims=True) + epsilon)
    mixed = (wide * scale * gain_ref[...]).astype(bf16)
    mixed_ref[...] = mixed
    x = dot(mixed, value_ref[...]).astype(bf16)
    x_ref[...] = x
    maps = dot(mixed, state_ref[...]).astype(bf16)
    maps_ref[...] = maps
    sums = running_sum(decay_ref[...])
    end = sums[Q - 1 : Q]
    weight = per_channel(jnp.exp(end - sums) * step_ref[...])
    weighted = (x.astype(f32) * weight).astype(bf16)
    old = state[...]
    enter_ref[0] = old.astype(bf16)
    new = old * row_per_channel(jnp.exp(end)) + dot_first(maps[:, :N], weighted)
    state[...] = new
    total[0:1, :] = total[0:1, :] + end

    @pl.when(block == pl.num_programs(0) - 1)
    def _():
        parts = sent_ref.shape[0]
        channels = new.shape[1]
        log_total = row_per_channel(total[0:1, :])
        coarse = log_total.astype(bf16).astype(f32)
        which = iota((8, channels), 0)
        tail = jnp.where(which == 0, coarse, jnp.where(which == 1, log_total - coarse, 0.0))
        rows = new.reshape(parts, N // parts, channels)
        sent_ref[...] = jnp.concatenate(
            [rows, jnp.broadcast_to(tail[None], (parts, 8, channels))], axis=1
        ).astype(bf16)


def prefix_kernel(got_ref, out_ref):
    count = got_ref.shape[0]
    rows = out_ref.shape[1]
    carry = jnp.zeros(out_ref.shape[1:], f32)
    for shard in range(count):
        out_ref[shard] = carry.astype(bf16)
        got = got_ref[shard].astype(f32)
        decay = jnp.exp(got[rows : rows + 1] + got[rows + 1 : rows + 2])
        carry = decay * carry + got[:rows]


def within_kernel(
    mixed_ref, gate_w_ref, x_ref, maps_ref, decay_ref, step_ref, gate_ref, within_ref
):
    gate_ref[...] = dot(mixed_ref[...], gate_w_ref[...]).astype(bf16)
    sums = running_sum(decay_ref[...])
    heads = sums.shape[1]
    blank = jnp.zeros((Q, 128 - 2 * heads), f32)
    across = jnp.concatenate([sums, step_ref[...], blank], axis=1).T
    maps = maps_ref[...]
    scores = dot_last(maps[:, N:], maps[:, :N])
    scores = jnp.where(iota((Q, Q), 0) >= iota((Q, Q), 1), scores, 0.0)
    causal = iota((Q, Q), 0) >= iota((Q, Q), 1)
    left = (iota((Q, 2 * P_SIZE), 1) < P_SIZE).astype(f32).astype(bf16)
    right = (iota((Q, 2 * P_SIZE), 1) >= P_SIZE).astype(f32).astype(bf16)
    for pair in range(heads // 2):
        weights = []
        for head in (2 * pair, 2 * pair + 1):
            gap = sums[:, head : head + 1] - across[head : head + 1]
            decay = jnp.exp(jnp.where(causal, gap, -1e30))
            weights.append(
                (scores * decay * across[heads + head : heads + head + 1]).astype(bf16)
            )
        lanes = slice(pair * 2 * P_SIZE, (pair + 1) * 2 * P_SIZE)
        x = x_ref[:, lanes]
        within_ref[:, lanes] = dot(
            jnp.concatenate(weights, axis=1), jnp.concatenate([x * left, x * right], axis=0)
        )


def normed_kernel(
    core_ref,
    within_ref,
    x_ref,
    maps_ref,
    gate_ref,
    decay_ref,
    enter_ref,
    incoming_ref,
    skip_ref,
    gain_ref,
    own_ref,
    other_ref,
    before,
):
    block = pl.program_id(0)

    @pl.when(block == 0)
    def _():
        before[...] = jnp.zeros_like(before)

    passed = before[0:1, :]
    sums = running_sum(decay_ref[...])
    entering = enter_ref[0].astype(f32) + row_per_channel(jnp.exp(passed)) * incoming_ref[
        ...
    ].astype(f32)
    before[0:1, :] = passed + sums[Q - 1 : Q]
    carried = per_channel(jnp.exp(sums)) * dot(maps_ref[:, N:], entering.astype(bf16))
    heads = within_ref[...] + carried + row_per_channel(skip_ref[...]) * x_ref[...].astype(f32)
    gate = gate_ref[...].astype(f32)
    gated = heads * (gate * jax.nn.sigmoid(gate))
    scale = lax.rsqrt(jnp.mean(gated * gated, axis=-1, keepdims=True) + epsilon)
    normed = gated * scale * gain_ref[...]
    rows = own_ref.shape[0]
    first, second = normed[:rows], normed[rows:]
    mine = core_ref[0] == 0
    own_ref[...] = jnp.where(mine, first, second).astype(bf16)
    other_ref[...] = jnp.where(mine, second, first).astype(bf16)


def project_kernel(where_ref, own_ref, got_ref, own_w_ref, got_w_ref, out_ref):
    out_ref[...] = (
        dot(own_ref[...], own_w_ref[...]) + dot(got_ref[...], got_w_ref[...])
    ).astype(bf16)


def slots(row):
    place = row - SLAB * jnp.floor((row + 0.5) * (1.0 / SLAB))
    slot = jnp.where(place < 8, place, jnp.where(place < 20, place - 8, place - 12))
    second = ((place >= 8) & (place < 16)) | (place >= 20)
    return slot, second


def expert_of(block, rows, experts):
    gap = iota((rows, experts), 0) + block * rows - SLAB * iota((rows, experts), 1)
    return ((gap >= 0) & (gap < SLAB)).astype(f32).astype(bf16)


def dispatch_kernel(
    where_ref,
    a_ref,
    b_ref,
    c_ref,
    d_ref,
    hidden_ref,
    gain_ref,
    router_ref,
    ids_ref,
    mixer_ref,
    rank_ref,
    weight_ref,
    out_ref,
    rows_in,
    ranks,
):
    block = pl.program_id(0)
    experts = router_ref.shape[1]
    tokens = ids_ref.shape[0]

    @pl.when(block == 0)
    def _():
        head_sum = (
            a_ref[...].astype(f32)
            + b_ref[...].astype(f32)
            + c_ref[...].astype(f32)
            + d_ref[...].astype(f32)
        )
        mixer_out = (hidden_ref[...].astype(f32) + head_sum).astype(bf16)
        mixer_ref[...] = mixer_out
        wide = mixer_out.astype(f32)
        scale = lax.rsqrt(jnp.mean(wide * wide, axis=-1, keepdims=True) + epsilon)
        expert_input = (wide * scale * gain_ref[...]).astype(bf16)
        rows_in[:tokens, :] = expert_input[:, :HALF]
        rows_in[tokens:, :] = expert_input[:, HALF:]
        affinity = jax.nn.sigmoid(dot(expert_input, router_ref[...]))
        lane = iota((tokens, experts), 1)
        named = jnp.zeros((tokens, experts), f32)
        for k in range(ids_ref.shape[1]):
            named = named + (ids_ref[:, k : k + 1] == lane).astype(f32)
        picked = named * affinity
        weight_ref[...] = picked / jnp.sum(picked, axis=-1, keepdims=True)
        earlier = (iota((tokens, tokens), 0) > iota((tokens, tokens), 1)).astype(f32)
        rank = dot(earlier.astype(bf16), named.astype(bf16))
        rank = jnp.where(named > 0.5, rank, -1.0)
        rank_ref[...] = rank
        ranks[...] = rank.astype(bf16)

    rows = out_ref.shape[0]
    ranked = dot_last(expert_of(block, rows, experts), ranks[...])
    slot, second = slots(iota((rows, tokens), 0, f32))
    hit = ranked == slot
    first_half = (hit & jnp.logical_not(second)).astype(f32).astype(bf16)
    second_half = (hit & second).astype(f32).astype(bf16)
    picker = jnp.concatenate([first_half, second_half], axis=1)
    out_ref[...] = dot(picker, rows_in[...]).astype(bf16)


def expert_kernel(a_ref, b_ref, c_ref, up_ref, down_ref, out_ref):
    peers = a_ref.shape[0]
    rows = peers * 8
    part = rows // 2
    place = iota((rows, rows), 0)
    lane = iota((rows, rows), 1)

    def source(row):
        inner = row & (part - 1)
        return ((inner >> 2) << 3) + jnp.where(row >= part, 4, 0) + (inner & 3)

    apart = (source(place) == lane).astype(f32).astype(bf16)
    together = (place == source(lane)).astype(f32).astype(bf16)
    tail = dot(apart, c_ref[...].reshape(rows, HALF)).astype(bf16)
    x0 = jnp.concatenate([a_ref[...].reshape(rows, HALF), tail[:part]], axis=0)
    x1 = jnp.concatenate([b_ref[...].reshape(rows, HALF), tail[part:]], axis=0)
    projected = dot(x0, up_ref[0, :HALF]) + dot(x1, up_ref[0, HALF:])
    gate = projected[:, :F]
    hidden = (gate * jax.nn.sigmoid(gate) * projected[:, F:]).astype(bf16)
    y0 = dot(hidden, down_ref[0, :, :HALF]).astype(bf16)
    y1 = dot(hidden, down_ref[0, :, HALF:]).astype(bf16)
    out_ref[:, 0] = y0[:rows].reshape(peers, 8, HALF)
    out_ref[:, 1] = y1[:rows].reshape(peers, 8, HALF)
    tail = jnp.concatenate([y0[rows:], y1[rows:]], axis=0)
    out_ref[:, 2] = dot(together, tail).astype(bf16).reshape(peers, 8, HALF)


def combine_kernel(got_ref, rank_ref, weight_ref, mixer_ref, out_ref, total):
    block = pl.program_id(0)
    rows = got_ref.shape[0]
    tokens, experts = rank_ref.shape

    @pl.when(block == 0)
    def _():
        total[...] = jnp.zeros_like(total)

    member = expert_of(block, rows, experts)
    ranked = dot_last(rank_ref[...].astype(bf16), member)
    weight = dot_last(weight_ref[...].astype(bf16), member)
    slot, second = slots(iota((tokens, rows), 1, f32))
    weight = jnp.where(ranked == slot, weight, 0.0)
    first_half = jnp.where(second, 0.0, weight).astype(bf16)
    second_half = jnp.where(second, weight, 0.0).astype(bf16)
    total[...] += dot(jnp.concatenate([first_half, second_half], axis=0), got_ref[...])

    @pl.when(block == pl.num_programs(0) - 1)
    def _():
        out_ref[:, :HALF] = (mixer_ref[:, :HALF].astype(f32) + total[:tokens]).astype(bf16)
        out_ref[:, HALF:] = (mixer_ref[:, HALF:].astype(f32) + total[tokens:]).astype(bf16)


def fixed(*shape):
    return pl.BlockSpec(shape, lambda *_: (0,) * len(shape))


def fixed_once(*shape):
    return pl.BlockSpec(
        shape, lambda *_: (0,) * len(shape), pipeline_mode=pl.Buffered(1)
    )


def by_rows(*shape):
    rest = (0,) * (len(shape) - 1)
    return pl.BlockSpec(shape, lambda i, *_: (i, *rest))


def shape_of(kind, *shape):
    return jax.ShapeDtypeStruct(shape, kind)


def body(
    hidden,
    mixer_gain,
    gate_proj,
    value_proj,
    state_proj,
    log_decay,
    step_size,
    skip_gain,
    group_gain,
    out_proj,
    moe_gain,
    router,
    expert_ids,
    expert_gate_up,
    expert_down,
):
    rows = hidden.shape[0]
    heads = log_decay.shape[1]
    channels = heads * P_SIZE
    blocks = rows // Q
    seq_count = lax.axis_size("seq")
    exp_count = lax.axis_size("exp")
    peers = seq_count * exp_count
    place = lax.axis_index("exp")
    core, line = place % 2, place // 2
    lines = exp_count // 2
    own_rows = rows // exp_count
    slice_rows = N // seq_count

    swap = [(i, i ^ 1) for i in range(exp_count)]
    other_proj = lax.ppermute(out_proj, "exp", swap)

    mixed, x, maps, enter, sent = pl.pallas_call(
        local_state_kernel,
        grid=(blocks,),
        in_specs=[
            by_rows(Q, D),
            fixed(1, D),
            fixed_once(D, channels),
            fixed_once(D, 2 * N),
            by_rows(Q, heads),
            by_rows(Q, heads),
        ],
        out_specs=[
            by_rows(Q, D),
            by_rows(Q, channels),
            by_rows(Q, 2 * N),
            by_rows(1, N, channels),
            fixed(seq_count, slice_rows + 8, channels),
        ],
        out_shape=[
            shape_of(bf16, rows, D),
            shape_of(bf16, rows, channels),
            shape_of(bf16, rows, 2 * N),
            shape_of(bf16, blocks, N, channels),
            shape_of(bf16, seq_count, slice_rows + 8, channels),
        ],
        scratch_shapes=[pltpu.VMEM((N, channels), f32), pltpu.VMEM((8, heads), f32)],
        compiler_params=params(),
        cost_estimate=cost(2 * rows * D * (channels + 2 * N), 16 * 2**20),
        name="local_state",
    )(hidden, mixer_gain.reshape(1, D), value_proj, state_proj, log_decay, step_size)

    slices = lax.all_to_all(sent, "seq", split_axis=0, concat_axis=0, tiled=True)
    before = pl.pallas_call(
        prefix_kernel,
        out_shape=shape_of(bf16, seq_count, slice_rows, channels),
        compiler_params=pltpu.CompilerParams(vmem_limit_bytes=VMEM_LIMIT),
        name="prefix",
    )(slices)
    incoming = lax.all_to_all(before, "seq", split_axis=0, concat_axis=0, tiled=True)
    incoming = incoming.reshape(N, channels)

    gate, within = pl.pallas_call(
        within_kernel,
        grid=(blocks,),
        in_specs=[
            by_rows(Q, D),
            fixed_once(D, channels),
            by_rows(Q, channels),
            by_rows(Q, 2 * N),
            by_rows(Q, heads),
            by_rows(Q, heads),
        ],
        out_specs=[by_rows(Q, channels), by_rows(Q, channels)],
        out_shape=[shape_of(bf16, rows, channels), shape_of(f32, rows, channels)],
        compiler_params=params(),
        cost_estimate=cost(2 * rows * channels * (D + Q), 12 * 2**20, rows * Q * heads),
        name="within",
    )(mixed, gate_proj, x, maps, log_decay, step_size)

    own, other = pl.pallas_call(
        normed_kernel,
        grid_spec=pltpu.PrefetchScalarGridSpec(
            num_scalar_prefetch=1,
            grid=(blocks,),
            in_specs=[
                by_rows(Q, channels),
                by_rows(Q, channels),
                by_rows(Q, 2 * N),
                by_rows(Q, channels),
                by_rows(Q, heads),
                by_rows(1, N, channels),
                fixed(N, channels),
                fixed(1, heads),
                fixed(1, channels),
            ],
            out_specs=[by_rows(own_rows, channels), by_rows(own_rows, channels)],
            scratch_shapes=[pltpu.VMEM((8, heads), f32)],
        ),
        out_shape=[shape_of(bf16, rows // 2, channels)] * 2,
        compiler_params=params(),
        cost_estimate=cost(2 * rows * N * channels, 8 * 2**20),
        name="normed",
    )(
        core.reshape(1),
        within,
        x,
        maps,
        gate,
        log_decay,
        enter,
        incoming,
        skip_gain.reshape(1, heads),
        group_gain.reshape(1, channels),
    )
    got = lax.ppermute(other, "exp", swap)

    def project(target):
        return pl.pallas_call(
            project_kernel,
            grid_spec=pltpu.PrefetchScalarGridSpec(
                num_scalar_prefetch=1,
                grid=(1,),
                in_specs=[
                    pl.BlockSpec((own_rows, channels), lambda i, at: (at[0], 0)),
                    pl.BlockSpec((own_rows, channels), lambda i, at: (at[0], 0)),
                    fixed_once(channels, D),
                    fixed_once(channels, D),
                ],
                out_specs=fixed(own_rows, D),
            ),
            out_shape=shape_of(bf16, own_rows, D),
            compiler_params=params(),
            cost_estimate=cost(4 * own_rows * channels * D, 5 * 2**20),
            name="project",
        )(target.reshape(1), own, got, out_proj, other_proj)

    pieces = []
    for hop in (2, 1, 3):
        partial = project((line + hop) % lines)
        pieces.append(
            lax.ppermute(
                partial, "exp", [(i, (i + 2 * hop) % exp_count) for i in range(exp_count)]
            )
        )
    mine = project(line)

    experts = router.shape[1]
    slab_rows = experts * SLAB
    per_step = slab_rows // 4
    mixer_out, rank, weight, outgoing = pl.pallas_call(
        dispatch_kernel,
        grid_spec=pltpu.PrefetchScalarGridSpec(
            num_scalar_prefetch=1,
            grid=(4,),
            in_specs=[fixed(own_rows, D)] * 4
            + [
                pl.BlockSpec((own_rows, D), lambda i, at: (at[0], 0)),
                fixed(1, D),
                fixed(D, experts),
                fixed(own_rows, expert_ids.shape[1]),
            ],
            out_specs=[
                fixed(own_rows, D),
                fixed(own_rows, experts),
                fixed(own_rows, experts),
                by_rows(per_step, HALF),
            ],
            scratch_shapes=[
                pltpu.VMEM((2 * own_rows, HALF), bf16),
                pltpu.VMEM((own_rows, experts), bf16),
            ],
        ),
        out_shape=[
            shape_of(bf16, own_rows, D),
            shape_of(f32, own_rows, experts),
            shape_of(f32, own_rows, experts),
            shape_of(bf16, slab_rows, HALF),
        ],
        compiler_params=params(),
        cost_estimate=cost(4 * slab_rows * own_rows * HALF, 10 * 2**20),
        name="dispatch",
    )(
        place.reshape(1),
        mine,
        *pieces,
        hidden,
        moe_gain.reshape(1, D),
        router,
        expert_ids,
    )

    arrived = lax.all_to_all(
        outgoing.reshape(peers, SLAB, HALF),
        ("seq", "exp"),
        split_axis=0,
        concat_axis=0,
        tiled=True,
    ).reshape(peers, 3, 8, HALF)
    group = peers // 4

    def piece(index):
        return pl.BlockSpec((group, None, 8, HALF), lambda i: (i, index, 0, 0))

    results = pl.pallas_call(
        expert_kernel,
        grid=(4,),
        in_specs=[
            piece(0),
            piece(1),
            piece(2),
            fixed_once(1, D, 2 * F),
            fixed_once(1, F, D),
        ],
        out_specs=by_rows(group, 3, 8, HALF),
        out_shape=shape_of(bf16, peers, 3, 8, HALF),
        compiler_params=params(),
        cost_estimate=cost(6 * peers * CAP * D * F, 22 * 2**20, peers * CAP * F),
        name="experts",
    )(arrived, arrived, arrived, expert_gate_up, expert_down)
    returned = lax.all_to_all(
        results.reshape(peers, SLAB, HALF),
        ("seq", "exp"),
        split_axis=0,
        concat_axis=0,
        tiled=True,
    ).reshape(slab_rows, HALF)

    layer_out = pl.pallas_call(
        combine_kernel,
        grid=(4,),
        in_specs=[
            by_rows(per_step, HALF),
            fixed(own_rows, experts),
            fixed(own_rows, experts),
            fixed(own_rows, D),
        ],
        out_specs=fixed(own_rows, D),
        out_shape=shape_of(bf16, own_rows, D),
        scratch_shapes=[pltpu.VMEM((2 * own_rows, HALF), f32)],
        compiler_params=params(),
        cost_estimate=cost(4 * slab_rows * own_rows * HALF, 8 * 2**20),
        name="combine",
    )(returned, rank, weight, mixer_out)
    return (mixer_out, layer_out)


def solution(mesh):
    in_specs = (
        P("seq", None),
        P(),
        P(None, "exp"),
        P(None, "exp"),
        P(None, "exp"),
        P("seq", "exp"),
        P("seq", "exp"),
        P("exp"),
        P("exp"),
        P("exp", None),
        P(),
        P(),
        P(("seq", "exp"), None),
        P(("seq", "exp"), None, None),
        P(("seq", "exp"), None, None),
    )
    out_specs = (P(("seq", "exp"), None), P(("seq", "exp"), None))
    return jax.shard_map(body, mesh=mesh, in_specs=in_specs, out_specs=out_specs, check_vma=False)
```

time: 588 us -> 296 us (0.50); the launches traced: 578 us -> 295 us
  waiting for transfers between devices: 180 us -> 22.1 us
  local copies, waits for them, and re-layouts: 116 us -> 8.78 us
  matrix products: 78.4 us -> 0 us
  Pallas kernels: 0 us -> 76.3 us
  other arithmetic: 34.4 us -> 0 us
  blocking collectives: 144 us -> 167 us
  between operations: 15.3 us -> 0.76 us
  starting transfers between devices: 9.44 us -> 20 us
    all_to_all x1 -> x2, waiting for transfers between devices: 102 us -> 7.81 us  [the longest x1 7.81 us: body(): lax.all_to_all(sent, 'seq', split_axis=0, concat_axis=0, tiled=True)]
    dot_general x11 -> x0, matrix products: 78.4 us -> none  [the longest x1 25.7 us: apply_experts(): jnp.einsum('sjcd,jdf->sjcf', arrived, gate_up, preferred_element_type=jnp...]
    reduce_scatter x1 -> x0, waiting for transfers between devices: 77.9 us -> none  [body(): lax.psum_scatter(lax.optimization_barrier(partial_value.astype(jnp.bfloat...]
    pallas_call x0 -> x11, Pallas kernels: none -> 76.3 us  [the longest x1 21.6 us: body(): pl.pallas_call(expert_kernel, grid=(4,), in_specs=[piece(0), piece(1), pi...]
    all_to_all x1 -> x2, blocking collectives: 109 us -> 167 us  [the longest x1 85.3 us: body(): lax.all_to_all(outgoing.reshape(peers, SLAB, HALF), ('seq', 'exp'), split...]
    unnamed x1 -> x0, blocking collectives: 35.8 us -> none
    reshape x4 -> x0, local copies, waits for them, and re-layouts: 26.4 us -> none  [the longest x1 10.7 us: body(): gathered_back_rows.reshape(experts_all * capacity, D)[slot_index]]
    slice x5 -> x0, local copies, waits for them, and re-layouts: 24.6 us -> none  [the longest x1 20.8 us: body(): fetched_all[:, position].astype(jnp.float32)]
  transfers between devices with their start and end apart: 3 -> 7, of which waited for: 2 -> 4; matrix products, arithmetic and copies ran while one was open for 5% -> 1% of each run, Pallas kernels for 0% -> 13%
where the time goes in v1:
time: 296 us; the launch traced here: 295 us
  blocking collectives  167 us (56%)
  Pallas kernels  76.3 us (26%)
  waiting for transfers between devices  22.1 us (7%)
  starting transfers between devices  20 us (7%)
  local copies, waits for them, and re-layouts  8.78 us (3%)
    all_to_all x1, blocking collectives, body(): lax.all_to_all(outgoing.reshape(peers, SLAB, HALF), ('seq', 'exp'), split...  85.3 us
    all_to_all x1, blocking collectives, body(): lax.all_to_all(results.reshape(peers, SLAB, HALF), ('seq', 'exp'), split_...  81.5 us
    pallas_call x1, Pallas kernels, body(): pl.pallas_call(expert_kernel, grid=(4,), in_specs=[piece(0), piece(1), pi...  21.6 us
    ppermute x3, waiting for transfers between devices, body(): lax.ppermute(partial, 'exp', [(i, (i + 2 * hop) % exp_count) for i in ran...  12.6 us
    pallas_call x4, Pallas kernels, project(): pl.pallas_call(project_kernel, grid_spec=pltpu.PrefetchScalarGridSpec(num...  11.7 us
    pallas_call x1, Pallas kernels, body(): pl.pallas_call(local_state_kernel, grid=(blocks,), in_specs=[by_rows(Q, D...  11.7 us
    pallas_call x1, Pallas kernels, body(): pl.pallas_call(within_kernel, grid=(blocks,), in_specs=[by_rows(Q, D), fi...  9.92 us
    unnamed x35, local copies, waits for them, and re-layouts  8.78 us
  transfers between devices with their start and end apart: 7, of which 4 were waited for; matrix products, arithmetic and copies ran while one was open for 1% of the time, Pallas kernels for 13%

profile of v1, /device:TPU:1, one launch (start us, length us, event | category | flops | bytes accessed | tf_op | source)
XLA Modules:
  0.0 294.8 jit_solution(11516677112109727653)
XLA Ops:
  0.6 1.5 collective-permute-start.1
  2.1 0.9 copy.17.decay_ref
  3.1 1.0 copy.18.step_ref
  4.1 0.7 copy-done.14
  4.8 11.7 %local_state.1 = (bf16[1024,2048]{1,0:T(8,128)(2,1)}, bf16[1024,512]{1,0:T(8,128)(2,1)S(1)}, bf16[1024,256]{1,0:T(8,128)(2,1)S(1)}, bf16[4,128,512]{2,1,0:T(8,128)(2,1)S(1)}, bf16[16,16,512]{2,1,0:T(8,128)(2,1)}) custom-call(bf16[1024,2048]{1,0:T(8,128)(2,1)} %hidden_ref.3, f32[1,2048]{1,0:T(1,128)S(1)} %bitcast.19, bf16[2048,512]{1,0:T(8,128)(2,1)} %value_ref.1, ...), custom_call_target="tpu_custom_call" | custom-call | flops 3221225472 | bytes 16777216 | tf_op jit(solution)/shard_map/local_state/pallas_call | solution.py:387
  16.5 0.8 copy-done.7
  17.2 7.7 %all-to-all-start = ((bf16[16,16,512]{2,1,0:T(8,128)(2,1)}), bf16[16,16,512]{2,1,0:T(8,128)(2,1)S(1)}, u32[]{:S(2)}, u32[]{:S(2)}) async-start(bf16[16,16,512]{2,1,0:T(8,128)(2,1)} %get-tuple-element.21), calls=%async_computation | async-start | bytes 524288 | tf_op jit(solution)/shard_map/all_to_all | solution.py:418
  24.9 7.8 %all-to-all-done.got_ref = bf16[16,16,512]{2,1,0:T(8,128)(2,1)S(1)} async-done(((bf16[16,16,512]{2,1,0:T(8,128)(2,1)}), bf16[16,16,512]{2,1,0:T(8,128)(2,1)S(1)}, u32[]{:S(2)}, u32[]{:S(2)}) %all-to-all-start) | async-done | bytes 262176 | tf_op jit(solution)/shard_map/all_to_all | solution.py:418
  32.8 0.7 prefix.1
  33.5 3.9 %all-to-all-start.1 = ((bf16[16,8,512]{2,1,0:T(8,128)(2,1)}), bf16[16,8,512]{2,1,0:T(8,128)(2,1)S(1)}, u32[]{:S(2)}, u32[]{:S(2)}) async-start(bf16[16,8,512]{2,1,0:T(8,128)(2,1)} %prefix.1), calls=%async_computation.1 | async-start | bytes 262144 | tf_op jit(solution)/shard_map/all_to_all | solution.py:425
  37.4 9.9 %within.1 = (bf16[1024,512]{1,0:T(8,128)(2,1)S(1)}, f32[1024,512]{1,0:T(8,128)}) custom-call(bf16[1024,2048]{1,0:T(8,128)(2,1)} %get-tuple-element.15.mixed_ref, bf16[2048,512]{1,0:T(8,128)(2,1)} %gate_w_ref.1, bf16[1024,512]{1,0:T(8,128)(2,1)S(1)} %get-tuple-element.16.x_ref, bf16[1024,256]{1,0:T(8,128)(2,1)S(1)} %get-tuple-element.17.maps_ref, ...), custom_call_target="tpu_custom_call" | custom-call | flops 2415919104 | bytes 12582912 | tf_op jit(solution)/shard_map/within/pallas_call | solution.py:428
  47.3 1.0 copy-done.3
  48.3 0.8 copy-done.5
  49.2 1.4 copy-done.2
  50.5 1.0 copy-done.6
  51.6 1.0 copy-done.8
  52.6 7.2 %normed.1 = (bf16[512,512]{1,0:T(8,128)(2,1)S(1)}, bf16[512,512]{1,0:T(8,128)(2,1)}) custom-call(s32[1]{0:T(128)} %bitcast.2.core_ref, f32[1024,512]{1,0:T(8,128)} %get-tuple-element.18.within_ref, bf16[1024,512]{1,0:T(8,128)(2,1)S(1)} %copy-done.2, bf16[1024,256]{1,0:T(8,128)(2,1)S(1)} %copy-done.6, bf16[1024,512]{1,0:T(8,128)(2,1)} %copy-done.3, ...), custom_call_target="tpu_custom_call" | custom-call | flops 134217728 | bytes 8388608 | tf_op jit(solution)/shard_map/normed/pallas_call | solution.py:446
  59.8 1.4 collective-permute-start
  61.2 1.7 collective-permute-done.got_ref
  62.9 3.1 %project.5 = bf16[128,2048]{1,0:T(8,128)(2,1)} custom-call(s32[1]{0:T(128)} %bitcast.7.where_ref, bf16[512,512]{1,0:T(8,128)(2,1)S(1)} %get-tuple-element.22.own_ref, bf16[512,512]{1,0:T(8,128)(2,1)S(1)} %collective-permute-done.got_ref, bf16[512,2048]{1,0:T(8,128)(2,1)S(1)} %copy-done, bf16[512,2048]{1,0:T(8,128)(2,1)} %collective-permute-done.1.got_w_ref), custom_call_target="tpu_custom_call" | custom-call | flops 536870912 | bytes 5242880 | tf_op jit(solution)/shard_map/project/pallas_call | solution.py:484
  66.0 2.9 collective-permute-start.2
  69.0 3.1 %project.6 = bf16[128,2048]{1,0:T(8,128)(2,1)} custom-call(s32[1]{0:T(128)} %bitcast.8.where_ref, bf16[512,512]{1,0:T(8,128)(2,1)S(1)} %get-tuple-element.22.own_ref, bf16[512,512]{1,0:T(8,128)(2,1)S(1)} %collective-permute-done.got_ref, bf16[512,2048]{1,0:T(8,128)(2,1)S(1)} %copy-done, bf16[512,2048]{1,0:T(8,128)(2,1)} %collective-permute-done.1.got_w_ref), custom_call_target="tpu_custom_call" | custom-call | flops 536870912 | bytes 5242880 | tf_op jit(solution)/shard_map/project/pallas_call | solution.py:484
  72.5 3.1 %project.7 = bf16[128,2048]{1,0:T(8,128)(2,1)} custom-call(s32[1]{0:T(128)} %bitcast.9.where_ref, bf16[512,512]{1,0:T(8,128)(2,1)S(1)} %get-tuple-element.22.own_ref, bf16[512,512]{1,0:T(8,128)(2,1)S(1)} %collective-permute-done.got_ref, bf16[512,2048]{1,0:T(8,128)(2,1)S(1)} %copy-done, bf16[512,2048]{1,0:T(8,128)(2,1)} %collective-permute-done.1.got_w_ref), custom_call_target="tpu_custom_call" | custom-call | flops 536870912 | bytes 5242880 | tf_op jit(solution)/shard_map/project/pallas_call | solution.py:484
  75.6 2.3 collective-permute-start.4
  78.0 2.4 project.4.a_ref
  80.4 0.7 collective-permute-done.2.b_ref
  81.0 11.9 %collective-permute-done.3.c_ref = bf16[128,2048]{1,0:T(8,128)(2,1)} collective-permute-done((bf16[128,2048]{1,0:T(8,128)(2,1)}, bf16[128,2048]{1,0:T(8,128)(2,1)}, u32[]{:S(2)}, u32[]{:S(2)}) %collective-permute-start.3) | collective-permute-done | bytes 524320 | tf_op jit(solution)/shard_map/ppermute | solution.py:507
  93.0 7.2 %dispatch.1 = (bf16[128,2048]{1,0:T(8,128)(2,1)}, f32[128,128]{1,0:T(8,128)S(1)}, f32[128,128]{1,0:T(8,128)S(1)}, bf16[3072,1024]{1,0:T(8,128)(2,1)}) custom-call(s32[1]{0:T(128)} %bitcast.where_ref, bf16[128,2048]{1,0:T(8,128)(2,1)S(1)} %project.4.a_ref, bf16[128,2048]{1,0:T(8,128)(2,1)} %collective-permute-done.2.b_ref, ...), custom_call_target="tpu_custom_call" | custom-call | flops 1610612736 | bytes 10485760 | tf_op jit(solution)/shard_map/dispatch/pallas_call | solution.py:516
  100.2 85.3 %all_to_all.20 = bf16[128,24,1024]{2,1,0:T(8,128)(2,1)} all-to-all(bf16[128,24,1024]{2,1,0:T(8,128)(2,1)} %bitcast.21), channel_id=1, replica_groups=mesh['seq'=16,'exp'=8] {'seq','exp'}, dimensions={0} | all-to-all | bytes 12582912 | tf_op jit(solution)/shard_map/all_to_all | solution.py:558
  185.5 21.6 %experts.1 = bf16[128,3,8,1024]{3,2,1,0:T(8,128)(2,1)} custom-call(bf16[128,3,8,1024]{3,2,1,0:T(8,128)(2,1)} %bitcast.22, bf16[128,3,8,1024]{3,2,1,0:T(8,128)(2,1)} %bitcast.23, bf16[128,3,8,1024]{3,2,1,0:T(8,128)(2,1)} %bitcast.24, bf16[1,2048,1536]{2,1,0:T(8,128)(2,1)} %up_ref.1, bf16[1,768,2048]{2,1,0:T(8,128)(2,1)S(1)} %copy-done.13), custom_call_target="tpu_custom_call" | custom-call | flops 14495514624 | bytes 23068672 | tf_op jit(solution)/shard_map/experts/pallas_call | solution.py:570
  207.0 81.5 %all_to_all.21 = bf16[128,24,1024]{2,1,0:T(8,128)(2,1)} all-to-all(bf16[128,24,1024]{2,1,0:T(8,128)(2,1)} %bitcast.25), channel_id=1, replica_groups=mesh['seq'=16,'exp'=8] {'seq','exp'}, dimensions={0} | all-to-all | bytes 12582912 | tf_op jit(solution)/shard_map/all_to_all | solution.py:586
  288.5 6.3 %combine.1 = bf16[128,2048]{1,0:T(8,128)(2,1)} custom-call(bf16[3072,1024]{1,0:T(8,128)(2,1)} %bitcast.20, f32[128,128]{1,0:T(8,128)S(1)} %get-tuple-element.26.rank_ref, f32[128,128]{1,0:T(8,128)S(1)} %get-tuple-element.27.weight_ref, bf16[128,2048]{1,0:T(8,128)(2,1)S(1)} %copy-done.4), custom_call_target="tpu_custom_call" | custom-call | flops 1610612736 | bytes 8388608 | tf_op jit(solution)/shard_map/combine/pallas_call | solution.py:594
  (30 shorter events, 0.6 us)
Async XLA Ops:
  0.6 62.3 %collective-permute-start.1 = (bf16[512,2048]{1,0:T(8,128)(2,1)}, bf16[512,2048]{1,0:T(8,128)(2,1)}, u32[]{:S(2)}, u32[]{:S(2)}) collective-permute-start(bf16[512,2048]{1,0:T(8,128)(2,1)} %own_w_ref.7), channel_id=1, source_target_pairs={{0,1},{1,0},{2,3},{3,2},{4,5},{5,4},{6,7},{7,6},{8,9},{9,8},{10,11... | collective-permute-start | bytes 6291464 | tf_op jit(solution)/shard_map/ppermute | solution.py:385
  4.1 0.7 copy-start.14
  16.4 0.8 copy-start.7
  17.2 20.1 %copy-start.1 = (bf16[1024,512]{1,0:T(8,128)(2,1)}, bf16[1024,512]{1,0:T(8,128)(2,1)S(1)}, u32[]{:S(2)}) copy-start(bf16[1024,512]{1,0:T(8,128)(2,1)S(1)} %get-tuple-element.16.x_ref) | copy-start | bytes 3145732
  17.2 15.5 %all-to-all-start = ((bf16[16,16,512]{2,1,0:T(8,128)(2,1)}), bf16[16,16,512]{2,1,0:T(8,128)(2,1)S(1)}, u32[]{:S(2)}, u32[]{:S(2)}) async-start(bf16[16,16,512]{2,1,0:T(8,128)(2,1)} %get-tuple-element.21), calls=%async_computation | async-start | bytes 524288 | tf_op jit(solution)/shard_map/all_to_all | solution.py:418
  33.5 15.6 %all-to-all-start.1 = ((bf16[16,8,512]{2,1,0:T(8,128)(2,1)}), bf16[16,8,512]{2,1,0:T(8,128)(2,1)S(1)}, u32[]{:S(2)}, u32[]{:S(2)}) async-start(bf16[16,8,512]{2,1,0:T(8,128)(2,1)} %prefix.1), calls=%async_computation.1 | async-start | bytes 262144 | tf_op jit(solution)/shard_map/all_to_all | solution.py:425
  37.4 11.8 %copy-start.11 = (f32[512]{0:T(512)S(1)}, f32[512]{0:T(512)}, u32[]{:S(2)}) copy-start(f32[512]{0:T(512)} %param.23) | copy-start | bytes 6148
  37.4 11.7 %copy-start.12 = (f32[8]{0:T(128)S(1)}, f32[8]{0:T(128)}, u32[]{:S(2)}) copy-start(f32[8]{0:T(128)} %param.22) | copy-start | bytes 100
  47.3 1.0 copy-start.3
  48.3 0.8 copy-start.5
  49.1 13.8 %copy-start = (bf16[512,2048]{1,0:T(8,128)(2,1)S(1)}, bf16[512,2048]{1,0:T(8,128)(2,1)}, u32[]{:S(2)}) copy-start(bf16[512,2048]{1,0:T(8,128)(2,1)} %own_w_ref.7) | copy-start | bytes 6291460
  49.1 1.4 copy-start.2
  50.5 1.0 copy-start.6
  51.6 1.0 copy-start.8
  59.8 3.1 %collective-permute-start = (bf16[512,512]{1,0:T(8,128)(2,1)}, bf16[512,512]{1,0:T(8,128)(2,1)S(1)}, u32[]{:S(2)}, u32[]{:S(2)}) collective-permute-start(bf16[512,512]{1,0:T(8,128)(2,1)} %get-tuple-element.23), channel_id=1, source_target_pairs={{0,1},{1,0},{2,3},{3,2},{4,5},{5,4},{6,7},{7,6},{8,9},{9,8},{10,11... | collective-permute-start | bytes 1572872 | tf_op jit(solution)/shard_map/ppermute | solution.py:481
  66.0 15.0 %collective-permute-start.2 = (bf16[128,2048]{1,0:T(8,128)(2,1)}, bf16[128,2048]{1,0:T(8,128)(2,1)}, u32[]{:S(2)}, u32[]{:S(2)}) collective-permute-start(bf16[128,2048]{1,0:T(8,128)(2,1)} %project.5), channel_id=1, source_target_pairs={{0,4},{1,5},{2,6},{3,7},{4,0},{5,1},{6,2},{7,3},{8,12},{9,13},{10,... | collective-permute-start | bytes 1572872 | tf_op jit(solution)/shard_map/ppermute | solution.py:507
  72.1 5.8 %copy-start.15 = (s32[128,8]{0,1:T(8,128)S(1)}, s32[128,8]{0,1:T(8,128)}, u32[]{:S(2)}) copy-start(s32[128,8]{0,1:T(8,128)} %param.27) | copy-start | bytes 12292
  72.1 20.9 %collective-permute-start.3 = (bf16[128,2048]{1,0:T(8,128)(2,1)}, bf16[128,2048]{1,0:T(8,128)(2,1)}, u32[]{:S(2)}, u32[]{:S(2)}) collective-permute-start(bf16[128,2048]{1,0:T(8,128)(2,1)} %project.6), channel_id=1, source_target_pairs={{0,2},{1,3},{2,4},{3,5},{4,6},{5,7},{6,0},{7,1},{8,10},{9,11},{10,... | collective-permute-start | bytes 1572872 | tf_op jit(solution)/shard_map/ppermute | solution.py:507
  75.6 17.4 %copy-start.10 = (f32[2048]{0:T(1024)S(1)}, f32[2048]{0:T(1024)}, u32[]{:S(2)}) copy-start(f32[2048]{0:T(1024)} %param.25) | copy-start | bytes 24580
  75.6 17.4 %collective-permute-start.4 = (bf16[128,2048]{1,0:T(8,128)(2,1)}, bf16[128,2048]{1,0:T(8,128)(2,1)}, u32[]{:S(2)}, u32[]{:S(2)}) collective-permute-start(bf16[128,2048]{1,0:T(8,128)(2,1)} %project.7), channel_id=1, source_target_pairs={{0,6},{1,7},{2,0},{3,1},{4,2},{5,3},{6,4},{7,5},{8,14},{9,15},{10,... | collective-permute-start | bytes 1572872 | tf_op jit(solution)/shard_map/ppermute | solution.py:507
  78.0 15.0 %copy-start.9 = (bf16[2048,128]{1,0:T(8,128)(2,1)S(1)}, bf16[2048,128]{1,0:T(8,128)(2,1)}, u32[]{:S(2)}) copy-start(bf16[2048,128]{1,0:T(8,128)(2,1)} %router_ref.1) | copy-start | bytes 1572868
  100.2 85.3 %copy-start.13 = (bf16[1,768,2048]{2,1,0:T(8,128)(2,1)S(1)}, bf16[1,768,2048]{2,1,0:T(8,128)(2,1)}, u32[]{:S(2)}) copy-start(bf16[1,768,2048]{2,1,0:T(8,128)(2,1)} %down_ref.1) | copy-start | bytes 9437188
  207.0 81.5 %copy-start.4 = (bf16[128,2048]{1,0:T(8,128)(2,1)S(1)}, bf16[128,2048]{1,0:T(8,128)(2,1)}, u32[]{:S(2)}) copy-start(bf16[128,2048]{1,0:T(8,128)(2,1)} %get-tuple-element.13.mixer_ref) | copy-start | bytes 1572868

commit v2 on v1

v2 whole, which is shorter than its diff:
```python
import jax
import jax.numpy as jnp
from jax import lax
from jax.experimental import pallas as pl
from jax.experimental.pallas import tpu as pltpu
from jax.sharding import PartitionSpec as P

D = 2048
HALF = D // 2
P_SIZE = 64
N = 128
Q = 256
F = 768
CAP = 12
SLAB = 2 * CAP

f32 = jnp.float32
bf16 = jnp.bfloat16
epsilon = 1e-05
LOG2_E = 1.4426950408889634


def params(mib):
    return pltpu.CompilerParams(
        dimension_semantics=("arbitrary",), vmem_limit_bytes=mib * 2**20
    )


def cost(flops, nbytes, transcendentals=0):
    return pl.CostEstimate(
        flops=int(flops), bytes_accessed=int(nbytes), transcendentals=int(transcendentals)
    )


def iota(shape, axis, kind=jnp.int32):
    return lax.broadcasted_iota(jnp.int32, shape, axis).astype(kind)


def dot(a, b):
    return jnp.dot(a, b, preferred_element_type=f32)


def dot_first(a, b):
    return lax.dot_general(a, b, (((0,), (0,)), ((), ())), preferred_element_type=f32)


def dot_last(a, b):
    return lax.dot_general(a, b, (((1,), (1,)), ((), ())), preferred_element_type=f32)


def running_sum(rates):
    heads, count = rates.shape
    upper = (iota((count, count), 0) <= iota((count, count), 1)).astype(f32).astype(bf16)
    terms = []
    for _ in range(3):
        term = rates.astype(bf16)
        terms.append(term)
        rates = rates - term.astype(f32)
    sums = dot(jnp.concatenate(terms, axis=0), upper)
    return sums[:heads] + (sums[heads : 2 * heads] + sums[2 * heads :])


def per_channel(values):
    heads = values.shape[0]
    lanes = heads * P_SIZE
    first = iota((heads, lanes), 0) * P_SIZE
    lane = iota((heads, lanes), 1)
    spread = ((lane >= first) & (lane < first + P_SIZE)).astype(f32)
    coarse = values.astype(bf16).astype(f32)
    terms = jnp.concatenate([coarse, values - coarse], axis=0).astype(bf16)
    return dot_first(terms, jnp.concatenate([spread, spread], axis=0).astype(bf16))


def row_per_channel(column):
    return per_channel(jnp.broadcast_to(column, (column.shape[0], 128)))[0:1]


def local_state_kernel(
    hidden_ref,
    gain_ref,
    value_ref,
    state_ref,
    decay_ref,
    step_ref,
    mixed_ref,
    x_ref,
    maps_ref,
    enter_ref,
    sent_ref,
    state,
    total,
):
    block = pl.program_id(0)

    @pl.when(block == 0)
    def _():
        state[...] = jnp.zeros_like(state)
        total[...] = jnp.zeros_like(total)

    wide = hidden_ref[...].astype(f32)
    scale = lax.rsqrt(jnp.mean(wide * wide, axis=-1, keepdims=True) + epsilon)
    mixed = (wide * scale * gain_ref[...]).astype(bf16)
    mixed_ref[...] = mixed
    x = dot(mixed, value_ref[...]).astype(bf16)
    x_ref[...] = x
    maps = dot(mixed, state_ref[...]).astype(bf16)
    maps_ref[...] = maps
    sums = running_sum(decay_ref[...])
    end = sums[:, Q - 1 : Q]
    weight = per_channel(jnp.exp(end - sums) * step_ref[...])
    weighted = (x.astype(f32) * weight).astype(bf16)
    old = state[...]
    enter_ref[0] = old.astype(bf16)
    new = old * row_per_channel(jnp.exp(end)) + dot_first(maps[:, :N], weighted)
    state[...] = new
    total[...] = total[...] + end

    @pl.when(block == pl.num_programs(0) - 1)
    def _():
        parts = sent_ref.shape[0]
        channels = new.shape[1]
        log_total = row_per_channel(total[:, 0:1])
        coarse = log_total.astype(bf16).astype(f32)
        which = iota((8, channels), 0)
        tail = jnp.where(which == 0, coarse, jnp.where(which == 1, log_total - coarse, 0.0))
        rows = new.reshape(parts, N // parts, channels)
        sent_ref[...] = jnp.concatenate(
            [rows, jnp.broadcast_to(tail[None], (parts, 8, channels))], axis=1
        ).astype(bf16)


def prefix_kernel(got_ref, out_ref):
    count = got_ref.shape[0]
    rows = out_ref.shape[1]
    carry = jnp.zeros(out_ref.shape[1:], f32)
    for shard in range(count):
        out_ref[shard] = carry.astype(bf16)
        got = got_ref[shard].astype(f32)
        decay = jnp.exp(got[rows : rows + 1] + got[rows + 1 : rows + 2])
        carry = decay * carry + got[:rows]


def gate_kernel(mixed_ref, gate_w_ref, gate_ref):
    gate_ref[...] = dot(mixed_ref[...], gate_w_ref[...]).astype(bf16)


def within_kernel(x_ref, maps_ref, decay_ref, step_ref, enter_ref, skip_ref, within_ref):
    sums = running_sum(decay_ref[...])
    heads = sums.shape[0]
    maps = maps_ref[...]
    part = Q // 2
    scores = dot_last(maps[:, N:], maps[:, :N])
    from_start = per_channel(jnp.exp(sums)) * dot(maps[:, N:], enter_ref[0])
    scaled = sums * LOG2_E
    source = scaled - jnp.log2(step_ref[...])
    blank = jnp.zeros((128 - heads, Q), f32)
    target = jnp.concatenate([scaled, blank], axis=0).T
    causal = iota((part, part), 0) >= iota((part, part), 1)
    left = (iota((Q, 2 * P_SIZE), 1) < P_SIZE).astype(f32).astype(bf16)
    right = (iota((Q, 2 * P_SIZE), 1) >= P_SIZE).astype(f32).astype(bf16)
    for pair in range(heads // 2):
        top, bottom = [], []
        for head in (2 * pair, 2 * pair + 1):
            column = target[:, head : head + 1]
            row = source[head : head + 1]
            corner = jnp.where(causal, column[:part] - row[:, :part], -jnp.inf)
            top.append((scores[:part, :part] * jnp.exp2(corner)).astype(bf16))
            past = column[part:] - row[:, :part]
            bottom.append((scores[part:, :part] * jnp.exp2(past)).astype(bf16))
            corner = jnp.where(causal, column[part:] - row[:, part:], -jnp.inf)
            bottom.append((scores[part:, part:] * jnp.exp2(corner)).astype(bf16))
        lanes = slice(pair * 2 * P_SIZE, (pair + 1) * 2 * P_SIZE)
        x = x_ref[:, lanes]
        x_left, x_right = x * left, x * right
        skip = x.astype(f32) * skip_ref[:, lanes] + from_start[:, lanes]
        within_ref[:part, lanes] = skip[:part] + dot(
            jnp.concatenate(top, axis=1),
            jnp.concatenate([x_left[:part], x_right[:part]], axis=0),
        )
        within_ref[part:, lanes] = skip[part:] + dot(
            jnp.concatenate(bottom, axis=1), jnp.concatenate([x_left, x_right], axis=0)
        )


def normed_kernel(
    core_ref,
    within_ref,
    maps_ref,
    gate_ref,
    decay_ref,
    incoming_ref,
    gain_ref,
    own_ref,
    other_ref,
    before,
):
    block = pl.program_id(0)

    @pl.when(block == 0)
    def _():
        before[...] = jnp.zeros_like(before)

    sums = running_sum(decay_ref[...]) + before[:, 0:1]
    before[...] = jnp.broadcast_to(sums[:, Q - 1 : Q], before.shape)
    carried = per_channel(jnp.exp(sums)) * dot(maps_ref[...], incoming_ref[...])
    gate = gate_ref[...].astype(f32)
    gated = (within_ref[...] + carried) * (gate * jax.nn.sigmoid(gate))
    scale = lax.rsqrt(jnp.mean(gated * gated, axis=-1, keepdims=True) + epsilon)
    normed = gated * scale * gain_ref[...]
    rows = own_ref.shape[0]
    first, second = normed[:rows], normed[rows:]
    mine = core_ref[0] == 0
    own_ref[...] = jnp.where(mine, first, second).astype(bf16)
    other_ref[...] = jnp.where(mine, second, first).astype(bf16)


def project_kernel(where_ref, own_ref, got_ref, own_w_ref, got_w_ref, out_ref):
    out_ref[...] = (
        dot(own_ref[...], own_w_ref[...]) + dot(got_ref[...], got_w_ref[...])
    ).astype(bf16)


def slots(row):
    place = row - SLAB * jnp.floor((row + 0.5) * (1.0 / SLAB))
    slot = jnp.where(place < 8, place, jnp.where(place < 20, place - 8, place - 12))
    second = ((place >= 8) & (place < 16)) | (place >= 20)
    return slot, second


def expert_of(block, rows, experts):
    gap = iota((rows, experts), 0) + block * rows - SLAB * iota((rows, experts), 1)
    return ((gap >= 0) & (gap < SLAB)).astype(f32).astype(bf16)


def route_kernel(ids_ref, named_ref, rank_ref, picker_ref, ranks):
    block = pl.program_id(0)
    tokens, experts = named_ref.shape

    @pl.when(block == 0)
    def _():
        lane = iota((tokens, experts), 1)
        named = jnp.zeros((tokens, experts), f32)
        for k in range(ids_ref.shape[1]):
            named = named + (ids_ref[:, k : k + 1] == lane).astype(f32)
        named_ref[...] = named
        earlier = (iota((tokens, tokens), 0) > iota((tokens, tokens), 1)).astype(f32)
        rank = dot(earlier.astype(bf16), named.astype(bf16))
        rank = jnp.where(named > 0.5, rank, -1.0)
        rank_ref[...] = rank
        ranks[...] = rank.astype(bf16)

    rows = picker_ref.shape[0]
    ranked = dot_last(expert_of(block, rows, experts), ranks[...])
    slot, second = slots(iota((rows, tokens), 0, f32))
    hit = (ranked == slot).astype(f32)
    picker_ref[:, :tokens] = jnp.where(second, 0.0, hit).astype(bf16)
    picker_ref[:, tokens:] = jnp.where(second, hit, 0.0).astype(bf16)


def dispatch_kernel(
    where_ref,
    a_ref,
    b_ref,
    c_ref,
    d_ref,
    hidden_ref,
    gain_ref,
    router_ref,
    named_ref,
    picker_ref,
    mixer_ref,
    weight_ref,
    out_ref,
    rows_in,
):
    block = pl.program_id(0)
    tokens = named_ref.shape[0]

    @pl.when(block == 0)
    def _():
        head_sum = (
            a_ref[...].astype(f32)
            + b_ref[...].astype(f32)
            + c_ref[...].astype(f32)
            + d_ref[...].astype(f32)
        )
        mixer_out = (hidden_ref[...].astype(f32) + head_sum).astype(bf16)
        mixer_ref[...] = mixer_out
        wide = mixer_out.astype(f32)
        scale = lax.rsqrt(jnp.mean(wide * wide, axis=-1, keepdims=True) + epsilon)
        expert_input = (wide * scale * gain_ref[...]).astype(bf16)
        rows_in[:tokens, :] = expert_input[:, :HALF]
        rows_in[tokens:, :] = expert_input[:, HALF:]
        picked = named_ref[...] * jax.nn.sigmoid(dot(expert_input, router_ref[...]))
        weight_ref[...] = picked / jnp.sum(picked, axis=-1, keepdims=True)

    out_ref[...] = dot(picker_ref[...], rows_in[...]).astype(bf16)


def expert_kernel(a_ref, b_ref, c_ref, up_ref, down_ref, out_ref):
    peers = a_ref.shape[0]
    rows = peers * 8
    part = rows // 2
    place = iota((rows, rows), 0)
    lane = iota((rows, rows), 1)

    def source(row):
        inner = row & (part - 1)
        return ((inner >> 2) << 3) + jnp.where(row >= part, 4, 0) + (inner & 3)

    apart = (source(place) == lane).astype(f32).astype(bf16)
    together = (place == source(lane)).astype(f32).astype(bf16)
    tail = dot(apart, c_ref[...].reshape(rows, HALF)).astype(bf16)
    x0 = jnp.concatenate([a_ref[...].reshape(rows, HALF), tail[:part]], axis=0)
    x1 = jnp.concatenate([b_ref[...].reshape(rows, HALF), tail[part:]], axis=0)
    projected = dot(x0, up_ref[0, :HALF]) + dot(x1, up_ref[0, HALF:])
    gate = projected[:, :F]
    hidden = (gate * jax.nn.sigmoid(gate) * projected[:, F:]).astype(bf16)
    y0 = dot(hidden, down_ref[0, :, :HALF]).astype(bf16)
    y1 = dot(hidden, down_ref[0, :, HALF:]).astype(bf16)
    out_ref[:, 0] = y0[:rows].reshape(peers, 8, HALF)
    out_ref[:, 1] = y1[:rows].reshape(peers, 8, HALF)
    tail = jnp.concatenate([y0[rows:], y1[rows:]], axis=0)
    out_ref[:, 2] = dot(together, tail).astype(bf16).reshape(peers, 8, HALF)


def combine_weight_kernel(rank_ref, weight_ref, out_ref):
    block = pl.program_id(0)
    tokens, experts = rank_ref.shape
    rows = out_ref.shape[1]
    member = expert_of(block, rows, experts)
    ranked = dot_last(rank_ref[...].astype(bf16), member)
    weight = dot_last(weight_ref[...].astype(bf16), member)
    slot, second = slots(iota((tokens, rows), 1, f32))
    weight = jnp.where(ranked == slot, weight, 0.0)
    out_ref[:tokens] = jnp.where(second, 0.0, weight).astype(bf16)
    out_ref[tokens:] = jnp.where(second, weight, 0.0).astype(bf16)


def combine_kernel(got_ref, weight_ref, mixer_ref, out_ref, total):
    block = pl.program_id(0)
    tokens = mixer_ref.shape[0]

    @pl.when(block == 0)
    def _():
        total[...] = jnp.zeros_like(total)

    total[...] += dot(weight_ref[...], got_ref[...])

    @pl.when(block == pl.num_programs(0) - 1)
    def _():
        out_ref[:, :HALF] = (mixer_ref[:, :HALF].astype(f32) + total[:tokens]).astype(bf16)
        out_ref[:, HALF:] = (mixer_ref[:, HALF:].astype(f32) + total[tokens:]).astype(bf16)


def fixed(*shape):
    return pl.BlockSpec(shape, lambda *_: (0,) * len(shape))


def fixed_once(*shape):
    return pl.BlockSpec(
        shape, lambda *_: (0,) * len(shape), pipeline_mode=pl.Buffered(1)
    )


def by_rows(*shape):
    rest = (0,) * (len(shape) - 1)
    return pl.BlockSpec(shape, lambda i, *_: (i, *rest))


def by_lanes(*shape):
    return pl.BlockSpec(shape, lambda i, *_: (0, i))


def resident():
    return pl.BlockSpec(memory_space=pltpu.VMEM)


def shape_of(kind, *shape):
    return jax.ShapeDtypeStruct(shape, kind)


def stored(kind, *shape):
    return pltpu.HBM(shape, kind)


def from_hbm(*arrays):
    return [pltpu.with_memory_space_constraint(a, pltpu.HBM) for a in arrays]


def from_vmem(*arrays):
    return [pltpu.with_memory_space_constraint(a, pltpu.VMEM) for a in arrays]


def body(
    hidden,
    mixer_gain,
    gate_proj,
    value_proj,
    state_proj,
    log_decay,
    step_size,
    skip_gain,
    group_gain,
    out_proj,
    moe_gain,
    router,
    expert_ids,
    expert_gate_up,
    expert_down,
):
    rows = hidden.shape[0]
    heads = log_decay.shape[1]
    channels = heads * P_SIZE
    blocks = rows // Q
    seq_count = lax.axis_size("seq")
    exp_count = lax.axis_size("exp")
    peers = seq_count * exp_count
    place = lax.axis_index("exp")
    core, line = place % 2, place // 2
    lines = exp_count // 2
    own_rows = rows // exp_count
    slice_rows = N // seq_count
    experts = router.shape[1]
    slab_rows = experts * SLAB
    per_step = slab_rows // 4

    swap = [(i, i ^ 1) for i in range(exp_count)]
    other_proj = lax.ppermute(out_proj, "exp", swap)
    decay = log_decay.T
    step = step_size.T

    mixed, x, maps, enter, sent = pl.pallas_call(
        local_state_kernel,
        grid=(blocks,),
        in_specs=[
            by_rows(Q, D),
            fixed(1, D),
            fixed_once(D, channels),
            fixed_once(D, 2 * N),
            by_lanes(heads, Q),
            by_lanes(heads, Q),
        ],
        out_specs=[
            by_rows(Q, D),
            by_rows(Q, channels),
            by_rows(Q, 2 * N),
            by_rows(1, N, channels),
            fixed(seq_count, slice_rows + 8, channels),
        ],
        out_shape=[
            stored(bf16, rows, D),
            stored(bf16, rows, channels),
            stored(bf16, rows, 2 * N),
            stored(bf16, blocks, N, channels),
            shape_of(bf16, seq_count, slice_rows + 8, channels),
        ],
        scratch_shapes=[pltpu.VMEM((N, channels), f32), pltpu.VMEM((heads, 128), f32)],
        compiler_params=params(24),
        cost_estimate=cost(2 * rows * D * (channels + 2 * N), 16 * 2**20),
        name="local_state",
    )(*from_hbm(hidden, mixer_gain.reshape(1, D), value_proj, state_proj, decay, step))

    slices = lax.all_to_all(sent, "seq", split_axis=0, concat_axis=0, tiled=True)

    gate = pl.pallas_call(
        gate_kernel,
        grid=(blocks,),
        in_specs=[by_rows(Q, D), fixed_once(D, channels)],
        out_specs=by_rows(Q, channels),
        out_shape=stored(bf16, rows, channels),
        compiler_params=params(12),
        cost_estimate=cost(2 * rows * channels * D, 7 * 2**20),
        name="gate",
    )(*from_hbm(mixed, gate_proj))
    named, rank, picker = pl.pallas_call(
        route_kernel,
        grid=(4,),
        in_specs=[fixed(own_rows, expert_ids.shape[1])],
        out_specs=[
            fixed(own_rows, experts),
            fixed(own_rows, experts),
            by_rows(per_step, 2 * own_rows),
        ],
        out_shape=[
            shape_of(f32, own_rows, experts),
            shape_of(f32, own_rows, experts),
            stored(bf16, slab_rows, 2 * own_rows),
        ],
        scratch_shapes=[pltpu.VMEM((own_rows, experts), bf16)],
        compiler_params=params(12),
        cost_estimate=cost(2 * slab_rows * experts * own_rows, 4 * 2**20),
        name="route",
    )(expert_ids)
    slices, gate, named, rank, picker = lax.optimization_barrier(
        (slices, gate, named, rank, picker)
    )

    before = pl.pallas_call(
        prefix_kernel,
        out_shape=shape_of(bf16, seq_count, slice_rows, channels),
        compiler_params=pltpu.CompilerParams(vmem_limit_bytes=8 * 2**20),
        name="prefix",
    )(slices)
    incoming = lax.all_to_all(before, "seq", split_axis=0, concat_axis=0, tiled=True)
    incoming = incoming.reshape(N, channels)

    within = pl.pallas_call(
        within_kernel,
        grid=(blocks,),
        in_specs=[
            by_rows(Q, channels),
            by_rows(Q, 2 * N),
            by_lanes(heads, Q),
            by_lanes(heads, Q),
            by_rows(1, N, channels),
            fixed(1, channels),
        ],
        out_specs=by_rows(Q, channels),
        out_shape=stored(f32, rows, channels),
        compiler_params=params(16),
        cost_estimate=cost(4 * rows * channels * Q, 6 * 2**20, rows * Q * heads),
        name="within",
    )(
        *from_hbm(x, maps, decay, step, enter),
        jnp.repeat(skip_gain, P_SIZE).reshape(1, channels),
    )

    own, other = pl.pallas_call(
        normed_kernel,
        grid_spec=pltpu.PrefetchScalarGridSpec(
            num_scalar_prefetch=1,
            grid=(blocks,),
            in_specs=[
                by_rows(Q, channels),
                pl.BlockSpec((Q, N), lambda i, *_: (i, 1)),
                by_rows(Q, channels),
                by_lanes(heads, Q),
                fixed(N, channels),
                fixed(1, channels),
            ],
            out_specs=[by_rows(own_rows, channels), by_rows(own_rows, channels)],
            scratch_shapes=[pltpu.VMEM((heads, 128), f32)],
        ),
        out_shape=[shape_of(bf16, rows // 2, channels)] * 2,
        compiler_params=params(12),
        cost_estimate=cost(2 * rows * N * channels, 5 * 2**20),
        name="normed",
    )(
        core.reshape(1),
        *from_hbm(within, maps, gate, decay),
        incoming,
        group_gain.reshape(1, channels),
    )
    got = lax.ppermute(other, "exp", swap)

    projections = from_vmem(out_proj, other_proj)

    def project(target):
        return pl.pallas_call(
            project_kernel,
            grid_spec=pltpu.PrefetchScalarGridSpec(
                num_scalar_prefetch=1,
                grid=(1,),
                in_specs=[
                    pl.BlockSpec((own_rows, channels), lambda i, at: (at[0], 0)),
                    pl.BlockSpec((own_rows, channels), lambda i, at: (at[0], 0)),
                    resident(),
                    resident(),
                ],
                out_specs=fixed(own_rows, D),
            ),
            out_shape=shape_of(bf16, own_rows, D),
            compiler_params=params(8),
            cost_estimate=cost(4 * own_rows * channels * D, 5 * 2**20),
            name="project",
        )(target.reshape(1), own, got, *projections)

    pieces = []
    for hop in (2, 1, 3):
        partial = project((line + hop) % lines)
        pieces.append(
            lax.ppermute(
                partial, "exp", [(i, (i + 2 * hop) % exp_count) for i in range(exp_count)]
            )
        )
    mine = project(line)

    mixer_out, weight, outgoing = pl.pallas_call(
        dispatch_kernel,
        grid_spec=pltpu.PrefetchScalarGridSpec(
            num_scalar_prefetch=1,
            grid=(4,),
            in_specs=[fixed(own_rows, D)] * 4
            + [
                pl.BlockSpec((own_rows, D), lambda i, at: (at[0], 0)),
                fixed(1, D),
                fixed(D, experts),
                fixed(own_rows, experts),
                by_rows(per_step, 2 * own_rows),
            ],
            out_specs=[
                fixed(own_rows, D),
                fixed(own_rows, experts),
                by_rows(per_step, HALF),
            ],
            scratch_shapes=[pltpu.VMEM((2 * own_rows, HALF), bf16)],
        ),
        out_shape=[
            shape_of(bf16, own_rows, D),
            shape_of(f32, own_rows, experts),
            shape_of(bf16, slab_rows, HALF),
        ],
        compiler_params=params(24),
        cost_estimate=cost(4 * slab_rows * own_rows * HALF, 10 * 2**20),
        name="dispatch",
    )(
        place.reshape(1),
        mine,
        *pieces,
        *from_hbm(hidden, moe_gain.reshape(1, D), router),
        named,
        *from_hbm(picker),
    )

    arrived = lax.all_to_all(
        outgoing.reshape(peers, SLAB, HALF),
        ("seq", "exp"),
        split_axis=0,
        concat_axis=0,
        tiled=True,
    ).reshape(peers, 3, 8, HALF)
    group = peers // 4
    combine_weight = pl.pallas_call(
        combine_weight_kernel,
        grid=(4,),
        in_specs=[fixed(own_rows, experts), fixed(own_rows, experts)],
        out_specs=by_lanes(2 * own_rows, per_step),
        out_shape=stored(bf16, 2 * own_rows, slab_rows),
        compiler_params=params(12),
        cost_estimate=cost(4 * slab_rows * experts * own_rows, 4 * 2**20),
        name="combine_weight",
    )(rank, weight)

    def piece(index):
        return pl.BlockSpec((group, None, 8, HALF), lambda i: (i, index, 0, 0))

    results = pl.pallas_call(
        expert_kernel,
        grid=(4,),
        in_specs=[piece(0), piece(1), piece(2), resident(), resident()],
        out_specs=by_rows(group, 3, 8, HALF),
        out_shape=stored(bf16, peers, 3, 8, HALF),
        compiler_params=params(28),
        cost_estimate=cost(6 * peers * CAP * D * F, 22 * 2**20, peers * CAP * F),
        name="experts",
    )(arrived, arrived, arrived, *from_vmem(expert_gate_up, expert_down))
    returned = lax.all_to_all(
        results.reshape(peers, SLAB, HALF),
        ("seq", "exp"),
        split_axis=0,
        concat_axis=0,
        tiled=True,
    ).reshape(slab_rows, HALF)

    layer_out = pl.pallas_call(
        combine_kernel,
        grid=(4,),
        in_specs=[
            by_rows(per_step, HALF),
            by_lanes(2 * own_rows, per_step),
            fixed(own_rows, D),
        ],
        out_specs=fixed(own_rows, D),
        out_shape=shape_of(bf16, own_rows, D),
        scratch_shapes=[pltpu.VMEM((2 * own_rows, HALF), f32)],
        compiler_params=params(16),
        cost_estimate=cost(4 * slab_rows * own_rows * HALF, 8 * 2**20),
        name="combine",
    )(*from_hbm(returned, combine_weight, mixer_out))
    return (mixer_out, layer_out)


def solution(mesh):
    in_specs = (
        P("seq", None),
        P(),
        P(None, "exp"),
        P(None, "exp"),
        P(None, "exp"),
        P("seq", "exp"),
        P("seq", "exp"),
        P("exp"),
        P("exp"),
        P("exp", None),
        P(),
        P(),
        P(("seq", "exp"), None),
        P(("seq", "exp"), None, None),
        P(("seq", "exp"), None, None),
    )
    out_specs = (P(("seq", "exp"), None), P(("seq", "exp"), None))
    return jax.shard_map(body, mesh=mesh, in_specs=in_specs, out_specs=out_specs, check_vma=False)
```

time: 296 us -> 278 us (0.939)
  blocking collectives: 167 us -> 83.5 us
  waiting for transfers between devices: 22.1 us -> 89.4 us
  starting transfers between devices: 20 us -> 29.9 us
  local copies, waits for them, and re-layouts: 8.78 us -> 0.28 us
    all_to_all x1 -> x0, blocking collectives: 81.5 us -> none  [body(): lax.all_to_all(results.reshape(peers, SLAB, HALF), ('seq', 'exp'), split_...]
    all_to_all x0 -> x1, waiting for transfers between devices: none -> 73.2 us  [body(): lax.all_to_all(results.reshape(peers, SLAB, HALF), ('seq', 'exp'), split_...]
    unnamed x35 -> x15, local copies, waits for them, and re-layouts: 8.78 us -> 0.13 us
    pallas_call x1 -> x4, Pallas kernels: 9.92 us -> 18 us  [the longest x1 6.16 us: body(): pl.pallas_call(gate_kernel, grid=(blocks,), in_specs=[by_rows(Q, D), fixe...]
    all_to_all x1, waiting for transfers between devices: 7.81 us -> 0.01 us  [body(): lax.all_to_all(sent, 'seq', split_axis=0, concat_axis=0, tiled=True)]
    all_to_all x0 -> x1, starting transfers between devices: none -> 6.4 us  [body(): lax.all_to_all(results.reshape(peers, SLAB, HALF), ('seq', 'exp'), split_...]
    pallas_call x1, Pallas kernels: 21.6 us -> 18.3 us  [body(): pl.pallas_call(expert_kernel, grid=(4,), in_specs=[piece(0), piece(1), pi...]
  transfers between devices with their start and end apart: 7 -> 8, of which waited for: 4 -> 5; matrix products, arithmetic and copies ran while one was open for 1% -> 0% of each run, Pallas kernels for 13% -> 15%
where the time goes in v2:
time: 278 us
  waiting for transfers between devices  89.4 us (32%)
  blocking collectives  83.5 us (30%)
  Pallas kernels  73.7 us (27%)
  starting transfers between devices  29.9 us (11%)
    all_to_all x1, blocking collectives, body(): lax.all_to_all(outgoing.reshape(peers, SLAB, HALF), ('seq', 'exp'), split...  83.5 us
    all_to_all x1, waiting for transfers between devices, body(): lax.all_to_all(results.reshape(peers, SLAB, HALF), ('seq', 'exp'), split_...  73.2 us
    pallas_call x1, Pallas kernels, body(): pl.pallas_call(expert_kernel, grid=(4,), in_specs=[piece(0), piece(1), pi...  18.3 us
    ppermute x3, waiting for transfers between devices, body(): lax.ppermute(partial, 'exp', [(i, (i + 2 * hop) % exp_count) for i in ran...  13.9 us
    pallas_call x1, Pallas kernels, body(): pl.pallas_call(local_state_kernel, grid=(blocks,), in_specs=[by_rows(Q, D...  10.6 us
    pallas_call x4, Pallas kernels, project(): pl.pallas_call(project_kernel, grid_spec=pltpu.PrefetchScalarGridSpec(num...  9.21 us
    all_to_all x1, starting transfers between devices, body(): lax.all_to_all(sent, 'seq', split_axis=0, concat_axis=0, tiled=True)  7.7 us
    all_to_all x1, starting transfers between devices, body(): lax.all_to_all(before, 'seq', split_axis=0, concat_axis=0, tiled=True)  6.65 us
  transfers between devices with their start and end apart: 8, of which 5 were waited for; matrix products, arithmetic and copies ran while one was open for 0% of the time, Pallas kernels for 15%

profile of v2, /device:TPU:1, one launch (start us, length us, event | category | flops | bytes accessed | tf_op | source)
XLA Modules:
  0.0 277.5 jit_solution(7598272800754744722)
XLA Ops:
  0.6 1.5 collective-permute-start.1
  2.1 10.6 %local_state.1 = (bf16[1024,2048]{1,0:T(8,128)(2,1)}, bf16[1024,512]{1,0:T(8,128)(2,1)}, bf16[1024,256]{1,0:T(8,128)(2,1)}, bf16[4,128,512]{2,1,0:T(8,128)(2,1)}, bf16[16,16,512]{2,1,0:T(8,128)(2,1)}) custom-call(bf16[1024,2048]{1,0:T(8,128)(2,1)} %hidden_ref.3, f32[1,2048]{1,0:T(1,128)} %bitcast.31, bf16[2048,512]{1,0:T(8,128)(2,1)} %value_ref.1, ...), custom_call_target="tpu_custom_call" | custom-call | flops 3221225472 | bytes 16777216 | tf_op jit(solution)/shard_map/local_state/pallas_call | solution.py:433
  12.8 7.7 %all-to-all-start = ((bf16[16,16,512]{2,1,0:T(8,128)(2,1)}), bf16[16,16,512]{2,1,0:T(8,128)(2,1)S(1)}, u32[]{:S(2)}, u32[]{:S(2)}) async-start(bf16[16,16,512]{2,1,0:T(8,128)(2,1)} %get-tuple-element.23), calls=%async_computation | async-start | bytes 524288 | tf_op jit(solution)/shard_map/all_to_all | solution.py:464
  20.5 0.1 copy.17.ids_ref
  20.6 3.1 %route.1 = (f32[128,128]{1,0:T(8,128)S(1)}, f32[128,128]{1,0:T(8,128)S(1)}, bf16[3072,256]{1,0:T(8,128)(2,1)}) custom-call(s32[128,8]{1,0:T(8,128)S(1)} %copy.17.ids_ref), custom_call_target="tpu_custom_call" | custom-call | flops 100663296 | bytes 4194304 | tf_op jit(solution)/shard_map/route/pallas_call | solution.py:476
  23.7 6.2 %gate.1.gate_ref = bf16[1024,512]{1,0:T(8,128)(2,1)} custom-call(bf16[1024,2048]{1,0:T(8,128)(2,1)} %get-tuple-element.24.mixed_ref, bf16[2048,512]{1,0:T(8,128)(2,1)} %gate_w_ref.1), custom_call_target="tpu_custom_call" | custom-call | flops 2147483648 | bytes 7340032 | tf_op jit(solution)/shard_map/gate/pallas_call | solution.py:466
  29.8 0.7 prefix.1
  30.6 6.7 %all-to-all-start.1 = ((bf16[16,8,512]{2,1,0:T(8,128)(2,1)}), bf16[16,8,512]{2,1,0:T(8,128)(2,1)S(1)}, u32[]{:S(2)}, u32[]{:S(2)}) async-start(bf16[16,8,512]{2,1,0:T(8,128)(2,1)} %prefix.1), calls=%async_computation.1 | async-start | bytes 262144 | tf_op jit(solution)/shard_map/all_to_all | solution.py:505
  37.3 0.1 broadcast_in_dim.3
  37.3 0.1 reshape_reshape.3.skip_ref
  37.4 6.1 %within.1.within_ref = f32[1024,512]{1,0:T(8,128)} custom-call(bf16[1024,512]{1,0:T(8,128)(2,1)} %get-tuple-element.20.x_ref, bf16[1024,256]{1,0:T(8,128)(2,1)} %get-tuple-element.21.maps_ref, f32[8,1024]{1,0:T(8,128)} %bitcast.26, f32[8,1024]{1,0:T(8,128)} %bitcast.29, bf16[4,128,512]{2,1,0:T(8,128)(2,1)} %get-tuple-element.22.enter_ref, ...), custom_call_target="tpu_custom_call" | custom-call | flops 536870912 | bytes 6291456 | tf_op jit(solution)/shard_map/within/pallas_call | solution.py:508
  43.5 0.6 all-to-all-done.1
  44.1 5.1 %normed.1 = (bf16[512,512]{1,0:T(8,128)(2,1)S(1)}, bf16[512,512]{1,0:T(8,128)(2,1)}) custom-call(s32[1]{0:T(128)} %bitcast.2.core_ref, f32[1024,512]{1,0:T(8,128)} %within.1.within_ref, bf16[1024,256]{1,0:T(8,128)(2,1)} %get-tuple-element.21.maps_ref, bf16[1024,512]{1,0:T(8,128)(2,1)} %gate.1.gate_ref, f32[8,1024]{1,0:T(8,128)} %bitcast.27, ...), custom_call_target="tpu_custom_call" | custom-call | flops 134217728 | bytes 5242880 | tf_op jit(solution)/shard_map/normed/pallas_call | solution.py:529
  49.2 1.9 collective-permute-start
  51.0 1.7 collective-permute-done.got_ref
  52.8 0.0 collective-permute-done.1.got_w_ref
  52.8 2.3 project.5
  55.1 3.0 %collective-permute-start.2 = (bf16[128,2048]{1,0:T(8,128)(2,1)S(1)}, bf16[128,2048]{1,0:T(8,128)(2,1)S(1)}, u32[]{:S(2)}, u32[]{:S(2)}) collective-permute-start(bf16[128,2048]{1,0:T(8,128)(2,1)S(1)} %project.5), channel_id=1, source_target_pairs={{0,4},{1,5},{2,6},{3,7},{4,0},{5,1},{6,2},{7,3},{8,12},{9,13},{10,... | collective-permute-start | bytes 1572872 | tf_op jit(solution)/shard_map/ppermute | solution.py:583
  58.1 2.3 project.6
  60.4 0.5 collective-permute-start.3
  60.9 2.3 project.7
  63.2 2.3 collective-permute-start.4
  65.5 2.3 project.4.a_ref
  67.8 2.0 collective-permute-done.2.b_ref
  69.9 11.9 %collective-permute-done.3.c_ref = bf16[128,2048]{1,0:T(8,128)(2,1)S(1)} collective-permute-done((bf16[128,2048]{1,0:T(8,128)(2,1)S(1)}, bf16[128,2048]{1,0:T(8,128)(2,1)S(1)}, u32[]{:S(2)}, u32[]{:S(2)}) %collective-permute-start.3) | collective-permute-done | bytes 524320 | tf_op jit(solution)/shard_map/ppermute | solution.py:583
  81.8 5.8 %dispatch.1 = (bf16[128,2048]{1,0:T(8,128)(2,1)}, f32[128,128]{1,0:T(8,128)S(1)}, bf16[3072,1024]{1,0:T(8,128)(2,1)S(1)}) custom-call(s32[1]{0:T(128)} %bitcast.where_ref, bf16[128,2048]{1,0:T(8,128)(2,1)S(1)} %project.4.a_ref, bf16[128,2048]{1,0:T(8,128)(2,1)S(1)} %collective-permute-done.2.b_ref, bf16[128,2048]{1,0:T(8,128)(2,1)S(1)} %collective-permute-done.3.c_ref, ...), custom_call_target="tpu_custom_call" | custom-call | flops 1610612736 | bytes 10485760 | tf_op jit(solution)/shard_map/dispatch/pallas_call | solution.py:589
  87.5 83.5 %all_to_all.20 = bf16[128,24,1024]{2,1,0:T(8,128)(2,1)S(1)} all-to-all(bf16[128,24,1024]{2,1,0:T(8,128)(2,1)S(1)} %bitcast.16), channel_id=1, replica_groups=mesh['seq'=16,'exp'=8] {'seq','exp'}, dimensions={0} | all-to-all | bytes 12582912 | tf_op jit(solution)/shard_map/all_to_all | solution.py:626
  171.0 18.3 %experts.1 = bf16[128,3,8,1024]{3,2,1,0:T(8,128)(2,1)} custom-call(bf16[128,3,8,1024]{3,2,1,0:T(8,128)(2,1)S(1)} %bitcast.17, bf16[128,3,8,1024]{3,2,1,0:T(8,128)(2,1)S(1)} %bitcast.18, bf16[128,3,8,1024]{3,2,1,0:T(8,128)(2,1)S(1)} %bitcast.19, bf16[1,2048,1536]{2,1,0:T(8,128)(2,1)S(1)} %bitcast.23, bf16[1,768,2048]{2,1,0:T(8,128)(2,1)S(1)} %copy-done.2), custom_call_target="tpu_custom_call" | custom-call | flops 14495514624 | bytes 23068672 | tf_op jit(solution)/shard_map/experts/pallas_call | solution.py:648
  189.4 6.4 %all-to-all-start.3 = ((bf16[128,24,1024]{2,1,0:T(8,128)(2,1)}), bf16[128,24,1024]{2,1,0:T(8,128)(2,1)}, u32[]{:S(2)}, u32[]{:S(2)}) async-start(bf16[128,24,1024]{2,1,0:T(8,128)(2,1)} %bitcast.24), calls=%async_computation.3 | async-start | bytes 12582912 | tf_op jit(solution)/shard_map/all_to_all | solution.py:658
  195.8 2.6 combine_weight.1.weight_ref
  198.4 73.2 %all-to-all-done.3 = bf16[128,24,1024]{2,1,0:T(8,128)(2,1)} async-done(((bf16[128,24,1024]{2,1,0:T(8,128)(2,1)}), bf16[128,24,1024]{2,1,0:T(8,128)(2,1)}, u32[]{:S(2)}, u32[]{:S(2)}) %all-to-all-start.3) | async-done | bytes 6291488 | tf_op jit(solution)/shard_map/all_to_all | solution.py:658
  271.6 6.0 %combine.1 = bf16[128,2048]{1,0:T(8,128)(2,1)} custom-call(bf16[3072,1024]{1,0:T(8,128)(2,1)} %bitcast.15.got_ref, bf16[256,3072]{1,0:T(8,128)(2,1)} %combine_weight.1.weight_ref, bf16[128,2048]{1,0:T(8,128)(2,1)} %get-tuple-element.18.mixer_ref), custom_call_target="tpu_custom_call" | custom-call | flops 1610612736 | bytes 8388608 | tf_op jit(solution)/shard_map/combine/pallas_call | solution.py:666
  (17 shorter events, 0.0 us)
Async XLA Ops:
  0.6 52.2 %collective-permute-start.1 = (bf16[512,2048]{1,0:T(8,128)(2,1)}, bf16[512,2048]{1,0:T(8,128)(2,1)}, u32[]{:S(2)}, u32[]{:S(2)}) collective-permute-start(bf16[512,2048]{1,0:T(8,128)(2,1)} %own_w_ref.7), channel_id=1, source_target_pairs={{0,1},{1,0},{2,3},{3,2},{4,5},{5,4},{6,7},{7,6},{8,9},{9,8},{10,11... | collective-permute-start | bytes 6291464 | tf_op jit(solution)/shard_map/ppermute | solution.py:429
  2.1 18.4 %copy-start.3 = (s32[128,8]{0,1:T(8,128)S(1)}, s32[128,8]{0,1:T(8,128)}, u32[]{:S(2)}) copy-start(s32[128,8]{0,1:T(8,128)} %param.27) | copy-start | bytes 12292
  12.8 17.1 %all-to-all-start = ((bf16[16,16,512]{2,1,0:T(8,128)(2,1)}), bf16[16,16,512]{2,1,0:T(8,128)(2,1)S(1)}, u32[]{:S(2)}, u32[]{:S(2)}) async-start(bf16[16,16,512]{2,1,0:T(8,128)(2,1)} %get-tuple-element.23), calls=%async_computation | async-start | bytes 524288 | tf_op jit(solution)/shard_map/all_to_all | solution.py:464
  23.7 13.6 %copy-start.4 = (f32[8]{0:T(128)S(1)}, f32[8]{0:T(128)}, u32[]{:S(2)}) copy-start(f32[8]{0:T(128)} %param.22) | copy-start | bytes 100
  29.8 14.2 %copy-start.1 = (f32[512]{0:T(512)S(1)}, f32[512]{0:T(512)}, u32[]{:S(2)}) copy-start(f32[512]{0:T(512)} %param.23) | copy-start | bytes 6148
  30.6 13.5 %all-to-all-start.1 = ((bf16[16,8,512]{2,1,0:T(8,128)(2,1)}), bf16[16,8,512]{2,1,0:T(8,128)(2,1)S(1)}, u32[]{:S(2)}, u32[]{:S(2)}) async-start(bf16[16,8,512]{2,1,0:T(8,128)(2,1)} %prefix.1), calls=%async_computation.1 | async-start | bytes 262144 | tf_op jit(solution)/shard_map/all_to_all | solution.py:505
  37.4 15.4 %copy-start = (bf16[512,2048]{1,0:T(8,128)(2,1)S(1)}, bf16[512,2048]{1,0:T(8,128)(2,1)}, u32[]{:S(2)}) copy-start(bf16[512,2048]{1,0:T(8,128)(2,1)} %own_w_ref.7) | copy-start | bytes 6291460
  49.2 3.6 %collective-permute-start = (bf16[512,512]{1,0:T(8,128)(2,1)}, bf16[512,512]{1,0:T(8,128)(2,1)S(1)}, u32[]{:S(2)}, u32[]{:S(2)}) collective-permute-start(bf16[512,512]{1,0:T(8,128)(2,1)} %get-tuple-element.31), channel_id=1, source_target_pairs={{0,1},{1,0},{2,3},{3,2},{4,5},{5,4},{6,7},{7,6},{8,9},{9,8},{10,11... | collective-permute-start | bytes 1572872 | tf_op jit(solution)/shard_map/ppermute | solution.py:555
  55.1 14.8 %collective-permute-start.2 = (bf16[128,2048]{1,0:T(8,128)(2,1)S(1)}, bf16[128,2048]{1,0:T(8,128)(2,1)S(1)}, u32[]{:S(2)}, u32[]{:S(2)}) collective-permute-start(bf16[128,2048]{1,0:T(8,128)(2,1)S(1)} %project.5), channel_id=1, source_target_pairs={{0,4},{1,5},{2,6},{3,7},{4,0},{5,1},{6,2},{7,3},{8,12},{9,13},{10,... | collective-permute-start | bytes 1572872 | tf_op jit(solution)/shard_map/ppermute | solution.py:583
  60.4 21.4 %collective-permute-start.3 = (bf16[128,2048]{1,0:T(8,128)(2,1)S(1)}, bf16[128,2048]{1,0:T(8,128)(2,1)S(1)}, u32[]{:S(2)}, u32[]{:S(2)}) collective-permute-start(bf16[128,2048]{1,0:T(8,128)(2,1)S(1)} %project.6), channel_id=1, source_target_pairs={{0,2},{1,3},{2,4},{3,5},{4,6},{5,7},{6,0},{7,1},{8,10},{9,11},{10,... | collective-permute-start | bytes 1572872 | tf_op jit(solution)/shard_map/ppermute | solution.py:583
  63.2 18.6 %collective-permute-start.4 = (bf16[128,2048]{1,0:T(8,128)(2,1)S(1)}, bf16[128,2048]{1,0:T(8,128)(2,1)S(1)}, u32[]{:S(2)}, u32[]{:S(2)}) collective-permute-start(bf16[128,2048]{1,0:T(8,128)(2,1)S(1)} %project.7), channel_id=1, source_target_pairs={{0,6},{1,7},{2,0},{3,1},{4,2},{5,3},{6,4},{7,5},{8,14},{9,15},{10,... | collective-permute-start | bytes 1572872 | tf_op jit(solution)/shard_map/ppermute | solution.py:583
  81.8 89.2 %slice-start = ((s8[6291456]{0:T(1024)(128)(4,1)}), s8[2097152]{0:T(1024)(128)(4,1)S(1)}, s32[]{:S(2)}) async-start(s8[6291456]{0:T(1024)(128)(4,1)} %bitcast.22), calls=%async_computation.4 | async-start | bytes 4194304
  87.5 83.5 %slice-start.1 = ((s8[6291456]{0:T(1024)(128)(4,1)}), s8[4194304]{0:T(1024)(128)(4,1)S(1)}, s32[]{:S(2)}) async-start(s8[6291456]{0:T(1024)(128)(4,1)} %bitcast.22), calls=%async_computation.5 | async-start | bytes 8388608
  87.5 83.5 %copy-start.2 = (bf16[1,768,2048]{2,1,0:T(8,128)(2,1)S(1)}, bf16[1,768,2048]{2,1,0:T(8,128)(2,1)}, u32[]{:S(2)}) copy-start(bf16[1,768,2048]{2,1,0:T(8,128)(2,1)} %down_ref.1) | copy-start | bytes 9437188
  189.4 82.2 %all-to-all-start.3 = ((bf16[128,24,1024]{2,1,0:T(8,128)(2,1)}), bf16[128,24,1024]{2,1,0:T(8,128)(2,1)}, u32[]{:S(2)}, u32[]{:S(2)}) async-start(bf16[128,24,1024]{2,1,0:T(8,128)(2,1)} %bitcast.24), calls=%async_computation.3 | async-start | bytes 12582912 | tf_op jit(solution)/shard_map/all_to_all | solution.py:658

commit v3 on v2

--- a/solution.py
+++ b/solution.py
@@ -214,10 +214,31 @@
     other_ref[...] = jnp.where(mine, second, first).astype(bf16)
 
 
-def project_kernel(where_ref, own_ref, got_ref, own_w_ref, got_w_ref, out_ref):
-    out_ref[...] = (
-        dot(own_ref[...], own_w_ref[...]) + dot(got_ref[...], got_w_ref[...])
-    ).astype(bf16)
+def own_part_kernel(at_ref, own_ref, own_w_ref, got_w_ref, part_ref, kept_ref):
+    part_ref[...] = dot(own_ref[...], own_w_ref[...])
+    kept_ref[...] = got_w_ref[...]
+
+
+def finish_kernel(at_ref, part_ref, got_ref, got_w_ref, left_ref, right_ref):
+    out = part_ref[...] + dot(got_ref[...], got_w_ref[...])
+    left_ref[...] = out[:, :HALF].astype(bf16)
+    right_ref[...] = out[:, HALF:].astype(bf16)
+
+
+def halves_kernel(
+    at_ref, own_a_ref, got_a_ref, own_b_ref, got_b_ref, own_w_ref, got_w_ref, *rest
+):
+    *more, a_ref, b_ref = rest
+    halves = (slice(0, HALF), slice(HALF, D))
+    if not more:
+        halves = halves[::-1]
+    a = dot(own_a_ref[...], own_w_ref[:, halves[0]]) + dot(got_a_ref[...], got_w_ref[:, halves[0]])
+    b = dot(own_b_ref[...], own_w_ref[:, halves[1]]) + dot(got_b_ref[...], got_w_ref[:, halves[1]])
+    if more:
+        a = a + more[0][...].astype(f32)
+        b = b + more[1][...].astype(f32)
+    a_ref[...] = a.astype(bf16)
+    b_ref[...] = b.astype(bf16)
 
 
 def slots(row):
@@ -259,10 +280,12 @@
 
 def dispatch_kernel(
     where_ref,
-    a_ref,
-    b_ref,
-    c_ref,
-    d_ref,
+    left_a_ref,
+    left_b_ref,
+    left_c_ref,
+    right_a_ref,
+    right_b_ref,
+    right_c_ref,
     hidden_ref,
     gain_ref,
     router_ref,
@@ -271,30 +294,24 @@
     mixer_ref,
     weight_ref,
     out_ref,
-    rows_in,
 ):
-    block = pl.program_id(0)
-    tokens = named_ref.shape[0]
-
-    @pl.when(block == 0)
-    def _():
-        head_sum = (
-            a_ref[...].astype(f32)
-            + b_ref[...].astype(f32)
-            + c_ref[...].astype(f32)
-            + d_ref[...].astype(f32)
-        )
-        mixer_out = (hidden_ref[...].astype(f32) + head_sum).astype(bf16)
-        mixer_ref[...] = mixer_out
-        wide = mixer_out.astype(f32)
-        scale = lax.rsqrt(jnp.mean(wide * wide, axis=-1, keepdims=True) + epsilon)
-        expert_input = (wide * scale * gain_ref[...]).astype(bf16)
-        rows_in[:tokens, :] = expert_input[:, :HALF]
-        rows_in[tokens:, :] = expert_input[:, HALF:]
-        picked = named_ref[...] * jax.nn.sigmoid(dot(expert_input, router_ref[...]))
-        weight_ref[...] = picked / jnp.sum(picked, axis=-1, keepdims=True)
-
-    out_ref[...] = dot(picker_ref[...], rows_in[...]).astype(bf16)
+    left = left_a_ref[...].astype(f32) + left_b_ref[...].astype(f32)
+    right = right_a_ref[...].astype(f32) + right_b_ref[...].astype(f32)
+    head_sum = jnp.concatenate(
+        [left + left_c_ref[...].astype(f32), right + right_c_ref[...].astype(f32)], axis=1
+    )
+    mixer_out = (hidden_ref[...].astype(f32) + head_sum).astype(bf16)
+    mixer_ref[...] = mixer_out
+    wide = mixer_out.astype(f32)
+    scale = lax.rsqrt(jnp.mean(wide * wide, axis=-1, keepdims=True) + epsilon)
+    expert_input = (wide * scale * gain_ref[...]).astype(bf16)
+    rows_in = jnp.concatenate([expert_input[:, :HALF], expert_input[:, HALF:]], axis=0)
+    picked = named_ref[...] * jax.nn.sigmoid(dot(expert_input, router_ref[...]))
+    weight_ref[...] = picked / jnp.sum(picked, axis=-1, keepdims=True)
+    step = out_ref.shape[0] // 8
+    for i in range(8):
+        part = slice(i * step, (i + 1) * step)
+        out_ref[part] = dot(picker_ref[part], rows_in).astype(bf16)
 
 
 def expert_kernel(a_ref, b_ref, c_ref, up_ref, down_ref, out_ref):
@@ -337,20 +354,24 @@
     out_ref[tokens:] = jnp.where(second, weight, 0.0).astype(bf16)
 
 
-def combine_kernel(got_ref, weight_ref, mixer_ref, out_ref, total):
-    block = pl.program_id(0)
+def combine_kernel(got_ref, weight_ref, mixer_ref, out_ref, held, ready):
     tokens = mixer_ref.shape[0]
-
-    @pl.when(block == 0)
-    def _():
-        total[...] = jnp.zeros_like(total)
-
-    total[...] += dot(weight_ref[...], got_ref[...])
-
-    @pl.when(block == pl.num_programs(0) - 1)
-    def _():
-        out_ref[:, :HALF] = (mixer_ref[:, :HALF].astype(f32) + total[:tokens]).astype(bf16)
-        out_ref[:, HALF:] = (mixer_ref[:, HALF:].astype(f32) + total[tokens:]).astype(bf16)
+    parts, group = held.shape[0], held.shape[1]
+    rows = group * SLAB
+
+    def fetch(i):
+        return pltpu.make_async_copy(
+            got_ref.at[pl.ds(i * group, group)], held.at[i], ready.at[i]
+        )
+
+    for i in range(parts):
+        fetch(i).start()
+    total = jnp.zeros((2 * tokens, HALF), f32)
+    for i in range(parts):
+        fetch(i).wait()
+        total += dot(weight_ref[:, i * rows : (i + 1) * rows], held[i].reshape(rows, HALF))
+    out_ref[:, :HALF] = (mixer_ref[:, :HALF].astype(f32) + total[:tokens]).astype(bf16)
+    out_ref[:, HALF:] = (mixer_ref[:, HALF:].astype(f32) + total[tokens:]).astype(bf16)
 
 
 def fixed(*shape):
@@ -473,28 +494,7 @@
         cost_estimate=cost(2 * rows * channels * D, 7 * 2**20),
         name="gate",
     )(*from_hbm(mixed, gate_proj))
-    named, rank, picker = pl.pallas_call(
-        route_kernel,
-        grid=(4,),
-        in_specs=[fixed(own_rows, expert_ids.shape[1])],
-        out_specs=[
-            fixed(own_rows, experts),
-            fixed(own_rows, experts),
-            by_rows(per_step, 2 * own_rows),
-        ],
-        out_shape=[
-            shape_of(f32, own_rows, experts),
-            shape_of(f32, own_rows, experts),
-            stored(bf16, slab_rows, 2 * own_rows),
-        ],
-        scratch_shapes=[pltpu.VMEM((own_rows, experts), bf16)],
-        compiler_params=params(12),
-        cost_estimate=cost(2 * slab_rows * experts * own_rows, 4 * 2**20),
-        name="route",
-    )(expert_ids)
-    slices, gate, named, rank, picker = lax.optimization_barrier(
-        (slices, gate, named, rank, picker)
-    )
+    slices, gate = lax.optimization_barrier((slices, gate))
 
     before = pl.pallas_call(
         prefix_kernel,
@@ -525,6 +525,8 @@
         *from_hbm(x, maps, decay, step, enter),
         jnp.repeat(skip_gain, P_SIZE).reshape(1, channels),
     )
+
+    incoming, within = lax.optimization_barrier((incoming, within))
 
     own, other = pl.pallas_call(
         normed_kernel,
@@ -554,73 +556,123 @@
     )
     got = lax.ppermute(other, "exp", swap)
 
-    projections = from_vmem(out_proj, other_proj)
-
-    def project(target):
+    at = jnp.stack([(line + hop) % lines for hop in range(lines)])
+
+    def rows_of(hop):
+        return pl.BlockSpec((own_rows, channels), lambda i, at: (at[hop], 0))
+
+    def project(kernel, in_specs, out_specs, out_shape, share, name):
         return pl.pallas_call(
-            project_kernel,
+            kernel,
             grid_spec=pltpu.PrefetchScalarGridSpec(
-                num_scalar_prefetch=1,
-                grid=(1,),
-                in_specs=[
-                    pl.BlockSpec((own_rows, channels), lambda i, at: (at[0], 0)),
-                    pl.BlockSpec((own_rows, channels), lambda i, at: (at[0], 0)),
-                    resident(),
-                    resident(),
-                ],
-                out_specs=fixed(own_rows, D),
+                num_scalar_prefetch=1, grid=(1,), in_specs=in_specs, out_specs=out_specs
             ),
-            out_shape=shape_of(bf16, own_rows, D),
-            compiler_params=params(8),
-            cost_estimate=cost(4 * own_rows * channels * D, 5 * 2**20),
-            name="project",
-        )(target.reshape(1), own, got, *projections)
-
-    pieces = []
-    for hop in (2, 1, 3):
-        partial = project((line + hop) % lines)
-        pieces.append(
-            lax.ppermute(
-                partial, "exp", [(i, (i + 2 * hop) % exp_count) for i in range(exp_count)]
-            )
+            out_shape=out_shape,
+            compiler_params=params(10),
+            cost_estimate=cost(share * own_rows * channels * D, 3 * 2**20),
+            name=name,
         )
-    mine = project(line)
+
+    half = fixed(own_rows, HALF)
+    half_pair = [shape_of(bf16, own_rows, HALF)] * 2
+
+    own_w = from_vmem(out_proj)
+    part, got_w = project(
+        own_part_kernel,
+        [rows_of(2), resident(), fixed(channels, D)],
+        [fixed(own_rows, D), resident()],
+        [pltpu.VMEM((own_rows, D), f32), pltpu.VMEM((channels, D), bf16)],
+        2,
+        "own_part",
+    )(at, own, *own_w, *from_hbm(other_proj))
+    got, part = lax.optimization_barrier((got, part))
+    projections = own_w + from_vmem(got_w)
+
+    def halves(at, hop_a, hop_b, *arrived):
+        return project(
+            halves_kernel,
+            [rows_of(hop_a), rows_of(hop_a), rows_of(hop_b), rows_of(hop_b)]
+            + [resident(), resident()]
+            + [half] * len(arrived),
+            [half, half],
+            half_pair,
+            4,
+            "halves",
+        )(at, own, got, own, got, *projections, *arrived)
+
+    def send(piece, hop):
+        moves = [(i, (i + 2 * hop) % exp_count) for i in range(exp_count)]
+        return lax.ppermute(piece, "exp", moves)
+
+    far_left, far_right = project(
+        finish_kernel,
+        [fixed(own_rows, D), rows_of(2), resident()],
+        [half, half],
+        half_pair,
+        2,
+        "finish",
+    )(at, part, got, projections[1])
+    via_next, via_last = send(far_left, 1), send(far_right, 3)
+    next_right, last_left = halves(at, 1, 3)
+    right_pieces = [send(next_right, 1)]
+    left_pieces = [send(last_left, 3)]
+    next_left, last_right = halves(at, 1, 3, via_next, via_last)
+    left_pieces.append(send(next_left, 1))
+    right_pieces.append(send(last_right, 3))
+    late_at, late_ids, _ = lax.optimization_barrier((at, expert_ids, next_left))
+    mine_right, mine_left = halves(late_at, 0, 0)
+    left_pieces.append(mine_left)
+    right_pieces.append(mine_right)
+    named, rank, picker = pl.pallas_call(
+        route_kernel,
+        grid=(4,),
+        in_specs=[fixed(own_rows, expert_ids.shape[1])],
+        out_specs=[
+            fixed(own_rows, experts),
+            fixed(own_rows, experts),
+            by_rows(per_step, 2 * own_rows),
+        ],
+        out_shape=[
+            shape_of(f32, own_rows, experts),
+            shape_of(f32, own_rows, experts),
+            stored(bf16, slab_rows, 2 * own_rows),
+        ],
+        scratch_shapes=[pltpu.VMEM((own_rows, experts), bf16)],
+        compiler_params=params(12),
+        cost_estimate=cost(2 * slab_rows * experts * own_rows, 4 * 2**20),
+        name="route",
+    )(late_ids)
 
     mixer_out, weight, outgoing = pl.pallas_call(
         dispatch_kernel,
         grid_spec=pltpu.PrefetchScalarGridSpec(
             num_scalar_prefetch=1,
-            grid=(4,),
-            in_specs=[fixed(own_rows, D)] * 4
+            grid=(1,),
+            in_specs=[fixed(own_rows, HALF)] * 6
             + [
                 pl.BlockSpec((own_rows, D), lambda i, at: (at[0], 0)),
                 fixed(1, D),
                 fixed(D, experts),
                 fixed(own_rows, experts),
-                by_rows(per_step, 2 * own_rows),
+                resident(),
             ],
-            out_specs=[
-                fixed(own_rows, D),
-                fixed(own_rows, experts),
-                by_rows(per_step, HALF),
-            ],
-            scratch_shapes=[pltpu.VMEM((2 * own_rows, HALF), bf16)],
+            out_specs=[fixed(own_rows, D), fixed(own_rows, experts), resident()],
         ),
         out_shape=[
             shape_of(bf16, own_rows, D),
             shape_of(f32, own_rows, experts),
-            shape_of(bf16, slab_rows, HALF),
+            pltpu.VMEM((slab_rows, HALF), bf16),
         ],
         compiler_params=params(24),
         cost_estimate=cost(4 * slab_rows * own_rows * HALF, 10 * 2**20),
         name="dispatch",
     )(
         place.reshape(1),
-        mine,
-        *pieces,
+        *left_pieces,
+        *right_pieces,
         *from_hbm(hidden, moe_gain.reshape(1, D), router),
         named,
-        *from_hbm(picker),
+        *from_vmem(picker),
     )
 
     arrived = lax.all_to_all(
@@ -636,7 +688,7 @@
         grid=(4,),
         in_specs=[fixed(own_rows, experts), fixed(own_rows, experts)],
         out_specs=by_lanes(2 * own_rows, per_step),
-        out_shape=stored(bf16, 2 * own_rows, slab_rows),
+        out_shape=pltpu.VMEM((2 * own_rows, slab_rows), bf16),
         compiler_params=params(12),
         cost_estimate=cost(4 * slab_rows * experts * own_rows, 4 * 2**20),
         name="combine_weight",
@@ -661,23 +713,21 @@
         split_axis=0,
         concat_axis=0,
         tiled=True,
-    ).reshape(slab_rows, HALF)
+    )
 
     layer_out = pl.pallas_call(
         combine_kernel,
-        grid=(4,),
-        in_specs=[
-            by_rows(per_step, HALF),
-            by_lanes(2 * own_rows, per_step),
-            fixed(own_rows, D),
+        in_specs=[pl.BlockSpec(memory_space=pl.ANY), resident(), resident()],
+        out_specs=resident(),
+        out_shape=shape_of(bf16, own_rows, D),
+        scratch_shapes=[
+            pltpu.VMEM((8, peers // 8, SLAB, HALF), bf16),
+            pltpu.SemaphoreType.DMA((8,)),
         ],
-        out_specs=fixed(own_rows, D),
-        out_shape=shape_of(bf16, own_rows, D),
-        scratch_shapes=[pltpu.VMEM((2 * own_rows, HALF), f32)],
-        compiler_params=params(16),
+        compiler_params=pltpu.CompilerParams(vmem_limit_bytes=24 * 2**20),
         cost_estimate=cost(4 * slab_rows * own_rows * HALF, 8 * 2**20),
         name="combine",
-    )(*from_hbm(returned, combine_weight, mixer_out))
+    )(*from_hbm(returned), *from_vmem(combine_weight, mixer_out))
     return (mixer_out, layer_out)
 
 

time: 278 us -> 267 us (0.960)
  waiting for transfers between devices: 89.4 us -> 81.1 us
  Pallas kernels: 73.7 us -> 69.3 us
    ppermute x3 -> x6, waiting for transfers between devices: 13.9 us -> 4.55 us  [send(): return lax.ppermute(piece, 'exp', moves)]
    pallas_call x5 -> x6, Pallas kernels: 15.2 us -> 13.7 us  [the longest x3 5.16 us: halves(): project(halves_kernel, [rows_of(hop_a), rows_of(hop_a), rows_of(hop_b), r...]
    ppermute x3 -> x6, starting transfers between devices: 5.8 us -> 6.86 us  [send(): return lax.ppermute(piece, 'exp', moves)]
  transfers between devices with their start and end apart: 8 -> 11, of which waited for: 5 -> 6; matrix products, arithmetic and copies ran while one was open for 0% -> 0% of each run, Pallas kernels for 15% -> 15%
where the time goes in v3:
time: 267 us; the launch traced here: 266 us
  blocking collectives  83.4 us (31%)
  waiting for transfers between devices  81.1 us (30%)
  Pallas kernels  69.3 us (26%)
  starting transfers between devices  29.6 us (11%)
    all_to_all x1, blocking collectives, body(): lax.all_to_all(outgoing.reshape(peers, SLAB, HALF), ('seq', 'exp'), split...  83.4 us
    all_to_all x1, waiting for transfers between devices, body(): lax.all_to_all(results.reshape(peers, SLAB, HALF), ('seq', 'exp'), split_...  74.4 us
    pallas_call x1, Pallas kernels, body(): pl.pallas_call(expert_kernel, grid=(4,), in_specs=[piece(0), piece(1), pi...  18.4 us
    pallas_call x1, Pallas kernels, body(): pl.pallas_call(local_state_kernel, grid=(blocks,), in_specs=[by_rows(Q, D...  10.6 us
    all_to_all x1, starting transfers between devices, body(): lax.all_to_all(sent, 'seq', split_axis=0, concat_axis=0, tiled=True)  7.7 us
    ppermute x6, starting transfers between devices, send(): return lax.ppermute(piece, 'exp', moves)  6.86 us
    all_to_all x1, starting transfers between devices, body(): lax.all_to_all(results.reshape(peers, SLAB, HALF), ('seq', 'exp'), split_...  6.55 us
    pallas_call x1, Pallas kernels, body(): pl.pallas_call(gate_kernel, grid=(blocks,), in_specs=[by_rows(Q, D), fixe...  6.18 us
  transfers between devices with their start and end apart: 11, of which 6 were waited for; matrix products, arithmetic and copies ran while one was open for 0% of the time, Pallas kernels for 15%

profile of v3, /device:TPU:1, one launch (start us, length us, event | category | flops | bytes accessed | tf_op | source)
XLA Modules:
  0.0 266.2 jit_solution(3439129911796449148)
XLA Ops:
  0.6 1.5 collective-permute-start.1
  2.1 10.6 %local_state.1 = (bf16[1024,2048]{1,0:T(8,128)(2,1)}, bf16[1024,512]{1,0:T(8,128)(2,1)}, bf16[1024,256]{1,0:T(8,128)(2,1)}, bf16[4,128,512]{2,1,0:T(8,128)(2,1)}, bf16[16,16,512]{2,1,0:T(8,128)(2,1)}) custom-call(bf16[1024,2048]{1,0:T(8,128)(2,1)} %hidden_ref.3, f32[1,2048]{1,0:T(1,128)} %bitcast.30, bf16[2048,512]{1,0:T(8,128)(2,1)} %value_ref.1, ...), custom_call_target="tpu_custom_call" | custom-call | flops 3221225472 | bytes 16777216 | tf_op jit(solution)/shard_map/local_state/pallas_call | solution.py:454
  12.8 7.7 %all-to-all-start = ((bf16[16,16,512]{2,1,0:T(8,128)(2,1)}), bf16[16,16,512]{2,1,0:T(8,128)(2,1)S(1)}, u32[]{:S(2)}, u32[]{:S(2)}) async-start(bf16[16,16,512]{2,1,0:T(8,128)(2,1)} %get-tuple-element.33), calls=%async_computation | async-start | bytes 524288 | tf_op jit(solution)/shard_map/all_to_all | solution.py:485
  20.5 6.2 %gate.1.gate_ref = bf16[1024,512]{1,0:T(8,128)(2,1)} custom-call(bf16[1024,2048]{1,0:T(8,128)(2,1)} %get-tuple-element.34.mixed_ref, bf16[2048,512]{1,0:T(8,128)(2,1)} %gate_w_ref.1), custom_call_target="tpu_custom_call" | custom-call | flops 2147483648 | bytes 7340032 | tf_op jit(solution)/shard_map/gate/pallas_call | solution.py:487
  26.7 1.6 all-to-all-done.got_ref
  28.3 0.7 prefix.1
  29.0 5.1 %all-to-all-start.1 = ((bf16[16,8,512]{2,1,0:T(8,128)(2,1)}), bf16[16,8,512]{2,1,0:T(8,128)(2,1)S(1)}, u32[]{:S(2)}, u32[]{:S(2)}) async-start(bf16[16,8,512]{2,1,0:T(8,128)(2,1)} %prefix.1), calls=%async_computation.1 | async-start | bytes 262144 | tf_op jit(solution)/shard_map/all_to_all | solution.py:505
  34.2 6.1 %within.1.within_ref = f32[1024,512]{1,0:T(8,128)} custom-call(bf16[1024,512]{1,0:T(8,128)(2,1)} %get-tuple-element.36.x_ref, bf16[1024,256]{1,0:T(8,128)(2,1)} %get-tuple-element.37.maps_ref, f32[8,1024]{1,0:T(8,128)} %bitcast.25, f32[8,1024]{1,0:T(8,128)} %bitcast.28, bf16[4,128,512]{2,1,0:T(8,128)(2,1)} %get-tuple-element.38.enter_ref, ...), custom_call_target="tpu_custom_call" | custom-call | flops 536870912 | bytes 6291456 | tf_op jit(solution)/shard_map/within/pallas_call | solution.py:508
  40.3 0.6 all-to-all-done.1
  40.9 5.1 %normed.1 = (bf16[512,512]{1,0:T(8,128)(2,1)S(1)}, bf16[512,512]{1,0:T(8,128)(2,1)}) custom-call(s32[1]{0:T(128)} %bitcast.5.core_ref, f32[1024,512]{1,0:T(8,128)} %within.1.within_ref, bf16[1024,256]{1,0:T(8,128)(2,1)} %get-tuple-element.37.maps_ref, bf16[1024,512]{1,0:T(8,128)(2,1)} %gate.1.gate_ref, f32[8,1024]{1,0:T(8,128)} %bitcast.26, ...), custom_call_target="tpu_custom_call" | custom-call | flops 134217728 | bytes 5242880 | tf_op jit(solution)/shard_map/normed/pallas_call | solution.py:531
  46.0 1.9 collective-permute-start
  48.0 2.7 %own_part.1 = (f32[128,2048]{1,0:T(8,128)S(1)}, bf16[512,2048]{1,0:T(8,128)(2,1)S(1)}) custom-call(s32[4]{0:T(128)S(1)} %pad_add_fusion.at_ref, bf16[512,512]{1,0:T(8,128)(2,1)S(1)} %get-tuple-element.42.own_ref.own_a_ref.own_b_ref, bf16[512,2048]{1,0:T(8,128)(2,1)S(1)} %copy-done, bf16[512,2048]{1,0:T(8,128)(2,1)} %collective-permute-done.1.got_w_ref), custom_call_target="tpu_custom_call" | custom-call | flops 268435456 | bytes 3145728 | tf_op jit(solution)/shard_map/own_part/pallas_call | solution.py:580
  50.7 1.0 finish.1
  51.7 1.4 collective-permute-start.3
  53.1 1.5 collective-permute-start.4
  54.6 2.0 halves.3
  56.6 1.4 collective-permute-start.2
  58.0 3.1 %collective-permute-done.3.rest_0_ = bf16[128,1024]{1,0:T(8,128)(2,1)S(1)} collective-permute-done((bf16[128,1024]{1,0:T(8,128)(2,1)S(1)}, bf16[128,1024]{1,0:T(8,128)(2,1)S(1)}, u32[]{:S(2)}, u32[]{:S(2)}) %collective-permute-start.3) | collective-permute-done | bytes 262176 | tf_op jit(solution)/shard_map/ppermute | solution.py:605
  61.1 2.0 halves.4
  63.1 2.5 collective-permute-start.7
  65.7 3.1 %route.1 = (f32[128,128]{1,0:T(8,128)S(1)}, f32[128,128]{1,0:T(8,128)S(1)}, bf16[3072,256]{1,0:T(8,128)(2,1)}) custom-call(s32[128,8]{1,0:T(8,128)S(1)} %copy.17.ids_ref), custom_call_target="tpu_custom_call" | custom-call | flops 100663296 | bytes 4194304 | tf_op jit(solution)/shard_map/route/pallas_call | solution.py:626
  68.7 1.6 copy-done.2
  70.3 1.2 halves.5
  71.6 0.3 collective-permute-done.7.right_b_ref
  71.9 1.2 collective-permute-done.5.left_b_ref
  73.1 3.9 %dispatch.1 = (bf16[128,2048]{1,0:T(8,128)(2,1)}, f32[128,128]{1,0:T(8,128)S(1)}, bf16[3072,1024]{1,0:T(8,128)(2,1)S(1)}) custom-call(s32[1]{0:T(128)} %bitcast.where_ref, bf16[128,1024]{1,0:T(8,128)(2,1)S(1)} %collective-permute-done.2.left_a_ref, bf16[128,1024]{1,0:T(8,128)(2,1)} %collective-permute-done.5.left_b_ref, ...), custom_call_target="tpu_custom_call" | custom-call | flops 1610612736 | bytes 10485760 | tf_op jit(solution)/shard_map/dispatch/pallas_call | solution.py:646
  77.0 83.4 %all_to_all.20 = bf16[128,24,1024]{2,1,0:T(8,128)(2,1)S(1)} all-to-all(bf16[128,24,1024]{2,1,0:T(8,128)(2,1)S(1)} %bitcast.15), channel_id=1, replica_groups=mesh['seq'=16,'exp'=8] {'seq','exp'}, dimensions={0} | all-to-all | bytes 12582912 | tf_op jit(solution)/shard_map/all_to_all | solution.py:678
  160.4 18.4 %experts.1 = bf16[128,3,8,1024]{3,2,1,0:T(8,128)(2,1)} custom-call(bf16[128,3,8,1024]{3,2,1,0:T(8,128)(2,1)S(1)} %bitcast.16, bf16[128,3,8,1024]{3,2,1,0:T(8,128)(2,1)S(1)} %bitcast.17, bf16[128,3,8,1024]{3,2,1,0:T(8,128)(2,1)S(1)} %bitcast.18, bf16[1,2048,1536]{2,1,0:T(8,128)(2,1)S(1)} %bitcast.22, bf16[1,768,2048]{2,1,0:T(8,128)(2,1)S(1)} %copy-done.6), custom_call_target="tpu_custom_call" | custom-call | flops 14495514624 | bytes 23068672 | tf_op jit(solution)/shard_map/experts/pallas_call | solution.py:700
  178.8 6.6 %all-to-all-start.3 = ((bf16[128,24,1024]{2,1,0:T(8,128)(2,1)}), bf16[128,24,1024]{2,1,0:T(8,128)(2,1)}, u32[]{:S(2)}, u32[]{:S(2)}) async-start(bf16[128,24,1024]{2,1,0:T(8,128)(2,1)} %bitcast.23), calls=%async_computation.3 | async-start | bytes 12582912 | tf_op jit(solution)/shard_map/all_to_all | solution.py:710
  185.4 1.4 combine_weight.1.weight_ref
  186.8 74.4 %all-to-all-done.3.got_ref = bf16[128,24,1024]{2,1,0:T(8,128)(2,1)} async-done(((bf16[128,24,1024]{2,1,0:T(8,128)(2,1)}), bf16[128,24,1024]{2,1,0:T(8,128)(2,1)}, u32[]{:S(2)}, u32[]{:S(2)}) %all-to-all-start.3) | async-done | bytes 6291488 | tf_op jit(solution)/shard_map/all_to_all | solution.py:710
  261.2 4.9 %combine.1 = bf16[128,2048]{1,0:T(8,128)(2,1)} custom-call(bf16[128,24,1024]{2,1,0:T(8,128)(2,1)} %all-to-all-done.3.got_ref, bf16[256,3072]{1,0:T(8,128)(2,1)S(1)} %combine_weight.1.weight_ref, bf16[128,2048]{1,0:T(8,128)(2,1)S(1)} %copy-done.4), custom_call_target="tpu_custom_call" | custom-call | flops 1610612736 | bytes 8388608 | tf_op jit(solution)/shard_map/combine/pallas_call | solution.py:718
  (33 shorter events, 0.5 us)
Async XLA Ops:
  0.6 47.3 %collective-permute-start.1 = (bf16[512,2048]{1,0:T(8,128)(2,1)}, bf16[512,2048]{1,0:T(8,128)(2,1)}, u32[]{:S(2)}, u32[]{:S(2)}) collective-permute-start(bf16[512,2048]{1,0:T(8,128)(2,1)} %own_w_ref.7), channel_id=1, source_target_pairs={{0,1},{1,0},{2,3},{3,2},{4,5},{5,4},{6,7},{7,6},{8,9},{9,8},{10,11... | collective-permute-start | bytes 6291464 | tf_op jit(solution)/shard_map/ppermute | solution.py:450
  12.8 15.5 %all-to-all-start = ((bf16[16,16,512]{2,1,0:T(8,128)(2,1)}), bf16[16,16,512]{2,1,0:T(8,128)(2,1)S(1)}, u32[]{:S(2)}, u32[]{:S(2)}) async-start(bf16[16,16,512]{2,1,0:T(8,128)(2,1)} %get-tuple-element.33), calls=%async_computation | async-start | bytes 524288 | tf_op jit(solution)/shard_map/all_to_all | solution.py:485
  20.5 13.6 %copy-start.8 = (f32[8]{0:T(128)S(1)}, f32[8]{0:T(128)}, u32[]{:S(2)}) copy-start(f32[8]{0:T(128)} %param.22) | copy-start | bytes 100
  26.7 14.2 %copy-start.5 = (f32[512]{0:T(512)S(1)}, f32[512]{0:T(512)}, u32[]{:S(2)}) copy-start(f32[512]{0:T(512)} %param.23) | copy-start | bytes 6148
  29.0 11.9 %all-to-all-start.1 = ((bf16[16,8,512]{2,1,0:T(8,128)(2,1)}), bf16[16,8,512]{2,1,0:T(8,128)(2,1)S(1)}, u32[]{:S(2)}, u32[]{:S(2)}) async-start(bf16[16,8,512]{2,1,0:T(8,128)(2,1)} %prefix.1), calls=%async_computation.1 | async-start | bytes 262144 | tf_op jit(solution)/shard_map/all_to_all | solution.py:505
  34.2 13.7 %copy-start = (bf16[512,2048]{1,0:T(8,128)(2,1)S(1)}, bf16[512,2048]{1,0:T(8,128)(2,1)}, u32[]{:S(2)}) copy-start(bf16[512,2048]{1,0:T(8,128)(2,1)} %own_w_ref.7) | copy-start | bytes 6291460
  46.0 4.7 %collective-permute-start = (bf16[512,512]{1,0:T(8,128)(2,1)}, bf16[512,512]{1,0:T(8,128)(2,1)S(1)}, u32[]{:S(2)}, u32[]{:S(2)}) collective-permute-start(bf16[512,512]{1,0:T(8,128)(2,1)} %get-tuple-element.43), channel_id=1, source_target_pairs={{0,1},{1,0},{2,3},{3,2},{4,5},{5,4},{6,7},{7,6},{8,9},{9,8},{10,11... | collective-permute-start | bytes 1572872 | tf_op jit(solution)/shard_map/ppermute | solution.py:557
  50.7 10.4 %copy-start.1 = (bf16[512,2048]{1,0:T(8,128)(2,1)}, bf16[512,2048]{1,0:T(8,128)(2,1)S(1)}, u32[]{:S(2)}) copy-start(bf16[512,2048]{1,0:T(8,128)(2,1)S(1)} %get-tuple-element.46.got_w_ref) | copy-start | bytes 6291460
  51.7 9.4 %collective-permute-start.3 = (bf16[128,1024]{1,0:T(8,128)(2,1)S(1)}, bf16[128,1024]{1,0:T(8,128)(2,1)S(1)}, u32[]{:S(2)}, u32[]{:S(2)}) collective-permute-start(bf16[128,1024]{1,0:T(8,128)(2,1)S(1)} %get-tuple-element.49), channel_id=1, source_target_pairs={{0,2},{1,3},{2,4},{3,5},{4,6},{5,7},{6,0},{7,1},{8,10},{9,11},{10,... | collective-permute-start | bytes 786440 | tf_op jit(solution)/shard_map/ppermute | solution.py:605
  53.1 8.0 %collective-permute-start.4 = (bf16[128,1024]{1,0:T(8,128)(2,1)S(1)}, bf16[128,1024]{1,0:T(8,128)(2,1)S(1)}, u32[]{:S(2)}, u32[]{:S(2)}) collective-permute-start(bf16[128,1024]{1,0:T(8,128)(2,1)S(1)} %get-tuple-element.50), channel_id=1, source_target_pairs={{0,6},{1,7},{2,0},{3,1},{4,2},{5,3},{6,4},{7,5},{8,14},{9,15},{10,... | collective-permute-start | bytes 786440 | tf_op jit(solution)/shard_map/ppermute | solution.py:605
  56.6 15.0 %collective-permute-start.2 = (bf16[128,1024]{1,0:T(8,128)(2,1)}, bf16[128,1024]{1,0:T(8,128)(2,1)S(1)}, u32[]{:S(2)}, u32[]{:S(2)}) collective-permute-start(bf16[128,1024]{1,0:T(8,128)(2,1)} %get-tuple-element.47), channel_id=1, source_target_pairs={{0,6},{1,7},{2,0},{3,1},{4,2},{5,3},{6,4},{7,5},{8,14},{9,15},{10,... | collective-permute-start | bytes 786440 | tf_op jit(solution)/shard_map/ppermute | solution.py:605
  58.0 7.6 %copy-start.7 = (s32[128,8]{0,1:T(8,128)S(1)}, s32[128,8]{0,1:T(8,128)}, u32[]{:S(2)}) copy-start(s32[128,8]{0,1:T(8,128)} %param.27) | copy-start | bytes 12292
  58.0 13.6 %collective-permute-start.6 = (bf16[128,1024]{1,0:T(8,128)(2,1)}, bf16[128,1024]{1,0:T(8,128)(2,1)}, u32[]{:S(2)}, u32[]{:S(2)}) collective-permute-start(bf16[128,1024]{1,0:T(8,128)(2,1)} %get-tuple-element.54), channel_id=1, source_target_pairs={{0,2},{1,3},{2,4},{3,5},{4,6},{5,7},{6,0},{7,1},{8,10},{9,11},{10,... | collective-permute-start | bytes 786440 | tf_op jit(solution)/shard_map/ppermute | solution.py:605
  63.1 8.8 %collective-permute-start.7 = (bf16[128,1024]{1,0:T(8,128)(2,1)}, bf16[128,1024]{1,0:T(8,128)(2,1)}, u32[]{:S(2)}, u32[]{:S(2)}) collective-permute-start(bf16[128,1024]{1,0:T(8,128)(2,1)} %get-tuple-element.55), channel_id=1, source_target_pairs={{0,6},{1,7},{2,0},{3,1},{4,2},{5,3},{6,4},{7,5},{8,14},{9,15},{10,... | collective-permute-start | bytes 786440 | tf_op jit(solution)/shard_map/ppermute | solution.py:605
  65.6 7.5 %collective-permute-start.5 = (bf16[128,1024]{1,0:T(8,128)(2,1)}, bf16[128,1024]{1,0:T(8,128)(2,1)}, u32[]{:S(2)}, u32[]{:S(2)}) collective-permute-start(bf16[128,1024]{1,0:T(8,128)(2,1)} %get-tuple-element.51), channel_id=1, source_target_pairs={{0,2},{1,3},{2,4},{3,5},{4,6},{5,7},{6,0},{7,1},{8,10},{9,11},{10,... | collective-permute-start | bytes 786440 | tf_op jit(solution)/shard_map/ppermute | solution.py:605
  68.7 1.6 copy-start.2
  70.3 2.8 %copy-start.3 = (bf16[3072,256]{1,0:T(8,128)(2,1)S(1)}, bf16[3072,256]{1,0:T(8,128)(2,1)}, u32[]{:S(2)}) copy-start(bf16[3072,256]{1,0:T(8,128)(2,1)} %get-tuple-element.59.picker_ref) | copy-start | bytes 4718596
  73.1 87.3 %slice-start = ((s8[6291456]{0:T(1024)(128)(4,1)}), s8[4194304]{0:T(1024)(128)(4,1)S(1)}, s32[]{:S(2)}) async-start(s8[6291456]{0:T(1024)(128)(4,1)} %bitcast.21), calls=%async_computation.4 | async-start | bytes 8388608
  77.0 83.4 %slice-start.1 = ((s8[6291456]{0:T(1024)(128)(4,1)}), s8[2097152]{0:T(1024)(128)(4,1)S(1)}, s32[]{:S(2)}) async-start(s8[6291456]{0:T(1024)(128)(4,1)} %bitcast.21), calls=%async_computation.5 | async-start | bytes 4194304
  77.0 83.4 %copy-start.6 = (bf16[1,768,2048]{2,1,0:T(8,128)(2,1)S(1)}, bf16[1,768,2048]{2,1,0:T(8,128)(2,1)}, u32[]{:S(2)}) copy-start(bf16[1,768,2048]{2,1,0:T(8,128)(2,1)} %down_ref.1) | copy-start | bytes 9437188
  178.8 82.4 %copy-start.4 = (bf16[128,2048]{1,0:T(8,128)(2,1)S(1)}, bf16[128,2048]{1,0:T(8,128)(2,1)}, u32[]{:S(2)}) copy-start(bf16[128,2048]{1,0:T(8,128)(2,1)} %get-tuple-element.31.mixer_ref) | copy-start | bytes 1572868
  178.8 82.4 %all-to-all-start.3 = ((bf16[128,24,1024]{2,1,0:T(8,128)(2,1)}), bf16[128,24,1024]{2,1,0:T(8,128)(2,1)}, u32[]{:S(2)}, u32[]{:S(2)}) async-start(bf16[128,24,1024]{2,1,0:T(8,128)(2,1)} %bitcast.23), calls=%async_computation.3 | async-start | bytes 12582912 | tf_op jit(solution)/shard_map/all_to_all | solution.py:710

commit v4 on v3

--- a/solution.py
+++ b/solution.py
@@ -140,11 +140,19 @@
         carry = decay * carry + got[:rows]
 
 
-def gate_kernel(mixed_ref, gate_w_ref, gate_ref):
+def within_kernel(
+    mixed_ref,
+    gate_w_ref,
+    x_ref,
+    maps_ref,
+    decay_ref,
+    step_ref,
+    enter_ref,
+    skip_ref,
+    *rest,
+):
+    gate_ref, within_ref = rest[-2:]
     gate_ref[...] = dot(mixed_ref[...], gate_w_ref[...]).astype(bf16)
-
-
-def within_kernel(x_ref, maps_ref, decay_ref, step_ref, enter_ref, skip_ref, within_ref):
     sums = running_sum(decay_ref[...])
     heads = sums.shape[0]
     maps = maps_ref[...]
@@ -314,8 +322,9 @@
         out_ref[part] = dot(picker_ref[part], rows_in).astype(bf16)
 
 
-def expert_kernel(a_ref, b_ref, c_ref, up_ref, down_ref, out_ref):
-    peers = a_ref.shape[0]
+def expert_kernel(got_ref, up_ref, down_ref, out_ref):
+    peers = out_ref.shape[0]
+    group = pl.ds(pl.program_id(0) * peers, peers)
     rows = peers * 8
     part = rows // 2
     place = iota((rows, rows), 0)
@@ -327,9 +336,9 @@
 
     apart = (source(place) == lane).astype(f32).astype(bf16)
     together = (place == source(lane)).astype(f32).astype(bf16)
-    tail = dot(apart, c_ref[...].reshape(rows, HALF)).astype(bf16)
-    x0 = jnp.concatenate([a_ref[...].reshape(rows, HALF), tail[:part]], axis=0)
-    x1 = jnp.concatenate([b_ref[...].reshape(rows, HALF), tail[part:]], axis=0)
+    tail = dot(apart, got_ref[group, 2].reshape(rows, HALF)).astype(bf16)
+    x0 = jnp.concatenate([got_ref[group, 0].reshape(rows, HALF), tail[:part]], axis=0)
+    x1 = jnp.concatenate([got_ref[group, 1].reshape(rows, HALF), tail[part:]], axis=0)
     projected = dot(x0, up_ref[0, :HALF]) + dot(x1, up_ref[0, HALF:])
     gate = projected[:, :F]
     hidden = (gate * jax.nn.sigmoid(gate) * projected[:, F:]).astype(bf16)
@@ -484,17 +493,43 @@
 
     slices = lax.all_to_all(sent, "seq", split_axis=0, concat_axis=0, tiled=True)
 
-    gate = pl.pallas_call(
-        gate_kernel,
-        grid=(blocks,),
-        in_specs=[by_rows(Q, D), fixed_once(D, channels)],
-        out_specs=by_rows(Q, channels),
-        out_shape=stored(bf16, rows, channels),
-        compiler_params=params(12),
-        cost_estimate=cost(2 * rows * channels * D, 7 * 2**20),
-        name="gate",
-    )(*from_hbm(mixed, gate_proj))
-    slices, gate = lax.optimization_barrier((slices, gate))
+    gate_w = from_vmem(gate_proj)
+    inside = from_hbm(mixed, x, maps, decay, step, enter)
+    skip = jnp.repeat(skip_gain, P_SIZE).reshape(1, channels)
+    half_blocks = blocks // 2
+
+    def within_half(first, earlier):
+        def block(*shape):
+            return pl.BlockSpec(shape, lambda i: (i + first, *(0,) * (len(shape) - 1)))
+
+        def lanes():
+            return pl.BlockSpec((heads, Q), lambda i: (0, i + first))
+
+        mixed, x, maps, decay, step, enter = inside
+        return pl.pallas_call(
+            within_kernel,
+            grid=(half_blocks,),
+            in_specs=[
+                block(Q, D),
+                resident(),
+                block(Q, channels),
+                block(Q, 2 * N),
+                lanes(),
+                lanes(),
+                block(1, N, channels),
+                fixed(1, channels),
+            ]
+            + [pl.BlockSpec(memory_space=pl.ANY)] * len(earlier),
+            out_specs=[block(Q, channels), block(Q, channels)],
+            out_shape=[stored(bf16, rows, channels), stored(f32, rows, channels)],
+            input_output_aliases={8 + i: i for i in range(len(earlier))},
+            compiler_params=params(20),
+            cost_estimate=cost(rows * channels * (D + 2 * Q), 5 * 2**20, rows * Q * heads // 2),
+            name="within",
+        )(mixed, *gate_w, x, maps, decay, step, enter, skip, *earlier)
+
+    gate, within = within_half(0, ())
+    slices, gate, within = lax.optimization_barrier((slices, gate, within))
 
     before = pl.pallas_call(
         prefix_kernel,
@@ -505,28 +540,8 @@
     incoming = lax.all_to_all(before, "seq", split_axis=0, concat_axis=0, tiled=True)
     incoming = incoming.reshape(N, channels)
 
-    within = pl.pallas_call(
-        within_kernel,
-        grid=(blocks,),
-        in_specs=[
-            by_rows(Q, channels),
-            by_rows(Q, 2 * N),
-            by_lanes(heads, Q),
-            by_lanes(heads, Q),
-            by_rows(1, N, channels),
-            fixed(1, channels),
-        ],
-        out_specs=by_rows(Q, channels),
-        out_shape=stored(f32, rows, channels),
-        compiler_params=params(16),
-        cost_estimate=cost(4 * rows * channels * Q, 6 * 2**20, rows * Q * heads),
-        name="within",
-    )(
-        *from_hbm(x, maps, decay, step, enter),
-        jnp.repeat(skip_gain, P_SIZE).reshape(1, channels),
-    )
-
-    incoming, within = lax.optimization_barrier((incoming, within))
+    gate, within = within_half(half_blocks, from_hbm(gate, within))
+    incoming, gate, within = lax.optimization_barrier((incoming, gate, within))
 
     own, other = pl.pallas_call(
         normed_kernel,
@@ -588,14 +603,14 @@
     got, part = lax.optimization_barrier((got, part))
     projections = own_w + from_vmem(got_w)
 
-    def halves(at, hop_a, hop_b, *arrived):
+    def halves(at, hop_a, hop_b, *arrived, kept=half_pair):
         return project(
             halves_kernel,
             [rows_of(hop_a), rows_of(hop_a), rows_of(hop_b), rows_of(hop_b)]
             + [resident(), resident()]
             + [half] * len(arrived),
             [half, half],
-            half_pair,
+            kept,
             4,
             "halves",
         )(at, own, got, own, got, *projections, *arrived)
@@ -614,15 +629,19 @@
     )(at, part, got, projections[1])
     via_next, via_last = send(far_left, 1), send(far_right, 3)
     next_right, last_left = halves(at, 1, 3)
-    right_pieces = [send(next_right, 1)]
-    left_pieces = [send(last_left, 3)]
+    later_at, _ = lax.optimization_barrier((at, next_right))
+    mine_right, mine_left = from_hbm(
+        *halves(later_at, 0, 0, kept=[stored(bf16, own_rows, HALF)] * 2)
+    )
+    next_right, last_left, mine_left, mine_right = lax.optimization_barrier(
+        (next_right, last_left, mine_left, mine_right)
+    )
+    right_pieces = [send(next_right, 1), mine_right]
+    left_pieces = [send(last_left, 3), mine_left]
     next_left, last_right = halves(at, 1, 3, via_next, via_last)
     left_pieces.append(send(next_left, 1))
     right_pieces.append(send(last_right, 3))
-    late_at, late_ids, _ = lax.optimization_barrier((at, expert_ids, next_left))
-    mine_right, mine_left = halves(late_at, 0, 0)
-    left_pieces.append(mine_left)
-    right_pieces.append(mine_right)
+    late_ids, _ = lax.optimization_barrier((expert_ids, next_left))
     named, rank, picker = pl.pallas_call(
         route_kernel,
         grid=(4,),
@@ -635,7 +654,7 @@
         out_shape=[
             shape_of(f32, own_rows, experts),
             shape_of(f32, own_rows, experts),
-            stored(bf16, slab_rows, 2 * own_rows),
+            pltpu.VMEM((slab_rows, 2 * own_rows), bf16),
         ],
         scratch_shapes=[pltpu.VMEM((own_rows, experts), bf16)],
         compiler_params=params(12),
@@ -694,19 +713,16 @@
         name="combine_weight",
     )(rank, weight)
 
-    def piece(index):
-        return pl.BlockSpec((group, None, 8, HALF), lambda i: (i, index, 0, 0))
-
     results = pl.pallas_call(
         expert_kernel,
         grid=(4,),
-        in_specs=[piece(0), piece(1), piece(2), resident(), resident()],
+        in_specs=[resident()] * 3,
         out_specs=by_rows(group, 3, 8, HALF),
         out_shape=stored(bf16, peers, 3, 8, HALF),
         compiler_params=params(28),
         cost_estimate=cost(6 * peers * CAP * D * F, 22 * 2**20, peers * CAP * F),
         name="experts",
-    )(arrived, arrived, arrived, *from_vmem(expert_gate_up, expert_down))
+    )(*from_vmem(arrived, expert_gate_up, expert_down))
     returned = lax.all_to_all(
         results.reshape(peers, SLAB, HALF),
         ("seq", "exp"),

time: 267 us -> 265 us (level)
  waiting for transfers between devices: 81.1 us -> 85.4 us
where the time goes in v4:
time: 265 us; the launch traced here: 264 us
  waiting for transfers between devices  85.4 us (32%)
  blocking collectives  81.2 us (31%)
  Pallas kernels  67.1 us (25%)
  starting transfers between devices  29.2 us (11%)
    all_to_all x1, blocking collectives, body(): lax.all_to_all(outgoing.reshape(peers, SLAB, HALF), ('seq', 'exp'), split...  81.2 us
    all_to_all x1, waiting for transfers between devices, body(): lax.all_to_all(results.reshape(peers, SLAB, HALF), ('seq', 'exp'), split_...  74.4 us
    pallas_call x1, Pallas kernels, body(): pl.pallas_call(expert_kernel, grid=(4,), in_specs=[resident()] * 3, out_s...  18.2 us
    pallas_call x1, Pallas kernels, body(): pl.pallas_call(local_state_kernel, grid=(blocks,), in_specs=[by_rows(Q, D...  10.8 us
    pallas_call x2, Pallas kernels, within_half(): pl.pallas_call(within_kernel, grid=(half_blocks,), in_specs=[block(Q, D),...  10.4 us
    all_to_all x1, starting transfers between devices, body(): lax.all_to_all(sent, 'seq', split_axis=0, concat_axis=0, tiled=True)  7.7 us
    ppermute x6, waiting for transfers between devices, send(): return lax.ppermute(piece, 'exp', moves)  7.17 us
    ppermute x6, starting transfers between devices, send(): return lax.ppermute(piece, 'exp', moves)  7.02 us
  transfers between devices with their start and end apart: 11, of which 6 were waited for; matrix products, arithmetic and copies ran while one was open for 0% of the time, Pallas kernels for 15%

profile of v4, /device:TPU:1, one launch (start us, length us, event | category | flops | bytes accessed | tf_op | source)
XLA Modules:
  0.0 264.2 jit_solution(12879720111884754608)
XLA Ops:
  0.6 1.5 collective-permute-start.1
  2.1 10.8 %local_state.1 = (bf16[1024,2048]{1,0:T(8,128)(2,1)}, bf16[1024,512]{1,0:T(8,128)(2,1)}, bf16[1024,256]{1,0:T(8,128)(2,1)}, bf16[4,128,512]{2,1,0:T(8,128)(2,1)}, bf16[16,16,512]{2,1,0:T(8,128)(2,1)}) custom-call(bf16[1024,2048]{1,0:T(8,128)(2,1)} %hidden_ref.3, f32[1,2048]{1,0:T(1,128)} %bitcast.30, bf16[2048,512]{1,0:T(8,128)(2,1)} %value_ref.1, ...), custom_call_target="tpu_custom_call" | custom-call | flops 3221225472 | bytes 16777216 | tf_op jit(solution)/shard_map/local_state/pallas_call | solution.py:463
  12.9 7.7 %all-to-all-start = ((bf16[16,16,512]{2,1,0:T(8,128)(2,1)}), bf16[16,16,512]{2,1,0:T(8,128)(2,1)S(1)}, u32[]{:S(2)}, u32[]{:S(2)}) async-start(bf16[16,16,512]{2,1,0:T(8,128)(2,1)} %get-tuple-element.43), calls=%async_computation | async-start | bytes 524288 | tf_op jit(solution)/shard_map/all_to_all | solution.py:494
  20.8 5.2 %within.2 = (bf16[1024,512]{1,0:T(8,128)(2,1)}, f32[1024,512]{1,0:T(8,128)}) custom-call(bf16[1024,2048]{1,0:T(8,128)(2,1)} %get-tuple-element.44.mixed_ref, bf16[2048,512]{1,0:T(8,128)(2,1)S(1)} %copy-done.1, bf16[1024,512]{1,0:T(8,128)(2,1)} %get-tuple-element.45.x_ref, bf16[1024,256]{1,0:T(8,128)(2,1)} %get-tuple-element.46.maps_ref, f32[8,1024]{1,0:T(8,128)} %bitcast.23, ...), custom_call_target="tpu_custom_call" | custom-call | flops 1342177280 | bytes 5242880 | tf_op jit(solution)/shard_map/within/pallas_call | solution.py:509
  26.0 2.4 all-to-all-done.got_ref
  28.4 0.8 prefix.1
  29.2 4.2 %all-to-all-start.1 = ((bf16[16,8,512]{2,1,0:T(8,128)(2,1)}), bf16[16,8,512]{2,1,0:T(8,128)(2,1)S(1)}, u32[]{:S(2)}, u32[]{:S(2)}) async-start(bf16[16,8,512]{2,1,0:T(8,128)(2,1)} %prefix.1), calls=%async_computation.1 | async-start | bytes 262144 | tf_op jit(solution)/shard_map/all_to_all | solution.py:540
  33.4 5.2 %within.3 = (bf16[1024,512]{1,0:T(8,128)(2,1)}, f32[1024,512]{1,0:T(8,128)}) custom-call(bf16[1024,2048]{1,0:T(8,128)(2,1)} %get-tuple-element.44.mixed_ref, bf16[2048,512]{1,0:T(8,128)(2,1)S(1)} %copy-done.1, bf16[1024,512]{1,0:T(8,128)(2,1)} %get-tuple-element.45.x_ref, ...), custom_call_target="tpu_custom_call", output_to_operand_aliasing={{0}: (8, {}), {1}: (9, {})} | custom-call | flops 1342177280 | bytes 5242880 | tf_op jit(solution)/shard_map/within/pallas_call | solution.py:509
  38.7 1.5 all-to-all-done.1
  40.1 5.1 %normed.1 = (bf16[512,512]{1,0:T(8,128)(2,1)S(1)}, bf16[512,512]{1,0:T(8,128)(2,1)}) custom-call(s32[1]{0:T(128)} %bitcast.5.core_ref, f32[1024,512]{1,0:T(8,128)} %get-tuple-element.55.within_ref, bf16[1024,256]{1,0:T(8,128)(2,1)} %get-tuple-element.46.maps_ref, bf16[1024,512]{1,0:T(8,128)(2,1)} %get-tuple-element.56.gate_ref, f32[8,1024]{1,0:T(8,128)} %bitcast.25, ...), custom_call_target="tpu_custom_call" | custom-call | flops 134217728 | bytes 5242880 | tf_op jit(solution)/shard_map/normed/pallas_call | solution.py:546
  45.2 2.2 collective-permute-start
  47.5 2.7 %own_part.1 = (f32[128,2048]{1,0:T(8,128)S(1)}, bf16[512,2048]{1,0:T(8,128)(2,1)S(1)}) custom-call(s32[4]{0:T(128)S(1)} %pad_add_fusion.at_ref, bf16[512,512]{1,0:T(8,128)(2,1)S(1)} %get-tuple-element.58.own_ref.own_a_ref.own_b_ref, bf16[512,2048]{1,0:T(8,128)(2,1)S(1)} %copy-done, bf16[512,2048]{1,0:T(8,128)(2,1)} %collective-permute-done.1.got_w_ref), custom_call_target="tpu_custom_call" | custom-call | flops 268435456 | bytes 3145728 | tf_op jit(solution)/shard_map/own_part/pallas_call | solution.py:595
  50.2 1.0 finish.1
  51.3 1.4 collective-permute-start.3
  52.6 1.5 collective-permute-start.4
  54.1 2.0 halves.3
  56.1 2.0 halves.4
  58.1 1.4 collective-permute-start.2
  59.6 1.0 collective-permute-done.3.rest_0_
  60.6 2.0 halves.5
  62.6 0.9 collective-permute-start.5
  63.5 1.8 collective-permute-start.7
  65.4 2.0 route.1
  67.4 0.6 collective-permute-done.6.right_a_ref
  68.0 5.5 %collective-permute-done.5.left_c_ref = bf16[128,1024]{1,0:T(8,128)(2,1)S(1)} collective-permute-done((bf16[128,1024]{1,0:T(8,128)(2,1)}, bf16[128,1024]{1,0:T(8,128)(2,1)S(1)}, u32[]{:S(2)}, u32[]{:S(2)}) %collective-permute-start.5) | collective-permute-done | bytes 262176 | tf_op jit(solution)/shard_map/ppermute | solution.py:620
  73.5 3.9 %dispatch.1 = (bf16[128,2048]{1,0:T(8,128)(2,1)}, f32[128,128]{1,0:T(8,128)S(1)}, bf16[3072,1024]{1,0:T(8,128)(2,1)S(1)}) custom-call(s32[1]{0:T(128)} %bitcast.where_ref, bf16[128,1024]{1,0:T(8,128)(2,1)S(1)} %collective-permute-done.2.left_a_ref, bf16[128,1024]{1,0:T(8,128)(2,1)} %get-tuple-element.69.left_b_ref, ...), custom_call_target="tpu_custom_call" | custom-call | flops 1610612736 | bytes 10485760 | tf_op jit(solution)/shard_map/dispatch/pallas_call | solution.py:665
  77.4 81.2 %all_to_all.20 = bf16[128,24,1024]{2,1,0:T(8,128)(2,1)S(1)} all-to-all(bf16[128,24,1024]{2,1,0:T(8,128)(2,1)S(1)} %bitcast.15), channel_id=1, replica_groups=mesh['seq'=16,'exp'=8] {'seq','exp'}, dimensions={0} | all-to-all | bytes 12582912 | tf_op jit(solution)/shard_map/all_to_all | solution.py:697
  158.6 18.2 %experts.1 = bf16[128,3,8,1024]{3,2,1,0:T(8,128)(2,1)} custom-call(bf16[128,3,8,1024]{3,2,1,0:T(8,128)(2,1)S(1)} %bitcast.16, bf16[1,2048,1536]{2,1,0:T(8,128)(2,1)S(1)} %bitcast.20, bf16[1,768,2048]{2,1,0:T(8,128)(2,1)S(1)} %copy-done.4), custom_call_target="tpu_custom_call" | custom-call | flops 14495514624 | bytes 23068672 | tf_op jit(solution)/shard_map/experts/pallas_call | solution.py:716
  176.8 6.6 %all-to-all-start.3 = ((bf16[128,24,1024]{2,1,0:T(8,128)(2,1)}), bf16[128,24,1024]{2,1,0:T(8,128)(2,1)}, u32[]{:S(2)}, u32[]{:S(2)}) async-start(bf16[128,24,1024]{2,1,0:T(8,128)(2,1)} %bitcast.21), calls=%async_computation.3 | async-start | bytes 12582912 | tf_op jit(solution)/shard_map/all_to_all | solution.py:726
  183.4 1.4 combine_weight.1.weight_ref
  184.8 74.4 %all-to-all-done.3.got_ref = bf16[128,24,1024]{2,1,0:T(8,128)(2,1)} async-done(((bf16[128,24,1024]{2,1,0:T(8,128)(2,1)}), bf16[128,24,1024]{2,1,0:T(8,128)(2,1)}, u32[]{:S(2)}, u32[]{:S(2)}) %all-to-all-start.3) | async-done | bytes 6291488 | tf_op jit(solution)/shard_map/all_to_all | solution.py:726
  259.2 4.9 %combine.1 = bf16[128,2048]{1,0:T(8,128)(2,1)} custom-call(bf16[128,24,1024]{2,1,0:T(8,128)(2,1)} %all-to-all-done.3.got_ref, bf16[256,3072]{1,0:T(8,128)(2,1)S(1)} %combine_weight.1.weight_ref, bf16[128,2048]{1,0:T(8,128)(2,1)S(1)} %copy-done.2), custom_call_target="tpu_custom_call" | custom-call | flops 1610612736 | bytes 8388608 | tf_op jit(solution)/shard_map/combine/pallas_call | solution.py:734
  (29 shorter events, 0.5 us)
Async XLA Ops:
  0.6 46.9 %collective-permute-start.1 = (bf16[512,2048]{1,0:T(8,128)(2,1)}, bf16[512,2048]{1,0:T(8,128)(2,1)}, u32[]{:S(2)}, u32[]{:S(2)}) collective-permute-start(bf16[512,2048]{1,0:T(8,128)(2,1)} %own_w_ref.7), channel_id=1, source_target_pairs={{0,1},{1,0},{2,3},{3,2},{4,5},{5,4},{6,7},{7,6},{8,9},{9,8},{10,11... | collective-permute-start | bytes 6291464 | tf_op jit(solution)/shard_map/ppermute | solution.py:459
  2.1 18.5 %copy-start.6 = (f32[8]{0:T(128)S(1)}, f32[8]{0:T(128)}, u32[]{:S(2)}) copy-start(f32[8]{0:T(128)} %param.22) | copy-start | bytes 100
  2.1 18.7 %copy-start.1 = (bf16[2048,512]{1,0:T(8,128)(2,1)S(1)}, bf16[2048,512]{1,0:T(8,128)(2,1)}, u32[]{:S(2)}) copy-start(bf16[2048,512]{1,0:T(8,128)(2,1)} %gate_w_ref.3) | copy-start | bytes 6291460
  12.9 15.5 %all-to-all-start = ((bf16[16,16,512]{2,1,0:T(8,128)(2,1)}), bf16[16,16,512]{2,1,0:T(8,128)(2,1)S(1)}, u32[]{:S(2)}, u32[]{:S(2)}) async-start(bf16[16,16,512]{2,1,0:T(8,128)(2,1)} %get-tuple-element.43), calls=%async_computation | async-start | bytes 524288 | tf_op jit(solution)/shard_map/all_to_all | solution.py:494
  29.2 10.9 %all-to-all-start.1 = ((bf16[16,8,512]{2,1,0:T(8,128)(2,1)}), bf16[16,8,512]{2,1,0:T(8,128)(2,1)S(1)}, u32[]{:S(2)}, u32[]{:S(2)}) async-start(bf16[16,8,512]{2,1,0:T(8,128)(2,1)} %prefix.1), calls=%async_computation.1 | async-start | bytes 262144 | tf_op jit(solution)/shard_map/all_to_all | solution.py:540
  33.4 6.7 %copy-start.3 = (f32[512]{0:T(512)S(1)}, f32[512]{0:T(512)}, u32[]{:S(2)}) copy-start(f32[512]{0:T(512)} %param.23) | copy-start | bytes 6148
  38.7 8.8 %copy-start = (bf16[512,2048]{1,0:T(8,128)(2,1)S(1)}, bf16[512,2048]{1,0:T(8,128)(2,1)}, u32[]{:S(2)}) copy-start(bf16[512,2048]{1,0:T(8,128)(2,1)} %own_w_ref.7) | copy-start | bytes 6291460
  45.2 5.0 %collective-permute-start = (bf16[512,512]{1,0:T(8,128)(2,1)}, bf16[512,512]{1,0:T(8,128)(2,1)S(1)}, u32[]{:S(2)}, u32[]{:S(2)}) collective-permute-start(bf16[512,512]{1,0:T(8,128)(2,1)} %get-tuple-element.59), channel_id=1, source_target_pairs={{0,1},{1,0},{2,3},{3,2},{4,5},{5,4},{6,7},{7,6},{8,9},{9,8},{10,11... | collective-permute-start | bytes 1572872 | tf_op jit(solution)/shard_map/ppermute | solution.py:572
  51.3 9.3 %collective-permute-start.3 = (bf16[128,1024]{1,0:T(8,128)(2,1)S(1)}, bf16[128,1024]{1,0:T(8,128)(2,1)S(1)}, u32[]{:S(2)}, u32[]{:S(2)}) collective-permute-start(bf16[128,1024]{1,0:T(8,128)(2,1)S(1)} %get-tuple-element.71), channel_id=1, source_target_pairs={{0,2},{1,3},{2,4},{3,5},{4,6},{5,7},{6,0},{7,1},{8,10},{9,11},{10,... | collective-permute-start | bytes 786440 | tf_op jit(solution)/shard_map/ppermute | solution.py:620
  52.6 8.0 %collective-permute-start.4 = (bf16[128,1024]{1,0:T(8,128)(2,1)S(1)}, bf16[128,1024]{1,0:T(8,128)(2,1)S(1)}, u32[]{:S(2)}, u32[]{:S(2)}) collective-permute-start(bf16[128,1024]{1,0:T(8,128)(2,1)S(1)} %get-tuple-element.72), channel_id=1, source_target_pairs={{0,6},{1,7},{2,0},{3,1},{4,2},{5,3},{6,4},{7,5},{8,14},{9,15},{10,... | collective-permute-start | bytes 786440 | tf_op jit(solution)/shard_map/ppermute | solution.py:620
  58.1 7.2 %copy-start.5 = (s32[128,8]{0,1:T(8,128)S(1)}, s32[128,8]{0,1:T(8,128)}, u32[]{:S(2)}) copy-start(s32[128,8]{0,1:T(8,128)} %param.27) | copy-start | bytes 12292
  58.1 9.3 %collective-permute-start.2 = (bf16[128,1024]{1,0:T(8,128)(2,1)}, bf16[128,1024]{1,0:T(8,128)(2,1)S(1)}, u32[]{:S(2)}, u32[]{:S(2)}) collective-permute-start(bf16[128,1024]{1,0:T(8,128)(2,1)} %get-tuple-element.68), channel_id=1, source_target_pairs={{0,6},{1,7},{2,0},{3,1},{4,2},{5,3},{6,4},{7,5},{8,14},{9,15},{10,... | collective-permute-start | bytes 786440 | tf_op jit(solution)/shard_map/ppermute | solution.py:620
  59.5 8.5 %collective-permute-start.6 = (bf16[128,1024]{1,0:T(8,128)(2,1)}, bf16[128,1024]{1,0:T(8,128)(2,1)}, u32[]{:S(2)}, u32[]{:S(2)}) collective-permute-start(bf16[128,1024]{1,0:T(8,128)(2,1)} %get-tuple-element.74), channel_id=1, source_target_pairs={{0,2},{1,3},{2,4},{3,5},{4,6},{5,7},{6,0},{7,1},{8,10},{9,11},{10,... | collective-permute-start | bytes 786440 | tf_op jit(solution)/shard_map/ppermute | solution.py:620
  62.6 10.9 %collective-permute-start.5 = (bf16[128,1024]{1,0:T(8,128)(2,1)}, bf16[128,1024]{1,0:T(8,128)(2,1)S(1)}, u32[]{:S(2)}, u32[]{:S(2)}) collective-permute-start(bf16[128,1024]{1,0:T(8,128)(2,1)} %get-tuple-element.73), channel_id=1, source_target_pairs={{0,2},{1,3},{2,4},{3,5},{4,6},{5,7},{6,0},{7,1},{8,10},{9,11},{10,... | collective-permute-start | bytes 786440 | tf_op jit(solution)/shard_map/ppermute | solution.py:620
  63.5 10.0 %collective-permute-start.7 = (bf16[128,1024]{1,0:T(8,128)(2,1)}, bf16[128,1024]{1,0:T(8,128)(2,1)S(1)}, u32[]{:S(2)}, u32[]{:S(2)}) collective-permute-start(bf16[128,1024]{1,0:T(8,128)(2,1)} %get-tuple-element.76), channel_id=1, source_target_pairs={{0,6},{1,7},{2,0},{3,1},{4,2},{5,3},{6,4},{7,5},{8,14},{9,15},{10,... | collective-permute-start | bytes 786440 | tf_op jit(solution)/shard_map/ppermute | solution.py:620
  73.5 85.2 %slice-start = ((s8[6291456]{0:T(1024)(128)(4,1)}), s8[4194304]{0:T(1024)(128)(4,1)S(1)}, s32[]{:S(2)}) async-start(s8[6291456]{0:T(1024)(128)(4,1)} %bitcast.19), calls=%async_computation.4 | async-start | bytes 8388608
  77.4 81.2 %slice-start.1 = ((s8[6291456]{0:T(1024)(128)(4,1)}), s8[2097152]{0:T(1024)(128)(4,1)S(1)}, s32[]{:S(2)}) async-start(s8[6291456]{0:T(1024)(128)(4,1)} %bitcast.19), calls=%async_computation.5 | async-start | bytes 4194304
  77.4 81.2 %copy-start.4 = (bf16[1,768,2048]{2,1,0:T(8,128)(2,1)S(1)}, bf16[1,768,2048]{2,1,0:T(8,128)(2,1)}, u32[]{:S(2)}) copy-start(bf16[1,768,2048]{2,1,0:T(8,128)(2,1)} %down_ref.1) | copy-start | bytes 9437188
  176.8 82.4 %copy-start.2 = (bf16[128,2048]{1,0:T(8,128)(2,1)S(1)}, bf16[128,2048]{1,0:T(8,128)(2,1)}, u32[]{:S(2)}) copy-start(bf16[128,2048]{1,0:T(8,128)(2,1)} %get-tuple-element.41.mixer_ref) | copy-start | bytes 1572868
  176.8 82.4 %all-to-all-start.3 = ((bf16[128,24,1024]{2,1,0:T(8,128)(2,1)}), bf16[128,24,1024]{2,1,0:T(8,128)(2,1)}, u32[]{:S(2)}, u32[]{:S(2)}) async-start(bf16[128,24,1024]{2,1,0:T(8,128)(2,1)} %bitcast.21), calls=%async_computation.3 | async-start | bytes 12582912 | tf_op jit(solution)/shard_map/all_to_all | solution.py:726

commit v5 on v4

--- a/solution.py
+++ b/solution.py
@@ -222,9 +222,11 @@
     other_ref[...] = jnp.where(mine, second, first).astype(bf16)
 
 
-def own_part_kernel(at_ref, own_ref, own_w_ref, got_w_ref, part_ref, kept_ref):
+def own_part_kernel(at_ref, own_ref, own_w_ref, got_w_ref, part_ref, kept_ref, ready):
+    keep = pltpu.make_async_copy(got_w_ref, kept_ref, ready)
+    keep.start()
     part_ref[...] = dot(own_ref[...], own_w_ref[...])
-    kept_ref[...] = got_w_ref[...]
+    keep.wait()
 
 
 def finish_kernel(at_ref, part_ref, got_ref, got_w_ref, left_ref, right_ref):
@@ -576,11 +578,15 @@
     def rows_of(hop):
         return pl.BlockSpec((own_rows, channels), lambda i, at: (at[hop], 0))
 
-    def project(kernel, in_specs, out_specs, out_shape, share, name):
+    def project(kernel, in_specs, out_specs, out_shape, share, name, scratch=()):
         return pl.pallas_call(
             kernel,
             grid_spec=pltpu.PrefetchScalarGridSpec(
-                num_scalar_prefetch=1, grid=(1,), in_specs=in_specs, out_specs=out_specs
+                num_scalar_prefetch=1,
+                grid=(1,),
+                in_specs=in_specs,
+                out_specs=out_specs,
+                scratch_shapes=scratch,
             ),
             out_shape=out_shape,
             compiler_params=params(10),
@@ -594,11 +600,12 @@
     own_w = from_vmem(out_proj)
     part, got_w = project(
         own_part_kernel,
-        [rows_of(2), resident(), fixed(channels, D)],
+        [rows_of(2), resident(), pl.BlockSpec(memory_space=pl.ANY)],
         [fixed(own_rows, D), resident()],
         [pltpu.VMEM((own_rows, D), f32), pltpu.VMEM((channels, D), bf16)],
         2,
         "own_part",
+        [pltpu.SemaphoreType.DMA],
     )(at, own, *own_w, *from_hbm(other_proj))
     got, part = lax.optimization_barrier((got, part))
     projections = own_w + from_vmem(got_w)
@@ -667,12 +674,12 @@
         grid_spec=pltpu.PrefetchScalarGridSpec(
             num_scalar_prefetch=1,
             grid=(1,),
-            in_specs=[fixed(own_rows, HALF)] * 6
+            in_specs=[resident()] * 6
             + [
                 pl.BlockSpec((own_rows, D), lambda i, at: (at[0], 0)),
                 fixed(1, D),
                 fixed(D, experts),
-                fixed(own_rows, experts),
+                resident(),
                 resident(),
             ],
             out_specs=[fixed(own_rows, D), fixed(own_rows, experts), resident()],

time: 265 us -> 264 us (level)
  no operation moved by 1% of the time
where the time goes in v5:
time: 264 us
  waiting for transfers between devices  85.5 us (32%)
  blocking collectives  81.2 us (31%)
  Pallas kernels  66.5 us (25%)
  starting transfers between devices  29.2 us (11%)
    all_to_all x1, blocking collectives, body(): lax.all_to_all(outgoing.reshape(peers, SLAB, HALF), ('seq', 'exp'), split...  81.2 us
    all_to_all x1, waiting for transfers between devices, body(): lax.all_to_all(results.reshape(peers, SLAB, HALF), ('seq', 'exp'), split_...  74.4 us
    pallas_call x1, Pallas kernels, body(): pl.pallas_call(expert_kernel, grid=(4,), in_specs=[resident()] * 3, out_s...  18.2 us
    pallas_call x1, Pallas kernels, body(): pl.pallas_call(local_state_kernel, grid=(blocks,), in_specs=[by_rows(Q, D...  10.8 us
    pallas_call x2, Pallas kernels, within_half(): pl.pallas_call(within_kernel, grid=(half_blocks,), in_specs=[block(Q, D),...  10.4 us
    all_to_all x1, starting transfers between devices, body(): lax.all_to_all(sent, 'seq', split_axis=0, concat_axis=0, tiled=True)  7.7 us
    ppermute x6, waiting for transfers between devices, send(): return lax.ppermute(piece, 'exp', moves)  7.18 us
    ppermute x6, starting transfers between devices, send(): return lax.ppermute(piece, 'exp', moves)  7.02 us
  transfers between devices with their start and end apart: 11, of which 6 were waited for; matrix products, arithmetic and copies ran while one was open for 0% of the time, Pallas kernels for 15%

profile of v5, /device:TPU:1, one launch (start us, length us, event | category | flops | bytes accessed | tf_op | source)
XLA Modules:
  0.0 263.6 jit_solution(3174079868841057610)
XLA Ops:
  0.6 1.5 collective-permute-start.1
  2.1 10.8 %local_state.1 = (bf16[1024,2048]{1,0:T(8,128)(2,1)}, bf16[1024,512]{1,0:T(8,128)(2,1)}, bf16[1024,256]{1,0:T(8,128)(2,1)}, bf16[4,128,512]{2,1,0:T(8,128)(2,1)}, bf16[16,16,512]{2,1,0:T(8,128)(2,1)}) custom-call(bf16[1024,2048]{1,0:T(8,128)(2,1)} %hidden_ref.3, f32[1,2048]{1,0:T(1,128)} %bitcast.30, bf16[2048,512]{1,0:T(8,128)(2,1)} %value_ref.1, ...), custom_call_target="tpu_custom_call" | custom-call | flops 3221225472 | bytes 16777216 | tf_op jit(solution)/shard_map/local_state/pallas_call | solution.py:465
  12.9 7.7 %all-to-all-start = ((bf16[16,16,512]{2,1,0:T(8,128)(2,1)}), bf16[16,16,512]{2,1,0:T(8,128)(2,1)S(1)}, u32[]{:S(2)}, u32[]{:S(2)}) async-start(bf16[16,16,512]{2,1,0:T(8,128)(2,1)} %get-tuple-element.43), calls=%async_computation | async-start | bytes 524288 | tf_op jit(solution)/shard_map/all_to_all | solution.py:496
  20.8 5.2 %within.2 = (bf16[1024,512]{1,0:T(8,128)(2,1)}, f32[1024,512]{1,0:T(8,128)}) custom-call(bf16[1024,2048]{1,0:T(8,128)(2,1)} %get-tuple-element.44.mixed_ref, bf16[2048,512]{1,0:T(8,128)(2,1)S(1)} %copy-done.1, bf16[1024,512]{1,0:T(8,128)(2,1)} %get-tuple-element.45.x_ref, bf16[1024,256]{1,0:T(8,128)(2,1)} %get-tuple-element.46.maps_ref, f32[8,1024]{1,0:T(8,128)} %bitcast.23, ...), custom_call_target="tpu_custom_call" | custom-call | flops 1342177280 | bytes 5242880 | tf_op jit(solution)/shard_map/within/pallas_call | solution.py:511
  26.0 2.4 all-to-all-done.got_ref
  28.4 0.8 prefix.1
  29.2 4.2 %all-to-all-start.1 = ((bf16[16,8,512]{2,1,0:T(8,128)(2,1)}), bf16[16,8,512]{2,1,0:T(8,128)(2,1)S(1)}, u32[]{:S(2)}, u32[]{:S(2)}) async-start(bf16[16,8,512]{2,1,0:T(8,128)(2,1)} %prefix.1), calls=%async_computation.1 | async-start | bytes 262144 | tf_op jit(solution)/shard_map/all_to_all | solution.py:542
  33.4 5.2 %within.3 = (bf16[1024,512]{1,0:T(8,128)(2,1)}, f32[1024,512]{1,0:T(8,128)}) custom-call(bf16[1024,2048]{1,0:T(8,128)(2,1)} %get-tuple-element.44.mixed_ref, bf16[2048,512]{1,0:T(8,128)(2,1)S(1)} %copy-done.1, bf16[1024,512]{1,0:T(8,128)(2,1)} %get-tuple-element.45.x_ref, ...), custom_call_target="tpu_custom_call", output_to_operand_aliasing={{0}: (8, {}), {1}: (9, {})} | custom-call | flops 1342177280 | bytes 5242880 | tf_op jit(solution)/shard_map/within/pallas_call | solution.py:511
  38.7 1.5 all-to-all-done.1
  40.1 5.1 %normed.1 = (bf16[512,512]{1,0:T(8,128)(2,1)S(1)}, bf16[512,512]{1,0:T(8,128)(2,1)}) custom-call(s32[1]{0:T(128)} %bitcast.5.core_ref, f32[1024,512]{1,0:T(8,128)} %get-tuple-element.55.within_ref, bf16[1024,256]{1,0:T(8,128)(2,1)} %get-tuple-element.46.maps_ref, bf16[1024,512]{1,0:T(8,128)(2,1)} %get-tuple-element.56.gate_ref, f32[8,1024]{1,0:T(8,128)} %bitcast.25, ...), custom_call_target="tpu_custom_call" | custom-call | flops 134217728 | bytes 5242880 | tf_op jit(solution)/shard_map/normed/pallas_call | solution.py:548
  45.2 2.2 collective-permute-start
  47.5 2.1 own_part.1
  49.7 1.0 finish.1
  50.7 1.4 collective-permute-start.3
  52.1 1.5 collective-permute-start.4
  53.6 2.0 halves.3
  55.6 2.0 halves.4
  57.5 1.4 collective-permute-start.2
  59.0 1.0 collective-permute-done.3.rest_0_
  60.0 2.0 halves.5
  62.0 0.9 collective-permute-start.5
  63.0 1.7 collective-permute-start.7
  64.8 2.0 route.1
  66.8 0.6 collective-permute-done.6.right_a_ref
  67.4 5.5 %collective-permute-done.5.left_c_ref = bf16[128,1024]{1,0:T(8,128)(2,1)S(1)} collective-permute-done((bf16[128,1024]{1,0:T(8,128)(2,1)}, bf16[128,1024]{1,0:T(8,128)(2,1)S(1)}, u32[]{:S(2)}, u32[]{:S(2)}) %collective-permute-start.5) | collective-permute-done | bytes 262176 | tf_op jit(solution)/shard_map/ppermute | solution.py:627
  72.9 3.9 %dispatch.1 = (bf16[128,2048]{1,0:T(8,128)(2,1)}, f32[128,128]{1,0:T(8,128)S(1)}, bf16[3072,1024]{1,0:T(8,128)(2,1)S(1)}) custom-call(s32[1]{0:T(128)} %bitcast.where_ref, bf16[128,1024]{1,0:T(8,128)(2,1)S(1)} %collective-permute-done.2.left_a_ref, bf16[128,1024]{1,0:T(8,128)(2,1)} %get-tuple-element.69.left_b_ref, ...), custom_call_target="tpu_custom_call" | custom-call | flops 1610612736 | bytes 10485760 | tf_op jit(solution)/shard_map/dispatch/pallas_call | solution.py:672
  76.9 81.2 %all_to_all.20 = bf16[128,24,1024]{2,1,0:T(8,128)(2,1)S(1)} all-to-all(bf16[128,24,1024]{2,1,0:T(8,128)(2,1)S(1)} %bitcast.15), channel_id=1, replica_groups=mesh['seq'=16,'exp'=8] {'seq','exp'}, dimensions={0} | all-to-all | bytes 12582912 | tf_op jit(solution)/shard_map/all_to_all | solution.py:704
  158.1 18.2 %experts.1 = bf16[128,3,8,1024]{3,2,1,0:T(8,128)(2,1)} custom-call(bf16[128,3,8,1024]{3,2,1,0:T(8,128)(2,1)S(1)} %bitcast.16, bf16[1,2048,1536]{2,1,0:T(8,128)(2,1)S(1)} %bitcast.20, bf16[1,768,2048]{2,1,0:T(8,128)(2,1)S(1)} %copy-done.4), custom_call_target="tpu_custom_call" | custom-call | flops 14495514624 | bytes 23068672 | tf_op jit(solution)/shard_map/experts/pallas_call | solution.py:723
  176.2 6.6 %all-to-all-start.3 = ((bf16[128,24,1024]{2,1,0:T(8,128)(2,1)}), bf16[128,24,1024]{2,1,0:T(8,128)(2,1)}, u32[]{:S(2)}, u32[]{:S(2)}) async-start(bf16[128,24,1024]{2,1,0:T(8,128)(2,1)} %bitcast.21), calls=%async_computation.3 | async-start | bytes 12582912 | tf_op jit(solution)/shard_map/all_to_all | solution.py:733
  182.8 1.4 combine_weight.1.weight_ref
  184.3 74.4 %all-to-all-done.3.got_ref = bf16[128,24,1024]{2,1,0:T(8,128)(2,1)} async-done(((bf16[128,24,1024]{2,1,0:T(8,128)(2,1)}), bf16[128,24,1024]{2,1,0:T(8,128)(2,1)}, u32[]{:S(2)}, u32[]{:S(2)}) %all-to-all-start.3) | async-done | bytes 6291488 | tf_op jit(solution)/shard_map/all_to_all | solution.py:733
  258.6 4.9 %combine.1 = bf16[128,2048]{1,0:T(8,128)(2,1)} custom-call(bf16[128,24,1024]{2,1,0:T(8,128)(2,1)} %all-to-all-done.3.got_ref, bf16[256,3072]{1,0:T(8,128)(2,1)S(1)} %combine_weight.1.weight_ref, bf16[128,2048]{1,0:T(8,128)(2,1)S(1)} %copy-done.2), custom_call_target="tpu_custom_call" | custom-call | flops 1610612736 | bytes 8388608 | tf_op jit(solution)/shard_map/combine/pallas_call | solution.py:741
  (29 shorter events, 0.5 us)
Async XLA Ops:
  0.6 46.9 %collective-permute-start.1 = (bf16[512,2048]{1,0:T(8,128)(2,1)}, bf16[512,2048]{1,0:T(8,128)(2,1)}, u32[]{:S(2)}, u32[]{:S(2)}) collective-permute-start(bf16[512,2048]{1,0:T(8,128)(2,1)} %own_w_ref.7), channel_id=1, source_target_pairs={{0,1},{1,0},{2,3},{3,2},{4,5},{5,4},{6,7},{7,6},{8,9},{9,8},{10,11... | collective-permute-start | bytes 6291464 | tf_op jit(solution)/shard_map/ppermute | solution.py:461
  2.1 18.5 %copy-start.6 = (f32[8]{0:T(128)S(1)}, f32[8]{0:T(128)}, u32[]{:S(2)}) copy-start(f32[8]{0:T(128)} %param.22) | copy-start | bytes 100
  2.1 18.7 %copy-start.1 = (bf16[2048,512]{1,0:T(8,128)(2,1)S(1)}, bf16[2048,512]{1,0:T(8,128)(2,1)}, u32[]{:S(2)}) copy-start(bf16[2048,512]{1,0:T(8,128)(2,1)} %gate_w_ref.3) | copy-start | bytes 6291460
  12.9 15.5 %all-to-all-start = ((bf16[16,16,512]{2,1,0:T(8,128)(2,1)}), bf16[16,16,512]{2,1,0:T(8,128)(2,1)S(1)}, u32[]{:S(2)}, u32[]{:S(2)}) async-start(bf16[16,16,512]{2,1,0:T(8,128)(2,1)} %get-tuple-element.43), calls=%async_computation | async-start | bytes 524288 | tf_op jit(solution)/shard_map/all_to_all | solution.py:496
  29.2 10.9 %all-to-all-start.1 = ((bf16[16,8,512]{2,1,0:T(8,128)(2,1)}), bf16[16,8,512]{2,1,0:T(8,128)(2,1)S(1)}, u32[]{:S(2)}, u32[]{:S(2)}) async-start(bf16[16,8,512]{2,1,0:T(8,128)(2,1)} %prefix.1), calls=%async_computation.1 | async-start | bytes 262144 | tf_op jit(solution)/shard_map/all_to_all | solution.py:542
  33.4 6.7 %copy-start.3 = (f32[512]{0:T(512)S(1)}, f32[512]{0:T(512)}, u32[]{:S(2)}) copy-start(f32[512]{0:T(512)} %param.23) | copy-start | bytes 6148
  38.7 8.8 %copy-start = (bf16[512,2048]{1,0:T(8,128)(2,1)S(1)}, bf16[512,2048]{1,0:T(8,128)(2,1)}, u32[]{:S(2)}) copy-start(bf16[512,2048]{1,0:T(8,128)(2,1)} %own_w_ref.7) | copy-start | bytes 6291460
  45.2 4.4 %collective-permute-start = (bf16[512,512]{1,0:T(8,128)(2,1)}, bf16[512,512]{1,0:T(8,128)(2,1)S(1)}, u32[]{:S(2)}, u32[]{:S(2)}) collective-permute-start(bf16[512,512]{1,0:T(8,128)(2,1)} %get-tuple-element.59), channel_id=1, source_target_pairs={{0,1},{1,0},{2,3},{3,2},{4,5},{5,4},{6,7},{7,6},{8,9},{9,8},{10,11... | collective-permute-start | bytes 1572872 | tf_op jit(solution)/shard_map/ppermute | solution.py:574
  50.7 9.3 %collective-permute-start.3 = (bf16[128,1024]{1,0:T(8,128)(2,1)S(1)}, bf16[128,1024]{1,0:T(8,128)(2,1)S(1)}, u32[]{:S(2)}, u32[]{:S(2)}) collective-permute-start(bf16[128,1024]{1,0:T(8,128)(2,1)S(1)} %get-tuple-element.71), channel_id=1, source_target_pairs={{0,2},{1,3},{2,4},{3,5},{4,6},{5,7},{6,0},{7,1},{8,10},{9,11},{10,... | collective-permute-start | bytes 786440 | tf_op jit(solution)/shard_map/ppermute | solution.py:627
  52.1 8.0 %collective-permute-start.4 = (bf16[128,1024]{1,0:T(8,128)(2,1)S(1)}, bf16[128,1024]{1,0:T(8,128)(2,1)S(1)}, u32[]{:S(2)}, u32[]{:S(2)}) collective-permute-start(bf16[128,1024]{1,0:T(8,128)(2,1)S(1)} %get-tuple-element.72), channel_id=1, source_target_pairs={{0,6},{1,7},{2,0},{3,1},{4,2},{5,3},{6,4},{7,5},{8,14},{9,15},{10,... | collective-permute-start | bytes 786440 | tf_op jit(solution)/shard_map/ppermute | solution.py:627
  57.5 7.2 %copy-start.5 = (s32[128,8]{0,1:T(8,128)S(1)}, s32[128,8]{0,1:T(8,128)}, u32[]{:S(2)}) copy-start(s32[128,8]{0,1:T(8,128)} %param.27) | copy-start | bytes 12292
  57.5 9.2 %collective-permute-start.2 = (bf16[128,1024]{1,0:T(8,128)(2,1)}, bf16[128,1024]{1,0:T(8,128)(2,1)S(1)}, u32[]{:S(2)}, u32[]{:S(2)}) collective-permute-start(bf16[128,1024]{1,0:T(8,128)(2,1)} %get-tuple-element.68), channel_id=1, source_target_pairs={{0,6},{1,7},{2,0},{3,1},{4,2},{5,3},{6,4},{7,5},{8,14},{9,15},{10,... | collective-permute-start | bytes 786440 | tf_op jit(solution)/shard_map/ppermute | solution.py:627
  58.9 8.5 %collective-permute-start.6 = (bf16[128,1024]{1,0:T(8,128)(2,1)}, bf16[128,1024]{1,0:T(8,128)(2,1)}, u32[]{:S(2)}, u32[]{:S(2)}) collective-permute-start(bf16[128,1024]{1,0:T(8,128)(2,1)} %get-tuple-element.74), channel_id=1, source_target_pairs={{0,2},{1,3},{2,4},{3,5},{4,6},{5,7},{6,0},{7,1},{8,10},{9,11},{10,... | collective-permute-start | bytes 786440 | tf_op jit(solution)/shard_map/ppermute | solution.py:627
  62.0 10.9 %collective-permute-start.5 = (bf16[128,1024]{1,0:T(8,128)(2,1)}, bf16[128,1024]{1,0:T(8,128)(2,1)S(1)}, u32[]{:S(2)}, u32[]{:S(2)}) collective-permute-start(bf16[128,1024]{1,0:T(8,128)(2,1)} %get-tuple-element.73), channel_id=1, source_target_pairs={{0,2},{1,3},{2,4},{3,5},{4,6},{5,7},{6,0},{7,1},{8,10},{9,11},{10,... | collective-permute-start | bytes 786440 | tf_op jit(solution)/shard_map/ppermute | solution.py:627
  63.0 10.0 %collective-permute-start.7 = (bf16[128,1024]{1,0:T(8,128)(2,1)}, bf16[128,1024]{1,0:T(8,128)(2,1)S(1)}, u32[]{:S(2)}, u32[]{:S(2)}) collective-permute-start(bf16[128,1024]{1,0:T(8,128)(2,1)} %get-tuple-element.76), channel_id=1, source_target_pairs={{0,6},{1,7},{2,0},{3,1},{4,2},{5,3},{6,4},{7,5},{8,14},{9,15},{10,... | collective-permute-start | bytes 786440 | tf_op jit(solution)/shard_map/ppermute | solution.py:627
  72.9 85.1 %slice-start = ((s8[6291456]{0:T(1024)(128)(4,1)}), s8[4194304]{0:T(1024)(128)(4,1)S(1)}, s32[]{:S(2)}) async-start(s8[6291456]{0:T(1024)(128)(4,1)} %bitcast.19), calls=%async_computation.4 | async-start | bytes 8388608
  76.8 81.2 %slice-start.1 = ((s8[6291456]{0:T(1024)(128)(4,1)}), s8[2097152]{0:T(1024)(128)(4,1)S(1)}, s32[]{:S(2)}) async-start(s8[6291456]{0:T(1024)(128)(4,1)} %bitcast.19), calls=%async_computation.5 | async-start | bytes 4194304
  76.9 81.2 %copy-start.4 = (bf16[1,768,2048]{2,1,0:T(8,128)(2,1)S(1)}, bf16[1,768,2048]{2,1,0:T(8,128)(2,1)}, u32[]{:S(2)}) copy-start(bf16[1,768,2048]{2,1,0:T(8,128)(2,1)} %down_ref.1) | copy-start | bytes 9437188
  176.2 82.4 %copy-start.2 = (bf16[128,2048]{1,0:T(8,128)(2,1)S(1)}, bf16[128,2048]{1,0:T(8,128)(2,1)}, u32[]{:S(2)}) copy-start(bf16[128,2048]{1,0:T(8,128)(2,1)} %get-tuple-element.41.mixer_ref) | copy-start | bytes 1572868
  176.2 82.4 %all-to-all-start.3 = ((bf16[128,24,1024]{2,1,0:T(8,128)(2,1)}), bf16[128,24,1024]{2,1,0:T(8,128)(2,1)}, u32[]{:S(2)}, u32[]{:S(2)}) async-start(bf16[128,24,1024]{2,1,0:T(8,128)(2,1)} %bitcast.21), calls=%async_computation.3 | async-start | bytes 12582912 | tf_op jit(solution)/shard_map/all_to_all | solution.py:733

commit v6 on v5

--- a/solution.py
+++ b/solution.py
@@ -375,11 +375,14 @@
             got_ref.at[pl.ds(i * group, group)], held.at[i], ready.at[i]
         )
 
-    for i in range(parts):
+    ahead = 3
+    for i in range(ahead):
         fetch(i).start()
     total = jnp.zeros((2 * tokens, HALF), f32)
     for i in range(parts):
         fetch(i).wait()
+        if i + ahead < parts:
+            fetch(i + ahead).start()
         total += dot(weight_ref[:, i * rows : (i + 1) * rows], held[i].reshape(rows, HALF))
     out_ref[:, :HALF] = (mixer_ref[:, :HALF].astype(f32) + total[:tokens]).astype(bf16)
     out_ref[:, HALF:] = (mixer_ref[:, HALF:].astype(f32) + total[tokens:]).astype(bf16)

time: 264 us -> 265 us (level)
  no operation moved by 1% of the time
where the time goes in v6:
time: 265 us; the launch traced here: 264 us
  waiting for transfers between devices  85.5 us (32%)
  blocking collectives  81.2 us (31%)
  Pallas kernels  66.9 us (25%)
  starting transfers between devices  29.2 us (11%)
    all_to_all x1, blocking collectives, body(): lax.all_to_all(outgoing.reshape(peers, SLAB, HALF), ('seq', 'exp'), split...  81.2 us
    all_to_all x1, waiting for transfers between devices, body(): lax.all_to_all(results.reshape(peers, SLAB, HALF), ('seq', 'exp'), split_...  74.4 us
    pallas_call x1, Pallas kernels, body(): pl.pallas_call(expert_kernel, grid=(4,), in_specs=[resident()] * 3, out_s...  18.2 us
    pallas_call x1, Pallas kernels, body(): pl.pallas_call(local_state_kernel, grid=(blocks,), in_specs=[by_rows(Q, D...  10.8 us
    pallas_call x2, Pallas kernels, within_half(): pl.pallas_call(within_kernel, grid=(half_blocks,), in_specs=[block(Q, D),...  10.4 us
    all_to_all x1, starting transfers between devices, body(): lax.all_to_all(sent, 'seq', split_axis=0, concat_axis=0, tiled=True)  7.7 us
    ppermute x6, waiting for transfers between devices, send(): return lax.ppermute(piece, 'exp', moves)  7.18 us
    ppermute x6, starting transfers between devices, send(): return lax.ppermute(piece, 'exp', moves)  7.02 us
  transfers between devices with their start and end apart: 11, of which 6 were waited for; matrix products, arithmetic and copies ran while one was open for 0% of the time, Pallas kernels for 15%

profile of v6, /device:TPU:1, one launch (start us, length us, event | category | flops | bytes accessed | tf_op | source)
XLA Modules:
  0.0 264.0 jit_solution(15232781054721775192)
XLA Ops:
  0.6 1.5 collective-permute-start.1
  2.1 10.8 %local_state.1 = (bf16[1024,2048]{1,0:T(8,128)(2,1)}, bf16[1024,512]{1,0:T(8,128)(2,1)}, bf16[1024,256]{1,0:T(8,128)(2,1)}, bf16[4,128,512]{2,1,0:T(8,128)(2,1)}, bf16[16,16,512]{2,1,0:T(8,128)(2,1)}) custom-call(bf16[1024,2048]{1,0:T(8,128)(2,1)} %hidden_ref.3, f32[1,2048]{1,0:T(1,128)} %bitcast.30, bf16[2048,512]{1,0:T(8,128)(2,1)} %value_ref.1, ...), custom_call_target="tpu_custom_call" | custom-call | flops 3221225472 | bytes 16777216 | tf_op jit(solution)/shard_map/local_state/pallas_call | solution.py:468
  12.9 7.7 %all-to-all-start = ((bf16[16,16,512]{2,1,0:T(8,128)(2,1)}), bf16[16,16,512]{2,1,0:T(8,128)(2,1)S(1)}, u32[]{:S(2)}, u32[]{:S(2)}) async-start(bf16[16,16,512]{2,1,0:T(8,128)(2,1)} %get-tuple-element.43), calls=%async_computation | async-start | bytes 524288 | tf_op jit(solution)/shard_map/all_to_all | solution.py:499
  20.8 5.2 %within.2 = (bf16[1024,512]{1,0:T(8,128)(2,1)}, f32[1024,512]{1,0:T(8,128)}) custom-call(bf16[1024,2048]{1,0:T(8,128)(2,1)} %get-tuple-element.44.mixed_ref, bf16[2048,512]{1,0:T(8,128)(2,1)S(1)} %copy-done.1, bf16[1024,512]{1,0:T(8,128)(2,1)} %get-tuple-element.45.x_ref, bf16[1024,256]{1,0:T(8,128)(2,1)} %get-tuple-element.46.maps_ref, f32[8,1024]{1,0:T(8,128)} %bitcast.23, ...), custom_call_target="tpu_custom_call" | custom-call | flops 1342177280 | bytes 5242880 | tf_op jit(solution)/shard_map/within/pallas_call | solution.py:514
  26.0 2.4 all-to-all-done.got_ref
  28.4 0.8 prefix.1
  29.2 4.2 %all-to-all-start.1 = ((bf16[16,8,512]{2,1,0:T(8,128)(2,1)}), bf16[16,8,512]{2,1,0:T(8,128)(2,1)S(1)}, u32[]{:S(2)}, u32[]{:S(2)}) async-start(bf16[16,8,512]{2,1,0:T(8,128)(2,1)} %prefix.1), calls=%async_computation.1 | async-start | bytes 262144 | tf_op jit(solution)/shard_map/all_to_all | solution.py:545
  33.4 5.2 %within.3 = (bf16[1024,512]{1,0:T(8,128)(2,1)}, f32[1024,512]{1,0:T(8,128)}) custom-call(bf16[1024,2048]{1,0:T(8,128)(2,1)} %get-tuple-element.44.mixed_ref, bf16[2048,512]{1,0:T(8,128)(2,1)S(1)} %copy-done.1, bf16[1024,512]{1,0:T(8,128)(2,1)} %get-tuple-element.45.x_ref, ...), custom_call_target="tpu_custom_call", output_to_operand_aliasing={{0}: (8, {}), {1}: (9, {})} | custom-call | flops 1342177280 | bytes 5242880 | tf_op jit(solution)/shard_map/within/pallas_call | solution.py:514
  38.7 1.5 all-to-all-done.1
  40.1 5.1 %normed.1 = (bf16[512,512]{1,0:T(8,128)(2,1)S(1)}, bf16[512,512]{1,0:T(8,128)(2,1)}) custom-call(s32[1]{0:T(128)} %bitcast.5.core_ref, f32[1024,512]{1,0:T(8,128)} %get-tuple-element.55.within_ref, bf16[1024,256]{1,0:T(8,128)(2,1)} %get-tuple-element.46.maps_ref, bf16[1024,512]{1,0:T(8,128)(2,1)} %get-tuple-element.56.gate_ref, f32[8,1024]{1,0:T(8,128)} %bitcast.25, ...), custom_call_target="tpu_custom_call" | custom-call | flops 134217728 | bytes 5242880 | tf_op jit(solution)/shard_map/normed/pallas_call | solution.py:551
  45.2 2.2 collective-permute-start
  47.5 2.1 own_part.1
  49.7 1.0 finish.1
  50.7 1.4 collective-permute-start.3
  52.1 1.5 collective-permute-start.4
  53.6 2.0 halves.3
  55.6 2.0 halves.4
  57.5 1.4 collective-permute-start.2
  59.0 1.0 collective-permute-done.3.rest_0_
  60.0 2.0 halves.5
  62.0 0.9 collective-permute-start.5
  63.0 1.7 collective-permute-start.7
  64.8 2.0 route.1
  66.8 0.6 collective-permute-done.6.right_a_ref
  67.4 5.5 %collective-permute-done.5.left_c_ref = bf16[128,1024]{1,0:T(8,128)(2,1)S(1)} collective-permute-done((bf16[128,1024]{1,0:T(8,128)(2,1)}, bf16[128,1024]{1,0:T(8,128)(2,1)S(1)}, u32[]{:S(2)}, u32[]{:S(2)}) %collective-permute-start.5) | collective-permute-done | bytes 262176 | tf_op jit(solution)/shard_map/ppermute | solution.py:630
  72.9 3.9 %dispatch.1 = (bf16[128,2048]{1,0:T(8,128)(2,1)}, f32[128,128]{1,0:T(8,128)S(1)}, bf16[3072,1024]{1,0:T(8,128)(2,1)S(1)}) custom-call(s32[1]{0:T(128)} %bitcast.where_ref, bf16[128,1024]{1,0:T(8,128)(2,1)S(1)} %collective-permute-done.2.left_a_ref, bf16[128,1024]{1,0:T(8,128)(2,1)} %get-tuple-element.69.left_b_ref, ...), custom_call_target="tpu_custom_call" | custom-call | flops 1610612736 | bytes 10485760 | tf_op jit(solution)/shard_map/dispatch/pallas_call | solution.py:675
  76.9 81.2 %all_to_all.20 = bf16[128,24,1024]{2,1,0:T(8,128)(2,1)S(1)} all-to-all(bf16[128,24,1024]{2,1,0:T(8,128)(2,1)S(1)} %bitcast.15), channel_id=1, replica_groups=mesh['seq'=16,'exp'=8] {'seq','exp'}, dimensions={0} | all-to-all | bytes 12582912 | tf_op jit(solution)/shard_map/all_to_all | solution.py:707
  158.1 18.2 %experts.1 = bf16[128,3,8,1024]{3,2,1,0:T(8,128)(2,1)} custom-call(bf16[128,3,8,1024]{3,2,1,0:T(8,128)(2,1)S(1)} %bitcast.16, bf16[1,2048,1536]{2,1,0:T(8,128)(2,1)S(1)} %bitcast.20, bf16[1,768,2048]{2,1,0:T(8,128)(2,1)S(1)} %copy-done.4), custom_call_target="tpu_custom_call" | custom-call | flops 14495514624 | bytes 23068672 | tf_op jit(solution)/shard_map/experts/pallas_call | solution.py:726
  176.2 6.6 %all-to-all-start.3 = ((bf16[128,24,1024]{2,1,0:T(8,128)(2,1)}), bf16[128,24,1024]{2,1,0:T(8,128)(2,1)}, u32[]{:S(2)}, u32[]{:S(2)}) async-start(bf16[128,24,1024]{2,1,0:T(8,128)(2,1)} %bitcast.21), calls=%async_computation.3 | async-start | bytes 12582912 | tf_op jit(solution)/shard_map/all_to_all | solution.py:736
  182.8 1.4 combine_weight.1.weight_ref
  184.3 74.4 %all-to-all-done.3.got_ref = bf16[128,24,1024]{2,1,0:T(8,128)(2,1)} async-done(((bf16[128,24,1024]{2,1,0:T(8,128)(2,1)}), bf16[128,24,1024]{2,1,0:T(8,128)(2,1)}, u32[]{:S(2)}, u32[]{:S(2)}) %all-to-all-start.3) | async-done | bytes 6291488 | tf_op jit(solution)/shard_map/all_to_all | solution.py:736
  258.6 5.2 %combine.1 = bf16[128,2048]{1,0:T(8,128)(2,1)} custom-call(bf16[128,24,1024]{2,1,0:T(8,128)(2,1)} %all-to-all-done.3.got_ref, bf16[256,3072]{1,0:T(8,128)(2,1)S(1)} %combine_weight.1.weight_ref, bf16[128,2048]{1,0:T(8,128)(2,1)S(1)} %copy-done.2), custom_call_target="tpu_custom_call" | custom-call | flops 1610612736 | bytes 8388608 | tf_op jit(solution)/shard_map/combine/pallas_call | solution.py:744
  (29 shorter events, 0.5 us)
Async XLA Ops:
  0.6 46.9 %collective-permute-start.1 = (bf16[512,2048]{1,0:T(8,128)(2,1)}, bf16[512,2048]{1,0:T(8,128)(2,1)}, u32[]{:S(2)}, u32[]{:S(2)}) collective-permute-start(bf16[512,2048]{1,0:T(8,128)(2,1)} %own_w_ref.7), channel_id=1, source_target_pairs={{0,1},{1,0},{2,3},{3,2},{4,5},{5,4},{6,7},{7,6},{8,9},{9,8},{10,11... | collective-permute-start | bytes 6291464 | tf_op jit(solution)/shard_map/ppermute | solution.py:464
  2.1 18.5 %copy-start.6 = (f32[8]{0:T(128)S(1)}, f32[8]{0:T(128)}, u32[]{:S(2)}) copy-start(f32[8]{0:T(128)} %param.22) | copy-start | bytes 100
  2.1 18.7 %copy-start.1 = (bf16[2048,512]{1,0:T(8,128)(2,1)S(1)}, bf16[2048,512]{1,0:T(8,128)(2,1)}, u32[]{:S(2)}) copy-start(bf16[2048,512]{1,0:T(8,128)(2,1)} %gate_w_ref.3) | copy-start | bytes 6291460
  12.9 15.5 %all-to-all-start = ((bf16[16,16,512]{2,1,0:T(8,128)(2,1)}), bf16[16,16,512]{2,1,0:T(8,128)(2,1)S(1)}, u32[]{:S(2)}, u32[]{:S(2)}) async-start(bf16[16,16,512]{2,1,0:T(8,128)(2,1)} %get-tuple-element.43), calls=%async_computation | async-start | bytes 524288 | tf_op jit(solution)/shard_map/all_to_all | solution.py:499
  29.2 10.9 %all-to-all-start.1 = ((bf16[16,8,512]{2,1,0:T(8,128)(2,1)}), bf16[16,8,512]{2,1,0:T(8,128)(2,1)S(1)}, u32[]{:S(2)}, u32[]{:S(2)}) async-start(bf16[16,8,512]{2,1,0:T(8,128)(2,1)} %prefix.1), calls=%async_computation.1 | async-start | bytes 262144 | tf_op jit(solution)/shard_map/all_to_all | solution.py:545
  33.4 6.7 %copy-start.3 = (f32[512]{0:T(512)S(1)}, f32[512]{0:T(512)}, u32[]{:S(2)}) copy-start(f32[512]{0:T(512)} %param.23) | copy-start | bytes 6148
  38.7 8.8 %copy-start = (bf16[512,2048]{1,0:T(8,128)(2,1)S(1)}, bf16[512,2048]{1,0:T(8,128)(2,1)}, u32[]{:S(2)}) copy-start(bf16[512,2048]{1,0:T(8,128)(2,1)} %own_w_ref.7) | copy-start | bytes 6291460
  45.2 4.4 %collective-permute-start = (bf16[512,512]{1,0:T(8,128)(2,1)}, bf16[512,512]{1,0:T(8,128)(2,1)S(1)}, u32[]{:S(2)}, u32[]{:S(2)}) collective-permute-start(bf16[512,512]{1,0:T(8,128)(2,1)} %get-tuple-element.59), channel_id=1, source_target_pairs={{0,1},{1,0},{2,3},{3,2},{4,5},{5,4},{6,7},{7,6},{8,9},{9,8},{10,11... | collective-permute-start | bytes 1572872 | tf_op jit(solution)/shard_map/ppermute | solution.py:577
  50.7 9.3 %collective-permute-start.3 = (bf16[128,1024]{1,0:T(8,128)(2,1)S(1)}, bf16[128,1024]{1,0:T(8,128)(2,1)S(1)}, u32[]{:S(2)}, u32[]{:S(2)}) collective-permute-start(bf16[128,1024]{1,0:T(8,128)(2,1)S(1)} %get-tuple-element.71), channel_id=1, source_target_pairs={{0,2},{1,3},{2,4},{3,5},{4,6},{5,7},{6,0},{7,1},{8,10},{9,11},{10,... | collective-permute-start | bytes 786440 | tf_op jit(solution)/shard_map/ppermute | solution.py:630
  52.1 8.0 %collective-permute-start.4 = (bf16[128,1024]{1,0:T(8,128)(2,1)S(1)}, bf16[128,1024]{1,0:T(8,128)(2,1)S(1)}, u32[]{:S(2)}, u32[]{:S(2)}) collective-permute-start(bf16[128,1024]{1,0:T(8,128)(2,1)S(1)} %get-tuple-element.72), channel_id=1, source_target_pairs={{0,6},{1,7},{2,0},{3,1},{4,2},{5,3},{6,4},{7,5},{8,14},{9,15},{10,... | collective-permute-start | bytes 786440 | tf_op jit(solution)/shard_map/ppermute | solution.py:630
  57.5 7.2 %copy-start.5 = (s32[128,8]{0,1:T(8,128)S(1)}, s32[128,8]{0,1:T(8,128)}, u32[]{:S(2)}) copy-start(s32[128,8]{0,1:T(8,128)} %param.27) | copy-start | bytes 12292
  57.5 9.2 %collective-permute-start.2 = (bf16[128,1024]{1,0:T(8,128)(2,1)}, bf16[128,1024]{1,0:T(8,128)(2,1)S(1)}, u32[]{:S(2)}, u32[]{:S(2)}) collective-permute-start(bf16[128,1024]{1,0:T(8,128)(2,1)} %get-tuple-element.68), channel_id=1, source_target_pairs={{0,6},{1,7},{2,0},{3,1},{4,2},{5,3},{6,4},{7,5},{8,14},{9,15},{10,... | collective-permute-start | bytes 786440 | tf_op jit(solution)/shard_map/ppermute | solution.py:630
  58.9 8.5 %collective-permute-start.6 = (bf16[128,1024]{1,0:T(8,128)(2,1)}, bf16[128,1024]{1,0:T(8,128)(2,1)}, u32[]{:S(2)}, u32[]{:S(2)}) collective-permute-start(bf16[128,1024]{1,0:T(8,128)(2,1)} %get-tuple-element.74), channel_id=1, source_target_pairs={{0,2},{1,3},{2,4},{3,5},{4,6},{5,7},{6,0},{7,1},{8,10},{9,11},{10,... | collective-permute-start | bytes 786440 | tf_op jit(solution)/shard_map/ppermute | solution.py:630
  62.0 10.9 %collective-permute-start.5 = (bf16[128,1024]{1,0:T(8,128)(2,1)}, bf16[128,1024]{1,0:T(8,128)(2,1)S(1)}, u32[]{:S(2)}, u32[]{:S(2)}) collective-permute-start(bf16[128,1024]{1,0:T(8,128)(2,1)} %get-tuple-element.73), channel_id=1, source_target_pairs={{0,2},{1,3},{2,4},{3,5},{4,6},{5,7},{6,0},{7,1},{8,10},{9,11},{10,... | collective-permute-start | bytes 786440 | tf_op jit(solution)/shard_map/ppermute | solution.py:630
  63.0 10.0 %collective-permute-start.7 = (bf16[128,1024]{1,0:T(8,128)(2,1)}, bf16[128,1024]{1,0:T(8,128)(2,1)S(1)}, u32[]{:S(2)}, u32[]{:S(2)}) collective-permute-start(bf16[128,1024]{1,0:T(8,128)(2,1)} %get-tuple-element.76), channel_id=1, source_target_pairs={{0,6},{1,7},{2,0},{3,1},{4,2},{5,3},{6,4},{7,5},{8,14},{9,15},{10,... | collective-permute-start | bytes 786440 | tf_op jit(solution)/shard_map/ppermute | solution.py:630
  72.9 85.1 %slice-start = ((s8[6291456]{0:T(1024)(128)(4,1)}), s8[4194304]{0:T(1024)(128)(4,1)S(1)}, s32[]{:S(2)}) async-start(s8[6291456]{0:T(1024)(128)(4,1)} %bitcast.19), calls=%async_computation.4 | async-start | bytes 8388608
  76.8 81.2 %slice-start.1 = ((s8[6291456]{0:T(1024)(128)(4,1)}), s8[2097152]{0:T(1024)(128)(4,1)S(1)}, s32[]{:S(2)}) async-start(s8[6291456]{0:T(1024)(128)(4,1)} %bitcast.19), calls=%async_computation.5 | async-start | bytes 4194304
  76.9 81.2 %copy-start.4 = (bf16[1,768,2048]{2,1,0:T(8,128)(2,1)S(1)}, bf16[1,768,2048]{2,1,0:T(8,128)(2,1)}, u32[]{:S(2)}) copy-start(bf16[1,768,2048]{2,1,0:T(8,128)(2,1)} %down_ref.1) | copy-start | bytes 9437188
  176.2 82.4 %copy-start.2 = (bf16[128,2048]{1,0:T(8,128)(2,1)S(1)}, bf16[128,2048]{1,0:T(8,128)(2,1)}, u32[]{:S(2)}) copy-start(bf16[128,2048]{1,0:T(8,128)(2,1)} %get-tuple-element.41.mixer_ref) | copy-start | bytes 1572868
  176.2 82.4 %all-to-all-start.3 = ((bf16[128,24,1024]{2,1,0:T(8,128)(2,1)}), bf16[128,24,1024]{2,1,0:T(8,128)(2,1)}, u32[]{:S(2)}, u32[]{:S(2)}) async-start(bf16[128,24,1024]{2,1,0:T(8,128)(2,1)} %bitcast.21), calls=%async_computation.3 | async-start | bytes 12582912 | tf_op jit(solution)/shard_map/all_to_all | solution.py:736
